TPU v7x, 32 devices: a whole 2x2x4 slice. The times are simulated.
32 devices in a mesh: dp: 4 (over y, x), vocab: 8 (over z, core).
Axes of the slice: x: 2, y: 2, z: 4, core: 2. Of those that a mesh axis runs over, the one named last changes fastest.
Arguments:
- token_ids: int32 [64, 512], P(('dp', 'vocab')), may hold values from 0 to 30719, as said below
- type_ids: int32 [64, 512], P(('dp', 'vocab')), may hold values from 0 to 1
- lengths: int32 [64], P(('dp', 'vocab')), may hold values from 20 to 512, as said below
- word_table: bfloat16 [30720, 768], P('vocab'), may hold values from -6 to 6
- pos_table: bfloat16 [512, 768], replicated, may hold values from -4 to 4
- token_type_embeddings: bfloat16 [2, 768], replicated, may hold values from -4 to 4
- emb_gain: float32 [768], replicated, may hold values from 0.25 to 1.75
- emb_bias: float32 [768], replicated, may hold values from -3 to 3
- query_weight: bfloat16 [768, 768], replicated, may hold values from -0.21875 to 0.21875
- query_bias: float32 [768], replicated, may hold values from -3 to 3
- key_weight: bfloat16 [768, 768], replicated, may hold values from -0.21875 to 0.21875
- value_weight: bfloat16 [768, 768], replicated, may hold values from -0.21875 to 0.21875
- value_bias: float32 [768], replicated, may hold values from -3 to 3
- out_weight: bfloat16 [768, 768], replicated, may hold values from -0.875 to 0.875
- out_bias: float32 [768], replicated, may hold values from -3 to 3
- attn_gain: float32 [768], replicated, may hold values from 0.25 to 1.75
- attn_bias: float32 [768], replicated, may hold values from -3 to 3
- up_weight: bfloat16 [768, 3072], replicated, may hold values from -0.21875 to 0.21875
- up_bias: float32 [3072], replicated, may hold values from -3 to 3
- down_weight: bfloat16 [3072, 768], replicated, may hold values from -0.109375 to 0.109375
- down_bias: float32 [768], replicated, may hold values from -3 to 3
- final_gain: float32 [768], replicated, may hold values from 0.25 to 1.75
- final_bias: float32 [768], replicated, may hold values from -3 to 3
- cotangent: bfloat16 [64, 512, 768], P(('dp', 'vocab')), may hold values from -6 to 6
Outputs:
- encoded: float32 [64, 512, 768], P(('dp', 'vocab'))
- word_grad: float32 [30720, 768], P('vocab')
- pos_grad: float32 [512, 768], P('vocab')
- type_grad: float32 [2, 768], P(None, 'vocab')
- emb_gain_grad: float32 [768], P('vocab')
- emb_bias_grad: float32 [768], P('vocab')
- query_weight_grad: float32 [768, 768], P('vocab')
- query_bias_grad: float32 [768], P('vocab')
- key_weight_grad: float32 [768, 768], P('vocab')
- value_weight_grad: float32 [768, 768], P('vocab')
- value_bias_grad: float32 [768], P('vocab')
- out_weight_grad: float32 [768, 768], P('vocab')
- out_bias_grad: float32 [768], P('vocab')
- attn_gain_grad: float32 [768], P('vocab')
- attn_bias_grad: float32 [768], P('vocab')
- up_weight_grad: float32 [768, 3072], P('vocab')
- up_bias_grad: float32 [3072], P('vocab')
- down_weight_grad: float32 [3072, 768], P('vocab')
- down_bias_grad: float32 [768], P('vocab')
- final_gain_grad: float32 [768], P('vocab')
- final_bias_grad: float32 [768], P('vocab')
Inputs may be any that keep to these rules, and one draw needn't show every extreme that they name: `token_ids`: among the tokens of one device, at most 256 ids fall into the 3840 rows of word_table that one index of vocab holds; for one such block of rows, the same on every device, exactly 256 do. `lengths`: the tokens at positions from a sequence's length on are padding; some sequence has length 512 and some 20.
All inputs are finite; a program needn't handle non-finite values.
Results may differ from a plain program's by a relative error of at most 0.017.
Values may be sent and summed in bfloat16 or wider, within the bound.
A program may use at most 192 MiB of HBM per device.

v0:
```python
from functools import partial

import jax
import jax.numpy as jnp
from jax import lax
from jax.sharding import PartitionSpec as P

HEADS = 12
HEAD = 64
L = 512


EPSILON = 1e-12


def layer_norm(values, gain, bias):
    center = values - jnp.mean(values, -1, keepdims=True)
    spread = jnp.mean(center * center, -1, keepdims=True)
    return center * lax.rsqrt(spread + EPSILON) * gain + bias


def matmul(left, right):
    return jnp.dot(left, right, preferred_element_type=jnp.float32)


def matmul_tn(left, right):
    return lax.dot_general(
        left, right, (((0,), (0,)), ((), ())), preferred_element_type=jnp.float32
    )


def matmul_nt(left, right):
    return lax.dot_general(
        left, right, (((1,), (1,)), ((), ())), preferred_element_type=jnp.float32
    )


def masked_scores(query, keys, length):
    scores = jnp.einsum("qhd,khd->hqk", query, keys, preferred_element_type=jnp.float32) * HEAD ** (
        -0.5
    )
    visible = jnp.arange(L) < length
    return jnp.where(visible[None, None, :], scores, -1000000000.0)


def attend_forward(block):
    query, keys, values, length = block
    scores = masked_scores(query, keys, length)
    highest = jnp.max(scores, -1, keepdims=True)
    expd = jnp.exp(scores - highest)
    totals = jnp.sum(expd, -1, keepdims=True)
    probs_low = (expd / totals).astype(jnp.bfloat16)
    mixed = jnp.einsum("hqk,khd->qhd", probs_low, values, preferred_element_type=jnp.float32)
    return (mixed.astype(jnp.bfloat16), highest + jnp.log(totals))


def attend_backward(block):
    query, keys, values, grad_mixed, logsum, length = block
    probs = jnp.exp(masked_scores(query, keys, length) - logsum)
    probs_low = probs.astype(jnp.bfloat16)
    grad_values = jnp.einsum(
        "hqk,qhd->khd", probs_low, grad_mixed, preferred_element_type=jnp.float32
    )
    grad_probs = jnp.einsum("qhd,khd->hqk", grad_mixed, values, preferred_element_type=jnp.float32)
    inner = jnp.sum(grad_probs * probs, -1, keepdims=True)
    grad_scores = (probs * (grad_probs - inner)).astype(jnp.bfloat16)
    scale = HEAD ** (-0.5)
    grad_query = (
        jnp.einsum("hqk,khd->qhd", grad_scores, keys, preferred_element_type=jnp.float32) * scale
    )
    grad_keys = (
        jnp.einsum("hqk,qhd->khd", grad_scores, query, preferred_element_type=jnp.float32) * scale
    )
    return (grad_query, grad_keys, grad_values)


def local(
    token_ids,
    type_ids,
    lengths,
    word_table,
    pos_table,
    token_type_embeddings,
    emb_gain,
    emb_bias,
    query_weight,
    query_bias,
    key_weight,
    value_weight,
    value_bias,
    out_weight,
    out_bias,
    attn_gain,
    attn_bias,
    up_weight,
    up_bias,
    down_weight,
    down_bias,
    final_gain,
    final_bias,
    cotangent,
):
    seq_count, seq_len = token_ids.shape
    tokens = seq_count * seq_len
    width = word_table.shape[1]
    rows_local = word_table.shape[0]
    owners = lax.axis_size("vocab")
    capacity = max(2, 2 * tokens // owners)
    flat_ids = token_ids.reshape(tokens)
    owner = flat_ids // rows_local
    member = (owner[:, None] == jnp.arange(owners)[None, :]).astype(jnp.int32)
    earlier = jnp.cumsum(member, 0) - member
    rank = jnp.sum(earlier * member, 1)
    slot = owner * capacity + rank
    requests = (
        jnp.full((owners * capacity,), -1, jnp.int32).at[slot].set(flat_ids - owner * rows_local)
    )
    requests = requests.reshape(owners, capacity)
    asked = lax.all_to_all(requests, "vocab", split_axis=0, concat_axis=0, tiled=True)
    valid = asked >= 0
    found = word_table[jnp.maximum(asked, 0)]
    found = jnp.where(valid[..., None], found, jnp.zeros((), jnp.bfloat16))
    returned = lax.all_to_all(found, "vocab", split_axis=0, concat_axis=0, tiled=True)
    word_rows = returned.reshape(owners * capacity, width)[slot]
    kinds = token_type_embeddings.shape[0]
    selection_matrix = (type_ids[..., None] == jnp.arange(kinds)[None, None, :]).astype(jnp.float32)
    type_rows = jnp.einsum(
        "tcr,rb->tcb",
        selection_matrix,
        token_type_embeddings.astype(jnp.float32),
        precision=lax.Precision.HIGHEST,
    )
    embedded = (
        word_rows.reshape(seq_count, seq_len, width).astype(jnp.float32)
        + pos_table.astype(jnp.float32)[None]
        + type_rows
    )
    normed = layer_norm(embedded, emb_gain, emb_bias).reshape(tokens, width)
    normed_low = normed.astype(jnp.bfloat16)
    query = (matmul(normed_low, query_weight) + query_bias).astype(jnp.bfloat16)
    keys = matmul(normed_low, key_weight).astype(jnp.bfloat16)
    values = (matmul(normed_low, value_weight) + value_bias).astype(jnp.bfloat16)
    split_shape = (seq_count, seq_len, HEADS, HEAD)
    query_split = query.reshape(split_shape)
    keys_split = keys.reshape(split_shape)
    values_split = values.reshape(split_shape)
    mixed, logsum = lax.map(attend_forward, (query_split, keys_split, values_split, lengths))
    mixed_low = mixed.reshape(tokens, width)
    first = normed + matmul(mixed_low, out_weight) + out_bias
    hidden = layer_norm(first, attn_gain, attn_bias)
    hidden_reduced_precision = hidden.astype(jnp.bfloat16)
    upper = matmul(hidden_reduced_precision, up_weight) + up_bias
    active_low = jax.nn.gelu(upper, approximate=False).astype(jnp.bfloat16)
    second = hidden + matmul(active_low, down_weight) + down_bias
    encoded = layer_norm(second, final_gain, final_bias)
    grad_out = cotangent.reshape(tokens, width).astype(jnp.float32)
    _, final_pull = jax.vjp(layer_norm, second, final_gain, final_bias)
    grad_second, grad_final_gain, grad_final_bias = final_pull(grad_out)
    grad_down_bias = jnp.sum(grad_second, 0)
    second_matmul_gradient_reduced = grad_second.astype(jnp.bfloat16)
    grad_down = matmul_tn(active_low, second_matmul_gradient_reduced)
    grad_active = matmul_nt(second_matmul_gradient_reduced, down_weight)
    _, gelu_pull = jax.vjp(partial(jax.nn.gelu, approximate=False), upper)
    (grad_upper,) = gelu_pull(grad_active)
    grad_up_bias = jnp.sum(grad_upper, 0)
    grad_upper_low = grad_upper.astype(jnp.bfloat16)
    grad_up = matmul_tn(hidden_reduced_precision, grad_upper_low)
    grad_hidden = grad_second + matmul_nt(grad_upper_low, up_weight)
    _, attn_pull = jax.vjp(layer_norm, first, attn_gain, attn_bias)
    grad_first, grad_attn_gain, grad_attn_bias = attn_pull(grad_hidden)
    grad_out_bias = jnp.sum(grad_first, 0)
    grad_first_low = grad_first.astype(jnp.bfloat16)
    grad_out_weight = matmul_tn(mixed_low, grad_first_low)
    grad_mixed = matmul_nt(grad_first_low, out_weight).astype(jnp.bfloat16)
    grad_query, grad_keys, grad_values = lax.map(
        attend_backward,
        (query_split, keys_split, values_split, grad_mixed.reshape(split_shape), logsum, lengths),
    )
    grad_query = grad_query.reshape(tokens, width)
    grad_keys = grad_keys.reshape(tokens, width)
    grad_values = grad_values.reshape(tokens, width)
    grad_query_bias = jnp.sum(grad_query, 0)
    grad_value_bias = jnp.sum(grad_values, 0)
    grad_query_low = grad_query.astype(jnp.bfloat16)
    grad_keys_low = grad_keys.astype(jnp.bfloat16)
    grad_values_low = grad_values.astype(jnp.bfloat16)
    grad_query_weight = matmul_tn(normed_low, grad_query_low)
    grad_key_weight = matmul_tn(normed_low, grad_keys_low)
    grad_value_weight = matmul_tn(normed_low, grad_values_low)
    grad_normed = (
        grad_first
        + matmul_nt(grad_query_low, query_weight)
        + matmul_nt(grad_keys_low, key_weight)
        + matmul_nt(grad_values_low, value_weight)
    )
    _, emb_pull = jax.vjp(layer_norm, embedded, emb_gain, emb_bias)
    embedding_output_gradient, grad_emb_gain, grad_emb_bias = emb_pull(
        grad_normed.reshape(seq_count, seq_len, width)
    )
    grad_pos = jnp.sum(embedding_output_gradient, 0)
    token_type_gradient = jnp.einsum(
        "nox,noh->xh", selection_matrix, embedding_output_gradient, precision=lax.Precision.HIGHEST
    )
    outgoing = (
        jnp.zeros((owners * capacity, width), jnp.float32)
        .at[slot]
        .set(embedding_output_gradient.reshape(tokens, width))
    )
    incoming = lax.all_to_all(
        outgoing.reshape(owners, capacity, width).astype(jnp.bfloat16),
        "vocab",
        split_axis=0,
        concat_axis=0,
        tiled=True,
    ).astype(jnp.float32)
    keep_rows = asked >= 0
    incoming = jnp.where(keep_rows[..., None], incoming, 0.0)
    grad_word = (
        jnp.zeros((rows_local, width), jnp.float32)
        .at[jnp.maximum(asked, 0).reshape(-1)]
        .add(incoming.reshape(owners * capacity, width))
    )
    (
        grad_query_weight,
        grad_query_bias,
        grad_key_weight,
        grad_value_weight,
        grad_value_bias,
        grad_out_weight,
        grad_out_bias,
        grad_attn_gain,
        grad_attn_bias,
        grad_emb_gain,
        grad_emb_bias,
        grad_pos,
        token_type_gradient,
        grad_down,
        grad_down_bias,
        grad_up,
        grad_up_bias,
        grad_final_gain,
        grad_final_bias,
    ) = (
        lax.psum_scatter(grad_query_weight, "vocab", scatter_dimension=0, tiled=True),
        lax.psum_scatter(grad_query_bias, "vocab", scatter_dimension=0, tiled=True),
        lax.psum_scatter(grad_key_weight, "vocab", scatter_dimension=0, tiled=True),
        lax.psum_scatter(grad_value_weight, "vocab", scatter_dimension=0, tiled=True),
        lax.psum_scatter(grad_value_bias, "vocab", scatter_dimension=0, tiled=True),
        lax.psum_scatter(grad_out_weight, "vocab", scatter_dimension=0, tiled=True),
        lax.psum_scatter(grad_out_bias, "vocab", scatter_dimension=0, tiled=True),
        lax.psum_scatter(grad_attn_gain, "vocab", scatter_dimension=0, tiled=True),
        lax.psum_scatter(grad_attn_bias, "vocab", scatter_dimension=0, tiled=True),
        lax.psum_scatter(grad_emb_gain, "vocab", scatter_dimension=0, tiled=True),
        lax.psum_scatter(grad_emb_bias, "vocab", scatter_dimension=0, tiled=True),
        lax.psum_scatter(grad_pos, "vocab", scatter_dimension=0, tiled=True),
        lax.psum_scatter(token_type_gradient, "vocab", scatter_dimension=1, tiled=True),
        lax.psum_scatter(grad_down, "vocab", scatter_dimension=0, tiled=True),
        lax.psum_scatter(grad_down_bias, "vocab", scatter_dimension=0, tiled=True),
        lax.psum_scatter(grad_up, "vocab", scatter_dimension=0, tiled=True),
        lax.psum_scatter(grad_up_bias, "vocab", scatter_dimension=0, tiled=True),
        lax.psum_scatter(grad_final_gain, "vocab", scatter_dimension=0, tiled=True),
        lax.psum_scatter(grad_final_bias, "vocab", scatter_dimension=0, tiled=True),
    )
    (
        grad_query_weight,
        grad_query_bias,
        grad_key_weight,
        grad_value_weight,
        grad_value_bias,
        grad_out_weight,
        grad_out_bias,
        grad_attn_gain,
        grad_attn_bias,
        grad_emb_gain,
        grad_emb_bias,
        grad_pos,
        token_type_gradient,
        grad_down,
        grad_down_bias,
        grad_up,
        grad_up_bias,
        grad_final_gain,
        grad_final_bias,
        grad_word,
    ) = (
        lax.psum(grad_query_weight.astype(jnp.bfloat16), "dp").astype(jnp.float32),
        lax.psum(grad_query_bias.astype(jnp.bfloat16), "dp").astype(jnp.float32),
        lax.psum(grad_key_weight.astype(jnp.bfloat16), "dp").astype(jnp.float32),
        lax.psum(grad_value_weight.astype(jnp.bfloat16), "dp").astype(jnp.float32),
        lax.psum(grad_value_bias.astype(jnp.bfloat16), "dp").astype(jnp.float32),
        lax.psum(grad_out_weight.astype(jnp.bfloat16), "dp").astype(jnp.float32),
        lax.psum(grad_out_bias.astype(jnp.bfloat16), "dp").astype(jnp.float32),
        lax.psum(grad_attn_gain.astype(jnp.bfloat16), "dp").astype(jnp.float32),
        lax.psum(grad_attn_bias.astype(jnp.bfloat16), "dp").astype(jnp.float32),
        lax.psum(grad_emb_gain.astype(jnp.bfloat16), "dp").astype(jnp.float32),
        lax.psum(grad_emb_bias.astype(jnp.bfloat16), "dp").astype(jnp.float32),
        lax.psum(grad_pos.astype(jnp.bfloat16), "dp").astype(jnp.float32),
        lax.psum(token_type_gradient.astype(jnp.bfloat16), "dp").astype(jnp.float32),
        lax.psum(grad_down.astype(jnp.bfloat16), "dp").astype(jnp.float32),
        lax.psum(grad_down_bias.astype(jnp.bfloat16), "dp").astype(jnp.float32),
        lax.psum(grad_up.astype(jnp.bfloat16), "dp").astype(jnp.float32),
        lax.psum(grad_up_bias.astype(jnp.bfloat16), "dp").astype(jnp.float32),
        lax.psum(grad_final_gain.astype(jnp.bfloat16), "dp").astype(jnp.float32),
        lax.psum(grad_final_bias.astype(jnp.bfloat16), "dp").astype(jnp.float32),
        lax.psum(grad_word.astype(jnp.bfloat16), "dp").astype(jnp.float32),
    )
    return (
        encoded.reshape(seq_count, seq_len, width),
        grad_word,
        grad_pos,
        token_type_gradient,
        grad_emb_gain,
        grad_emb_bias,
        grad_query_weight,
        grad_query_bias,
        grad_key_weight,
        grad_value_weight,
        grad_value_bias,
        grad_out_weight,
        grad_out_bias,
        grad_attn_gain,
        grad_attn_bias,
        grad_up,
        grad_up_bias,
        grad_down,
        grad_down_bias,
        grad_final_gain,
        grad_final_bias,
    )


def solution(mesh):
    placed = (
        P(("dp", "vocab"), None),
        P(("dp", "vocab"), None),
        P(("dp", "vocab")),
        P("vocab", None),
        P(),
        P(),
        P(),
        P(),
        P(),
        P(),
        P(),
        P(),
        P(),
        P(),
        P(),
        P(),
        P(),
        P(),
        P(),
        P(),
        P(),
        P(),
        P(),
        P(("dp", "vocab"), None, None),
    )
    return jax.shard_map(
        local,
        mesh=mesh,
        in_specs=placed,
        out_specs=(
            P(("dp", "vocab"), None, None),
            P("vocab", None),
            P("vocab", None),
            P(None, "vocab"),
            P("vocab"),
            P("vocab"),
            P("vocab", None),
            P("vocab"),
            P("vocab", None),
            P("vocab", None),
            P("vocab"),
            P("vocab", None),
            P("vocab"),
            P("vocab"),
            P("vocab"),
            P("vocab", None),
            P("vocab"),
            P("vocab", None),
            P("vocab"),
            P("vocab"),
            P("vocab"),
        ),
        check_vma=False,
    )
```

profile of v0, /device:TPU:0, one launch (start us, length us, event | category | flops | bytes accessed | tf_op | source)
XLA Modules:
  0.0 1033.5 jit_solution(1598047318248244611)
XLA Ops:
  18.1 11.7 %all_to_all.19 = s32[8,1,256]{2,1,0:T(1,128)S(1)} all-to-all(s32[8,1,256]{2,1,0:T(1,128)S(1)} %bitcast.272), channel_id=1, replica_groups=mesh['dp'=4,'vocab'=8] {'vocab'}, dimensions={0} | all-to-all | bytes 16384 | tf_op jit(solution)/shard_map/all_to_all | solution.py:119
  30.4 13.5 %gather_fusion = bf16[2048,768]{1,0:T(8,128)(2,1)} fusion(bf16[3840,768]{1,0:T(8,128)(2,1)} %param.31, s32[2048]{0:T(1024)S(1)} %broadcast_clamp_fusion), kind=kCustom, calls=%fused_computation | custom fusion | bytes 6299648 | tf_op jit(solution)/shard_map/gather | solution.py:121
  52.8 71.1 %all-to-all-done.1 = bf16[8,256,768]{2,1,0:T(8,128)(2,1)} async-done(((bf16[8,256,768]{2,1,0:T(8,128)(2,1)}), bf16[8,256,768]{2,1,0:T(8,128)(2,1)}, u32[]{:S(2)}, u32[]{:S(2)}) %all-to-all-start.1) | async-done | bytes 3145760 | tf_op jit(solution)/shard_map/all_to_all | solution.py:123
  123.9 7.9 gather_fusion.1
  167.7 25.7 %while.26 = (s32[]{:T(128)}, bf16[2,512,12,64]{1,3,2,0:T(8,128)(2,1)}, f32[2,12,512,1]{2,1,3,0:T(8,128)}, bf16[2,512,12,64]{1,3,2,0:T(8,128)(2,1)}, s32[2]{0:T(1...) while((s32[]{:T(128)}, ...), condition=%wide.region_9.10_spmd, body=%wide.region_6.9_spmd.sunk | while | flops 843442688 | bytes 47411340 | solution.py:147
  201.9 35.5 %multiply_convert_fusion.1 = (bf16[1024,3072]{1,0:T(8,128)(2,1)S(1)}, f32[1024,3072]{1,0:T(8,128)}, f32[1024,3072]{1,0:T(8,128)}) fusion(f32[3072]{0:T(1024)S(1)} %copy-done.74, bf16[768,3072]{1,0:T(8,128)(2,1)S(1)} %bitcast.284, f32[1024,768]{1,0:T(8,128)S(1)} %get-tuple-element.280, f32[768]{0:T(1024)S(1)} %copy-done.48, f32[768]{0:T(1024)S(1)} %copy-done.42, ...), kind=kOutput, calls=%fused_computation.64 | convolution fusion | flops 5043388416 | bytes 39348224 | tf_op jit(solution)/shard_map/dot_general | solution.py:23
  237.5 5.4 fusion.98
  249.6 19.6 %fusion.100 = (f32[3072]{0:T(1024)}, bf16[1024,3072]{1,0:T(8,128)(2,1)}) fusion(f32[1024,3072]{1,0:T(8,128)} %get-tuple-element.265, bf16[3072,768]{1,0:T(8,128)(2,1)} %param.47, f32[1024,768]{1,0:T(8,128)} %get-tuple-element.263, f32[1024]{0:T(1024)S(1)} %negate_multiply_fusion.3, f32[1024,3072]{1,0:T(8,128)} %get-tuple-element.281, f32[3072]{0:T(1024)S(1)} %copy-done.74), kind=kOutput, calls=%fused_computation.197 | convolution fusion | flops 4883739648 | bytes 39350272 | tf_op jit(solution)/shard_map/dot_general | solution.py:33
  269.2 11.6 %multiply_reduce_fusion.1 = (f32[768]{0:T(1024)}, f32[1024]{0:T(1024)S(1)}, f32[768]{0:T(1024)}, f32[1024,768]{1,0:T(8,128)S(1)}) fusion(f32[1024,768]{1,0:T(8,128)} %copy-done.7, f32[1024]{0:T(1024)S(1)} %fusion.81, f32[1024]{0:T(1024)S(1)} %broadcast_multiply_fusion.1, f32[768]{0:T(1024)S(1)} %copy-done.42, bf16[768,3072]{1,0:T(8,128)(2,1)} %param.45, ...), kind=kOutput, calls=%fused_computation.96 | convolution fusion | flops 4839699456 | bytes 20472832 | tf_op jit(solution)/shard_map/dot_general | solution.py:33
  294.0 55.2 %while.27 = (s32[]{:T(128)}, f32[2,512,12,64]{1,3,2,0:T(8,128)}, bf16[2,512,12,64]{1,3,2,0:T(8,128)(2,1)}, f32[2,512,12,64]{1,3,2,0:T(8,128)}, bf16[2,512,12,64]...) while((s32[]{:T(128)}, f32[2,512,12,64]{1,3,2,0:T(8,128)}, ...), condition=%wide.region_20.21_spmd, body=%wide.region_18.20_spmd.sunk | while | flops 2061232640 | bytes 186580400 | solution.py:175
  301.6 7.3 multiply_reduce_fusion.9
  309.0 7.2 multiply_convert_fusion.3
  328.9 7.3 multiply_reduce_fusion.9
  336.3 7.2 multiply_convert_fusion.3
  349.1 5.5 fusion.94
  374.9 5.3 fusion.86
  394.2 10.7 %fusion.85 = f32[3072,768]{1,0:T(8,128)} fusion(bf16[1024,3072]{1,0:T(8,128)(2,1)} %copy-done.82, f32[1024,768]{1,0:T(8,128)} %get-tuple-element.263, f32[1024]{0:T(1024)S(1)} %copy-done.58), kind=kOutput, calls=%fused_computation.185 | convolution fusion | flops 4833411072 | bytes 18878464 | tf_op jit(solution)/shard_map/dot_general | solution.py:27
  405.6 11.3 %fusion.60 = f32[768,3072]{1,0:T(8,128)} fusion(bf16[1024,3072]{1,0:T(8,128)(2,1)} %get-tuple-element.288, f32[1024,768]{1,0:T(8,128)} %copy-done.7, f32[768]{0:T(1024)S(1)} %copy-done.49, f32[768]{0:T(1024)S(1)} %copy-done.43, f32[1024]{0:T(1024)S(1)} %copy-done.39, f32[1024]{0:T(1024)S(1)} %copy-done.37), kind=kOutput, calls=%fused_computation.101 | convolution fusion | flops 4835770368 | bytes 18888704 | tf_op jit(solution)/shard_map/dot_general | solution.py:27
  416.9 8.7 scatter_custom_fusion.1
  435.1 5.3 convolution_bitcast_fusion
  442.1 5.9 reduce-scatter.19.cloned.1.call-done
  449.6 70.5 %reduce-scatter.15.cloned.1.call-done = f32[96,768]{1,0:T(8,128)} async-done(((f32[768,768]{1,0:T(8,128)}), f32[96,768]{1,0:T(8,128)}) %reduce-scatter.15.cloned.1.call-update) | async-done | bytes 294928 | tf_op jit(solution)/shard_map/reduce_scatter | solution.py:246
  521.7 44.2 %reduce-scatter.13.cloned.1.call-done = f32[96,768]{1,0:T(8,128)} async-done(((f32[768,768]{1,0:T(8,128)}), f32[96,768]{1,0:T(8,128)}) %reduce-scatter.13.cloned.1.call-update) | async-done | bytes 294928 | tf_op jit(solution)/shard_map/reduce_scatter | solution.py:244
  567.6 36.2 %reduce-scatter.17.cloned.1.call-done = f32[96,768]{1,0:T(8,128)} async-done(((f32[768,768]{1,0:T(8,128)}), f32[96,768]{1,0:T(8,128)}) %reduce-scatter.17.cloned.1.call-update) | async-done | bytes 294928 | tf_op jit(solution)/shard_map/reduce_scatter | solution.py:247
  610.1 20.6 %scatter_custom_fusion.2 = f32[3840,768]{1,0:T(8,128)} fusion(s32[2048]{0:T(1024)} %bitcast.271, f32[2048,768]{1,0:T(8,128)} %bitcast.250, f32[]{:T(128)} %constant.47.clone.1), kind=kCustom, calls=%fused_computation.79 | custom fusion | flops 1572864 | bytes 11796992 | tf_op jit(solution)/shard_map/scatter-add | solution.py:221
  630.7 7.5 convert_element_type.255
  638.2 66.6 %reduce-scatter.23.cloned.1.call-done = f32[384,768]{1,0:T(8,128)} async-done(((f32[3072,768]{1,0:T(8,128)}), f32[384,768]{1,0:T(8,128)}) %reduce-scatter.23.cloned.1.call-update) | async-done | bytes 1179664 | tf_op jit(solution)/shard_map/reduce_scatter | solution.py:257
  706.9 98.1 %reduce-scatter.21.cloned.1.call-done = f32[96,3072]{1,0:T(8,128)} async-done(((f32[768,3072]{1,0:T(8,128)}), f32[96,3072]{1,0:T(8,128)}) %reduce-scatter.21.cloned.1.call-update) | async-done | bytes 1179664 | tf_op jit(solution)/shard_map/reduce_scatter | solution.py:259
  814.6 26.6 %all-reduce.11 = (bf16[768]{0:T(1024)(128)(2,1)S(1)}, bf16[768]{0:T(1024)(128)(2,1)S(1)}, bf16[768]{0:T(1024)(128)(2,1)S(1)}, bf16[768]{0:T(1024)(128)(2,1)S(1)}...) all-reduce(f32[768]{0:T(1024)S(1)} %get-tuple-element.190, ...), channel_id=4, replica_groups=mesh['dp'=4,'vocab'=8] {'vocab'}, use_global_device_ids=true, to_apply=%region_32.33.clone | all-reduce | flops 10752 | bytes 64512
  842.8 10.4 %all-reduce.12 = (bf16[2,96]{1,0:T(2,128)(2,1)S(1)}, bf16[96]{0:T(256)(128)(2,1)S(1)}, bf16[96]{0:T(256)(128)(2,1)S(1)}, bf16[96]{0:T(256)(128)(2,1)S(1)}, bf16[...) all-reduce(bf16[2,96]{1,0:T(2,128)(2,1)S(1)} %copy.120, ...), channel_id=1, replica_groups=mesh['dp'=4,'vocab'=8] {'dp'}, use_global_device_ids=true, to_apply=%region_30.31 | all-reduce | flops 1536 | bytes 6144 | tf_op jit(solution)/shard_map/psum | solution.py:298
  859.5 147.5 %all-reduce.16.cloned.1.call-done = (bf16[3840,768]{1,0:T(8,128)(2,1)}, bf16[64,768]{1,0:T(8,128)(2,1)}, bf16[96,768]{1,0:T(8,128)(2,1)}, bf16[96,768]{1,0:T(8,1...) async-done(((bf16[3840,768]{1,0:T(8,128)(2,1)}, bf16[64,768]{1,0:T(8,128)(2,1)}, ...) | async-done | bytes 7766032 | tf_op jit(solution)/shard_map/psum | solution.py:305
  1018.5 8.2 convert_element_type.256
  (378 shorter events, 221.4 us)
Async XLA Ops:
  7.2 190.3 %copy-start = (bf16[768,768]{1,0:T(8,128)(2,1)S(1)}, bf16[768,768]{1,0:T(8,128)(2,1)}, u32[]{:S(2)}) copy-start(bf16[768,768]{1,0:T(8,128)(2,1)} %param.41) | copy-start | bytes 3538948
  13.7 39.0 %copy-start.59 = (s32[1024,1]{0,1:T(1,128)}, s32[1024,1]{0,1:T(1,128)S(1)}, u32[]{:S(2)}) copy-start(s32[1024,1]{0,1:T(1,128)S(1)} %compare_select_fusion) | copy-start | bytes 12292
  47.8 76.1 %all-to-all-start.1 = ((bf16[8,256,768]{2,1,0:T(8,128)(2,1)}), bf16[8,256,768]{2,1,0:T(8,128)(2,1)}, u32[]{:S(2)}, u32[]{:S(2)}) async-start(bf16[8,256,768]{2,1,0:T(8,128)(2,1)} %broadcast_select_fusion), calls=%async_computation.1 | async-start | bytes 6291456 | tf_op jit(solution)/shard_map/all_to_all | solution.py:123
  52.4 388.1 %reduce-scatter.11.cloned.1.call-start = ((), (), s32[]{:S(2)}) async-start(), calls=%async_computation.11 | async-start | bytes 1769472 | tf_op jit(solution)/shard_map/reduce_scatter | solution.py:255
  123.9 7.9 copy-start.61
  123.9 7.9 copy-start.69
  197.5 39.9 %slice-start = ((s8[4718592]{0:T(1024)(128)(4,1)}), s8[4194304]{0:T(1024)(128)(4,1)S(1)}, s32[]{:S(2)}) async-start(s8[4718592]{0:T(1024)(128)(4,1)} %bitcast.281), calls=%async_computation.20 | async-start | bytes 8388608
  199.2 38.2 %copy-start.7 = (f32[1024,768]{1,0:T(8,128)}, f32[1024,768]{1,0:T(8,128)S(1)}, u32[]{:S(2)}) copy-start(f32[1024,768]{1,0:T(8,128)S(1)} %get-tuple-element.280) | copy-start | bytes 9437188
  199.3 81.5 %copy-start.36 = (f32[1024]{0:T(1024)}, f32[1024]{0:T(1024)S(1)}, u32[]{:S(2)}) copy-start(f32[1024]{0:T(1024)S(1)} %broadcast_multiply_fusion.1) | copy-start | bytes 12292
  201.9 78.9 %copy-start.38 = (f32[1024]{0:T(1024)}, f32[1024]{0:T(1024)S(1)}, u32[]{:S(2)}) copy-start(f32[1024]{0:T(1024)S(1)} %fusion.81) | copy-start | bytes 12292
  201.9 35.5 %slice-start.1 = ((s8[4718592]{0:T(1024)(128)(4,1)}), s8[524288]{0:T(1024)(128)(4,1)S(1)}, s32[]{:S(2)}) async-start(s8[4718592]{0:T(1024)(128)(4,1)} %bitcast.281), calls=%async_computation.21 | async-start | bytes 1048576
  201.9 35.6 %copy-start.78 = (f32[768]{0:T(1024)S(1)}, f32[768]{0:T(1024)}, u32[]{:S(2)}) copy-start(f32[768]{0:T(1024)} %param.48) | copy-start | bytes 9220
  249.6 19.6 %copy-start.57 = (f32[1024]{0:T(1024)}, f32[1024]{0:T(1024)S(1)}, u32[]{:S(2)}) copy-start(f32[1024]{0:T(1024)S(1)} %negate_multiply_fusion.3) | copy-start | bytes 12292
  269.2 11.6 %copy-start.8 = (f32[1024,768]{1,0:T(8,128)S(1)}, f32[1024,768]{1,0:T(8,128)}, u32[]{:S(2)}) copy-start(f32[1024,768]{1,0:T(8,128)} %copy-done.7) | copy-start | bytes 9437188
  287.1 6.9 copy-start.35
  287.1 6.9 copy-start.80
  301.6 7.3 copy-start.19
  309.0 7.3 copy-start.23
  328.9 7.3 copy-start.19
  336.3 7.3 copy-start.23
  374.9 73.1 %reduce-scatter.19.cloned.1.call-start = ((), (), s32[]{:S(2)}) async-start(), calls=%async_computation.15 | async-start | bytes 2654208 | tf_op jit(solution)/shard_map/reduce_scatter | solution.py:249
  380.2 139.9 %reduce-scatter.15.cloned.1.call-start = ((), (), s32[]{:S(2)}) async-start(), calls=%async_computation.13 | async-start | bytes 2654208 | tf_op jit(solution)/shard_map/reduce_scatter | solution.py:246
  385.0 181.0 %reduce-scatter.13.cloned.1.call-start = ((), (), s32[]{:S(2)}) async-start(), calls=%async_computation.12 | async-start | bytes 2654208 | tf_op jit(solution)/shard_map/reduce_scatter | solution.py:244
  389.9 213.9 %reduce-scatter.17.cloned.1.call-start = ((), (), s32[]{:S(2)}) async-start(), calls=%async_computation.14 | async-start | bytes 2654208 | tf_op jit(solution)/shard_map/reduce_scatter | solution.py:247
  394.2 310.6 %reduce-scatter.23.cloned.1.call-start = ((), (), s32[]{:S(2)}) async-start(), calls=%async_computation.17 | async-start | bytes 10616832 | tf_op jit(solution)/shard_map/reduce_scatter | solution.py:257
  404.9 400.0 %reduce-scatter.21.cloned.1.call-start = ((), (), s32[]{:S(2)}) async-start(), calls=%async_computation.16 | async-start | bytes 10616832 | tf_op jit(solution)/shard_map/reduce_scatter | solution.py:259
  430.4 175.1 %all-to-all-start.2 = ((bf16[8,256,768]{2,1,0:T(8,128)(2,1)}), bf16[8,256,768]{2,1,0:T(8,128)(2,1)}, u32[]{:S(2)}, u32[]{:S(2)}) async-start(bf16[8,256,768]{2,1,0:T(8,128)(2,1)} %bitcast.248), calls=%async_computation.2 | async-start | bytes 6291456 | tf_op jit(solution)/shard_map/all_to_all | solution.py:209
  435.0 170.5 %copy-start.56 = (pred[8,256]{1,0:T(8,128)(4,1)S(1)}, pred[8,256]{1,0:T(8,128)(4,1)}, u32[]{:S(2)}) copy-start(pred[8,256]{1,0:T(8,128)(4,1)} %copy-done.55) | copy-start | bytes 6148
  435.0 406.9 %reduce-scatter.25.cloned.1.call-start = ((), (), s32[]{:S(2)}) async-start(), calls=%async_computation.18 | async-start | bytes 442368
  440.4 566.6 %all-reduce.16.cloned.1.call-start = ((), (), s32[]{:S(2)}) async-start(), calls=%async_computation.19 | async-start | bytes 15532032 | tf_op jit(solution)/shard_map/psum | solution.py:305
  1007.0 10.4 %copy-start.34 = (bf16[384,768]{1,0:T(8,128)(2,1)S(1)}, bf16[384,768]{1,0:T(8,128)(2,1)}, u32[]{:S(2)}) copy-start(bf16[384,768]{1,0:T(8,128)(2,1)} %get-tuple-element.257) | copy-start | bytes 1769476
  1018.5 8.2 copy-start.1
  (76 other events, 195.0 us)
Sparse Core Ops, SparseCore 0:
  375.0 33.1 reduce-scatter.10
  410.5 37.4 reduce-scatter.18
  450.3 69.7 reduce-scatter.14
  522.3 43.6 reduce-scatter.12
  568.1 35.6 reduce-scatter.16
  606.0 98.7 reduce-scatter.22
  707.1 97.8 reduce-scatter.20
  807.2 29.1 reduce-scatter.24
  843.5 163.4 all-reduce.15
where the time goes:
time: 1040 us; the launch traced here: 1030 us
  waiting for transfers between devices  540 us (52%)
  matrix products  186 us (18%)
  other arithmetic  137 us (13%)
  local copies, waits for them, and re-layouts  95 us (9%)
  blocking collectives  48.7 us (5%)
  between operations  16.5 us (2%)
    psum x1, waiting for transfers between devices, local(): lax.psum(grad_word.astype(jnp.bfloat16), 'dp').astype(jnp.float32)  148 us
    reduce_scatter x1, waiting for transfers between devices, local(): lax.psum_scatter(grad_up, 'vocab', scatter_dimension=0, tiled=True)  98.1 us
    all_to_all x1, waiting for transfers between devices, local(): lax.all_to_all(found, 'vocab', split_axis=0, concat_axis=0, tiled=True)  71.1 us
    reduce_scatter x1, waiting for transfers between devices, local(): lax.psum_scatter(grad_key_weight, 'vocab', scatter_dimension=0, tiled=True)  70.5 us
    reduce_scatter x1, waiting for transfers between devices, local(): lax.psum_scatter(grad_down, 'vocab', scatter_dimension=0, tiled=True)  66.6 us
    dot_general x6, matrix products, matmul(): return jnp.dot(left, right, preferred_element_type=jnp.float32)  50.3 us
    reduce_scatter x1, waiting for transfers between devices, local(): lax.psum_scatter(grad_query_weight, 'vocab', scatter_dimension=0, tiled=T...  44.2 us
    dot_general x6, matrix products, matmul_tn(): lax.dot_general(left, right, (((0,), (0,)), ((), ())), preferred_element_...  40.9 us
  transfers between devices with their start and end apart: 11, of which 8 were waited for; matrix products, arithmetic and copies ran while one was open for 11% of the time, Pallas kernels for 0%

commit v1 on v0

--- a/solution.py
+++ b/solution.py
@@ -72,6 +72,100 @@
         jnp.einsum("hqk,qhd->khd", grad_scores, query, preferred_element_type=jnp.float32) * scale
     )
     return (grad_query, grad_keys, grad_values)
+
+
+def swap(value, axis_name, bit):
+    size = lax.axis_size(axis_name)
+    return lax.ppermute(value, axis_name, [(i, i ^ bit) for i in range(size)])
+
+
+def pick(value, index, axis):
+    return lax.dynamic_index_in_dim(value, index, axis, keepdims=False)
+
+
+def plus(left, right):
+    return (left.astype(jnp.float32) + right.astype(jnp.float32)).astype(jnp.bfloat16)
+
+
+def dp_bits():
+    index = lax.axis_index("dp")
+    return lax.rem(index, 2), index // 2
+
+
+def reorder(own, across_x, across_y, across_both):
+    xb, yb = dp_bits()
+    flip_x, flip_y = xb == 1, yb == 1
+    rows = [[own, across_y], [across_x, across_both]]
+    rows = [
+        [jnp.where(flip_x, rows[1 - i][j], rows[i][j]) for j in range(2)] for i in range(2)
+    ]
+    rows = [
+        [jnp.where(flip_y, rows[i][1 - j], rows[i][j]) for j in range(2)] for i in range(2)
+    ]
+    return rows
+
+
+def sum_over_all(grad):
+    size = lax.axis_size("vocab")
+    me = lax.axis_index("vocab")
+    core = lax.rem(me, 2)
+    place = me // 2
+    places = size // 2
+    total, n = grad.shape
+    r = total // size
+    xb, yb = dp_bits()
+    grad = grad.reshape(places, 2, r, n)
+    other = swap(pick(grad, 1 - core, 1), "vocab", 1)
+    held = plus(pick(grad, core, 1), other).reshape(places, 2, 2, r // 4, n)
+    first, last = held[: places // 2], held[places // 2 :]
+    first_in = swap(pick(first, 1 - xb, 1), "dp", 1)
+    last_in = swap(pick(last, 1 - yb, 2), "dp", 2)
+    first = plus(pick(first, xb, 1), first_in)
+    last = plus(pick(last, yb, 2), last_in)
+    first_in = swap(pick(first, 1 - yb, 1), "dp", 2)
+    last_in = swap(pick(last, 1 - xb, 1), "dp", 1)
+    first = plus(pick(first, yb, 1), first_in)
+    last = plus(pick(last, xb, 1), last_in)
+    held = jnp.concatenate([first, last], 0)
+    summed = pick(held, place, 0).astype(jnp.float32)
+    for step in range(1, places):
+        block = pick(held, lax.rem(place + step, places), 0)
+        block = lax.ppermute(
+            block, "vocab", [(i, (i + 2 * step) % size) for i in range(size)]
+        )
+        summed = summed + block.astype(jnp.float32)
+    own = summed.astype(jnp.bfloat16)
+    across_x = swap(own, "dp", 1)
+    across_y = swap(own, "dp", 2)
+    half = n // 2
+    both = jnp.concatenate(
+        [swap(across_x[:, :half], "dp", 2), swap(across_y[:, half:], "dp", 1)], 1
+    )
+    rows = reorder(own, across_x, across_y, both)
+    return jnp.stack([rows[0][0], rows[0][1], rows[1][0], rows[1][1]]).reshape(r, n).astype(jnp.float32)
+
+
+def sum_over_dp(grad):
+    rows, n = grad.shape
+    xb, yb = dp_bits()
+    held = grad.reshape(2, 2, 2, rows // 8, n)
+    first, last = held[0], held[1]
+    first_in = swap(pick(first, 1 - xb, 0), "dp", 1)
+    last_in = swap(pick(last, 1 - yb, 1), "dp", 2)
+    first = plus(pick(first, xb, 0), first_in)
+    last = plus(pick(last, yb, 1), last_in)
+    first_in = swap(pick(first, 1 - yb, 0), "dp", 2)
+    last_in = swap(pick(last, 1 - xb, 0), "dp", 1)
+    first = plus(pick(first, yb, 0), first_in)
+    last = plus(pick(last, xb, 0), last_in)
+    first_x = swap(first, "dp", 1)
+    last_y = swap(last, "dp", 2)
+    first_y = swap(jnp.stack([first, first_x]), "dp", 2)
+    last_x = swap(jnp.stack([last, last_y]), "dp", 1)
+    a = reorder(first, first_x, first_y[0], first_y[1])
+    b = reorder(last, last_x[0], last_y, last_x[1])
+    parts = [p for group in (a, b) for line in group for p in line]
+    return jnp.concatenate(parts, 0).astype(jnp.float32)
 
 
 def local(
@@ -201,109 +295,84 @@
     token_type_gradient = jnp.einsum(
         "nox,noh->xh", selection_matrix, embedding_output_gradient, precision=lax.Precision.HIGHEST
     )
-    outgoing = (
-        jnp.zeros((owners * capacity, width), jnp.float32)
-        .at[slot]
-        .set(embedding_output_gradient.reshape(tokens, width))
-    )
-    incoming = lax.all_to_all(
-        outgoing.reshape(owners, capacity, width).astype(jnp.bfloat16),
-        "vocab",
-        split_axis=0,
-        concat_axis=0,
-        tiled=True,
-    ).astype(jnp.float32)
-    keep_rows = asked >= 0
-    incoming = jnp.where(keep_rows[..., None], incoming, 0.0)
-    grad_word = (
-        jnp.zeros((rows_local, width), jnp.float32)
-        .at[jnp.maximum(asked, 0).reshape(-1)]
-        .add(incoming.reshape(owners * capacity, width))
-    )
+    bf = jnp.bfloat16
+    per = width // owners
+    grad_down_all = sum_over_all(grad_down.astype(bf))
+    grad_up_all = sum_over_all(grad_up.astype(bf))
+    places = slot[None, :] == jnp.arange(owners * capacity)[:, None]
+    outgoing = matmul(
+        places.astype(bf), embedding_output_gradient.reshape(tokens, width).astype(bf)
+    ).astype(bf)
+    hits = (jnp.arange(rows_local)[:, None] == asked.reshape(-1)[None, :]).astype(bf)
+    pieces = []
+    step = 256
+    for start in range(0, width, step):
+        incoming = lax.all_to_all(
+            outgoing[:, start : start + step].reshape(owners, capacity, step),
+            "vocab",
+            split_axis=0,
+            concat_axis=0,
+            tiled=True,
+        )
+        dense = matmul(hits, incoming.reshape(owners * capacity, step)).astype(bf)
+        pieces.append(sum_over_dp(dense))
+    grad_word = jnp.concatenate(pieces, 1)
+    small = jnp.stack(
+        [
+            grad_query_bias,
+            grad_value_bias,
+            grad_out_bias,
+            grad_attn_gain,
+            grad_attn_bias,
+            grad_emb_gain,
+            grad_emb_bias,
+            grad_down_bias,
+            grad_final_gain,
+            grad_final_bias,
+            token_type_gradient[0],
+            token_type_gradient[1],
+        ]
+    )
+    small = small.reshape(12, owners, per).transpose(1, 0, 2).reshape(owners, 12 * per)
+    small = jnp.concatenate([small, grad_up_bias.reshape(owners, 4 * per)], 1)
+    wide = 4 * width
+    lines = (seq_len // owners) * width // wide
+    rest = per // 3 - lines
+    small_lines = jnp.pad(small, ((0, 0), (0, rest * wide - 16 * per))).reshape(owners, rest, wide)
+    mixed_grads = jnp.concatenate(
+        [grad_query_weight, grad_key_weight, grad_value_weight, grad_out_weight], 1
+    ).astype(bf)
+    packed = jnp.concatenate(
+        [
+            mixed_grads.reshape(owners, per, wide),
+            grad_pos.astype(bf).reshape(owners, lines, wide),
+            small_lines.astype(bf),
+        ],
+        1,
+    )
+    packed = sum_over_all(packed.reshape(-1, wide))
+    weights = packed[:per]
+    grad_query_weight = weights[:, :width]
+    grad_key_weight = weights[:, width : 2 * width]
+    grad_value_weight = weights[:, 2 * width : 3 * width]
+    grad_out_weight = weights[:, 3 * width :]
+    grad_pos = packed[per : per + lines].reshape(seq_len // owners, width)
+    small = packed[per + lines :].reshape(-1)[: 16 * per].reshape(16, per)
     (
-        grad_query_weight,
         grad_query_bias,
-        grad_key_weight,
-        grad_value_weight,
         grad_value_bias,
-        grad_out_weight,
         grad_out_bias,
         grad_attn_gain,
         grad_attn_bias,
         grad_emb_gain,
         grad_emb_bias,
-        grad_pos,
-        token_type_gradient,
-        grad_down,
         grad_down_bias,
-        grad_up,
-        grad_up_bias,
         grad_final_gain,
         grad_final_bias,
-    ) = (
-        lax.psum_scatter(grad_query_weight, "vocab", scatter_dimension=0, tiled=True),
-        lax.psum_scatter(grad_query_bias, "vocab", scatter_dimension=0, tiled=True),
-        lax.psum_scatter(grad_key_weight, "vocab", scatter_dimension=0, tiled=True),
-        lax.psum_scatter(grad_value_weight, "vocab", scatter_dimension=0, tiled=True),
-        lax.psum_scatter(grad_value_bias, "vocab", scatter_dimension=0, tiled=True),
-        lax.psum_scatter(grad_out_weight, "vocab", scatter_dimension=0, tiled=True),
-        lax.psum_scatter(grad_out_bias, "vocab", scatter_dimension=0, tiled=True),
-        lax.psum_scatter(grad_attn_gain, "vocab", scatter_dimension=0, tiled=True),
-        lax.psum_scatter(grad_attn_bias, "vocab", scatter_dimension=0, tiled=True),
-        lax.psum_scatter(grad_emb_gain, "vocab", scatter_dimension=0, tiled=True),
-        lax.psum_scatter(grad_emb_bias, "vocab", scatter_dimension=0, tiled=True),
-        lax.psum_scatter(grad_pos, "vocab", scatter_dimension=0, tiled=True),
-        lax.psum_scatter(token_type_gradient, "vocab", scatter_dimension=1, tiled=True),
-        lax.psum_scatter(grad_down, "vocab", scatter_dimension=0, tiled=True),
-        lax.psum_scatter(grad_down_bias, "vocab", scatter_dimension=0, tiled=True),
-        lax.psum_scatter(grad_up, "vocab", scatter_dimension=0, tiled=True),
-        lax.psum_scatter(grad_up_bias, "vocab", scatter_dimension=0, tiled=True),
-        lax.psum_scatter(grad_final_gain, "vocab", scatter_dimension=0, tiled=True),
-        lax.psum_scatter(grad_final_bias, "vocab", scatter_dimension=0, tiled=True),
-    )
-    (
-        grad_query_weight,
-        grad_query_bias,
-        grad_key_weight,
-        grad_value_weight,
-        grad_value_bias,
-        grad_out_weight,
-        grad_out_bias,
-        grad_attn_gain,
-        grad_attn_bias,
-        grad_emb_gain,
-        grad_emb_bias,
-        grad_pos,
-        token_type_gradient,
-        grad_down,
-        grad_down_bias,
-        grad_up,
-        grad_up_bias,
-        grad_final_gain,
-        grad_final_bias,
-        grad_word,
-    ) = (
-        lax.psum(grad_query_weight.astype(jnp.bfloat16), "dp").astype(jnp.float32),
-        lax.psum(grad_query_bias.astype(jnp.bfloat16), "dp").astype(jnp.float32),
-        lax.psum(grad_key_weight.astype(jnp.bfloat16), "dp").astype(jnp.float32),
-        lax.psum(grad_value_weight.astype(jnp.bfloat16), "dp").astype(jnp.float32),
-        lax.psum(grad_value_bias.astype(jnp.bfloat16), "dp").astype(jnp.float32),
-        lax.psum(grad_out_weight.astype(jnp.bfloat16), "dp").astype(jnp.float32),
-        lax.psum(grad_out_bias.astype(jnp.bfloat16), "dp").astype(jnp.float32),
-        lax.psum(grad_attn_gain.astype(jnp.bfloat16), "dp").astype(jnp.float32),
-        lax.psum(grad_attn_bias.astype(jnp.bfloat16), "dp").astype(jnp.float32),
-        lax.psum(grad_emb_gain.astype(jnp.bfloat16), "dp").astype(jnp.float32),
-        lax.psum(grad_emb_bias.astype(jnp.bfloat16), "dp").astype(jnp.float32),
-        lax.psum(grad_pos.astype(jnp.bfloat16), "dp").astype(jnp.float32),
-        lax.psum(token_type_gradient.astype(jnp.bfloat16), "dp").astype(jnp.float32),
-        lax.psum(grad_down.astype(jnp.bfloat16), "dp").astype(jnp.float32),
-        lax.psum(grad_down_bias.astype(jnp.bfloat16), "dp").astype(jnp.float32),
-        lax.psum(grad_up.astype(jnp.bfloat16), "dp").astype(jnp.float32),
-        lax.psum(grad_up_bias.astype(jnp.bfloat16), "dp").astype(jnp.float32),
-        lax.psum(grad_final_gain.astype(jnp.bfloat16), "dp").astype(jnp.float32),
-        lax.psum(grad_final_bias.astype(jnp.bfloat16), "dp").astype(jnp.float32),
-        lax.psum(grad_word.astype(jnp.bfloat16), "dp").astype(jnp.float32),
-    )
+    ) = [small[i] for i in range(10)]
+    token_type_gradient = small[10:12]
+    grad_up_bias = small[12:].reshape(-1)
+    grad_up, grad_down = grad_up_all, grad_down_all
     return (
         encoded.reshape(seq_count, seq_len, width),
         grad_word,

time: 1040 us -> 790 us (0.76)
  waiting for transfers between devices: 540 us -> 288 us
  starting transfers between devices: 9.71 us -> 87 us
  other arithmetic: 137 us -> 86.7 us
  blocking collectives: 48.7 us -> 11.7 us
  matrix products: 186 us -> 200 us
  between operations: 16.5 us -> 2.97 us
  local copies, waits for them, and re-layouts: 95 us -> 108 us
    reduce_scatter x7 -> x0, waiting for transfers between devices: 322 us -> none  [the longest x1 98.1 us: local(): lax.psum_scatter(grad_up, 'vocab', scatter_dimension=0, tiled=True)]
    ppermute x0 -> x60, waiting for transfers between devices: none -> 184 us  [the longest x51 172 us: swap(): return lax.ppermute(value, axis_name, [(i, i ^ bit) for i in range(size)])]
    psum x1 -> x0, waiting for transfers between devices: 148 us -> none  [local(): lax.psum(grad_word.astype(jnp.bfloat16), 'dp').astype(jnp.float32)]
    ppermute x0 -> x60, starting transfers between devices: none -> 68.8 us  [the longest x51 55.3 us: swap(): return lax.ppermute(value, axis_name, [(i, i ^ bit) for i in range(size)])]
    convert_element_type x29 -> x33, other arithmetic: 50.6 us -> 15.5 us  [the longest x27 12.5 us: plus(): (left.astype(jnp.float32) + right.astype(jnp.float32)).astype(jnp.bfloat16)]
    all_to_all x1 -> x3, waiting for transfers between devices: 0.01 us -> 34.7 us  [local(): lax.all_to_all(outgoing[:, start:start + step].reshape(owners, capacity,...]
    dot_general x6 -> x10, matrix products: 50.3 us -> 78.4 us  [matmul(): return jnp.dot(left, right, preferred_element_type=jnp.float32)]
    unnamed x1 -> x0, blocking collectives: 26.6 us -> none
  transfers between devices with their start and end apart: 11 -> 64, of which waited for: 8 -> 34; matrix products, arithmetic and copies ran while one was open for 11% -> 11% of each run, Pallas kernels for 0% -> 0%
where the time goes in v1:
time: 790 us; the launch traced here: 785 us
  waiting for transfers between devices  288 us (36%)
  matrix products  200 us (25%)
  local copies, waits for them, and re-layouts  108 us (14%)
  starting transfers between devices  87 us (11%)
  other arithmetic  86.7 us (11%)
  blocking collectives  11.7 us (1%)
    ppermute x51, waiting for transfers between devices, swap(): return lax.ppermute(value, axis_name, [(i, i ^ bit) for i in range(size)])  172 us
    dot_general x10, matrix products, matmul(): return jnp.dot(left, right, preferred_element_type=jnp.float32)  78.4 us
    all_to_all x1, waiting for transfers between devices, local(): lax.all_to_all(found, 'vocab', split_axis=0, concat_axis=0, tiled=True)  69.1 us
    ppermute x51, starting transfers between devices, swap(): return lax.ppermute(value, axis_name, [(i, i ^ bit) for i in range(size)])  55.3 us
    dot_general x6, matrix products, matmul_nt(): lax.dot_general(left, right, (((1,), (1,)), ((), ())), preferred_element_...  35.2 us
    all_to_all x3, waiting for transfers between devices, local(): lax.all_to_all(outgoing[:, start:start + step].reshape(owners, capacity,...  34.7 us
    dot_general x6, matrix products, matmul_tn(): lax.dot_general(left, right, (((0,), (0,)), ((), ())), preferred_element_...  29.6 us
  transfers between devices with their start and end apart: 64, of which 34 were waited for; matrix products, arithmetic and copies ran while one was open for 11% of the time, Pallas kernels for 0%

profile of v1, /device:TPU:0, one launch (start us, length us, event | category | flops | bytes accessed | tf_op | source)
XLA Modules:
  0.0 785.3 jit_solution(7070408737902939160)
XLA Ops:
  12.1 11.7 %all_to_all.29 = s32[8,1,256]{2,1,0:T(1,128)S(1)} all-to-all(s32[8,1,256]{2,1,0:T(1,128)S(1)} %bitcast.728), channel_id=1, replica_groups=mesh['dp'=4,'vocab'=8] {'vocab'}, dimensions={0} | all-to-all | bytes 16384 | tf_op jit(solution)/shard_map/all_to_all | solution.py:213
  23.9 13.5 %gather_fusion = bf16[2048,768]{1,0:T(8,128)(2,1)} fusion(bf16[3840,768]{1,0:T(8,128)(2,1)} %param.31, s32[2048]{0:T(1024)S(1)} %broadcast_clamp_fusion), kind=kCustom, calls=%fused_computation | custom fusion | bytes 6299648 | tf_op jit(solution)/shard_map/gather | solution.py:215
  47.9 69.1 %all-to-all-done.1 = bf16[8,256,768]{2,1,0:T(8,128)(2,1)} async-done(((bf16[8,256,768]{2,1,0:T(8,128)(2,1)}), bf16[8,256,768]{2,1,0:T(8,128)(2,1)}, u32[]{:S(2)}, u32[]{:S(2)}) %all-to-all-start.1) | async-done | bytes 3145760 | tf_op jit(solution)/shard_map/all_to_all | solution.py:217
  117.0 8.0 %gather_fusion.1 = bf16[1024,768]{1,0:T(8,128)(2,1)} fusion(bf16[2048,768]{1,0:T(8,128)(2,1)} %bitcast.25, s32[1024]{0:T(1024)S(1)} %broadcast_clamp_fusion.1), kind=kCustom, calls=%fused_computation.1 | custom fusion | bytes 3149824 | tf_op jit(solution)/shard_map/gather | solution.py:218
  163.7 25.7 %while.26 = (s32[]{:T(128)}, bf16[2,512,12,64]{1,3,2,0:T(8,128)(2,1)}, f32[2,12,512,1]{2,1,3,0:T(8,128)}, bf16[2,512,12,64]{1,3,2,0:T(8,128)(2,1)}, s32[2]{0:T(1...) while((s32[]{:T(128)}, ...), condition=%wide.region_9.10_spmd, body=%wide.region_6.9_spmd.sunk | while | flops 843442688 | bytes 47411840 | solution.py:241
  197.9 35.3 %multiply_convert_fusion.1 = (bf16[1024,3072]{1,0:T(8,128)(2,1)S(1)}, f32[1024,3072]{1,0:T(8,128)}, f32[1024,3072]{1,0:T(8,128)}) fusion(f32[3072]{0:T(1024)S(1)} %copy-done.82, bf16[768,3072]{1,0:T(8,128)(2,1)S(1)} %bitcast.738, f32[1024,768]{1,0:T(8,128)S(1)} %get-tuple-element.331, f32[768]{0:T(1024)S(1)} %copy-done.87, f32[768]{0:T(1024)S(1)} %copy-done.73, ...), kind=kOutput, calls=%fused_computation.69 | convolution fusion | flops 5043388416 | bytes 39348224 | tf_op jit(solution)/shard_map/dot_general | solution.py:23
  244.9 7.5 convolution_convert_fusion
  252.4 19.4 %fusion.216 = (bf16[3072]{0:T(1024)(128)(2,1)}, bf16[1024,3072]{1,0:T(8,128)(2,1)}) fusion(f32[1024,3072]{1,0:T(8,128)} %get-tuple-element.251, bf16[3072,768]{1,0:T(8,128)(2,1)} %param.47, f32[1024,768]{1,0:T(8,128)} %copy-done.21, f32[1024]{0:T(1024)S(1)} %negate_multiply_fusion.3, f32[1024,3072]{1,0:T(8,128)} %get-tuple-element.332, f32[3072]{0:T(1024)S(1)} %copy-done.82), kind=kOutput, calls=%fused_computation.487 | convolution fusion | flops 4883739648 | bytes 39344128 | tf_op jit(solution)/shard_map/dot_general | solution.py:33
  271.8 10.7 %convolution_convert_fusion.1 = bf16[768,3072]{1,0:T(8,128)(2,1)} fusion(bf16[1024,3072]{1,0:T(8,128)(2,1)} %get-tuple-element.337, f32[1024,768]{1,0:T(8,128)} %copy-done.19, f32[768]{0:T(1024)S(1)} %copy-done.87, f32[768]{0:T(1024)S(1)} %copy-done.73, f32[1024]{0:T(1024)S(1)} %fusion.191, f32[1024]{0:T(1024)S(1)} %broadcast_multiply_fusion.1), kind=kOutput, calls=%fused_computation.93 | convolution fusion | flops 4838129664 | bytes 14170112 | tf_op jit(solution)/shard_map/dot_general | solution.py:27
  282.6 8.9 %multiply_reduce_fusion.2 = (bf16[768]{0:T(1024)(128)(2,1)}, f32[1024]{0:T(1024)S(1)}, bf16[768]{0:T(1024)(128)(2,1)}, f32[1024,768]{1,0:T(8,128)S(1)}) fusion(f32[1024,768]{1,0:T(8,128)S(1)} %copy-done.20, f32[1024]{0:T(1024)S(1)} %fusion.191, f32[1024]{0:T(1024)S(1)} %broadcast_multiply_fusion.1, f32[768]{0:T(1024)S(1)} %copy-done.73, ...), kind=kOutput, calls=%fused_computation.116 | convolution fusion | flops 4839699456 | bytes 20469760 | tf_op jit(solution)/shard_map/dot_general | solution.py:33
  304.9 55.8 %while.27 = (s32[]{:T(128)}, f32[2,512,12,64]{1,3,2,0:T(8,128)}, bf16[2,512,12,64]{1,3,2,0:T(8,128)(2,1)}, f32[2,512,12,64]{1,3,2,0:T(8,128)}, bf16[2,512,12,64]...) while((s32[]{:T(128)}, f32[2,512,12,64]{1,3,2,0:T(8,128)}, ...), condition=%wide.region_20.21_spmd, body=%wide.region_18.20_spmd.sunk | while | flops 2061232640 | bytes 161414480 | solution.py:269
  309.8 7.3 multiply_reduce_fusion.9
  317.1 7.4 multiply_convert_fusion.3
  337.4 7.3 multiply_reduce_fusion.9
  344.7 7.4 multiply_convert_fusion.3
  423.8 10.6 %all-to-all-done.2 = bf16[8,256,256]{2,1,0:T(8,128)(2,1)} async-done(((bf16[8,256,256]{2,1,0:T(8,128)(2,1)}), bf16[8,256,256]{2,1,0:T(8,128)(2,1)}, u32[]{:S(2)}, u32[]{:S(2)}) %all-to-all-start.2) | async-done | bytes 1048608 | tf_op jit(solution)/shard_map/all_to_all | solution.py:310
  445.8 8.2 %fusion.60 = bf16[3840,256]{1,0:T(8,128)(2,1)} fusion(bf16[2048,256]{1,0:T(8,128)(2,1)} %bitcast.35, s32[2048]{0:T(1024)S(1)} %bitcast.722), kind=kOutput, calls=%fused_computation.89 | convolution fusion | flops 4035379200 | bytes 3022848 | tf_op jit(solution)/shard_map/dot_general | solution.py:23
  454.0 11.2 %all-to-all-done.3 = bf16[8,256,256]{2,1,0:T(8,128)(2,1)} async-done(((bf16[8,256,256]{2,1,0:T(8,128)(2,1)}), bf16[8,256,256]{2,1,0:T(8,128)(2,1)}, u32[]{:S(2)}, u32[]{:S(2)}) %all-to-all-start.3) | async-done | bytes 1048608 | tf_op jit(solution)/shard_map/all_to_all | solution.py:310
  474.0 7.2 fusion.61
  483.7 12.9 %all-to-all-done.4 = bf16[8,256,256]{2,1,0:T(8,128)(2,1)} async-done(((bf16[8,256,256]{2,1,0:T(8,128)(2,1)}), bf16[8,256,256]{2,1,0:T(8,128)(2,1)}, u32[]{:S(2)}, u32[]{:S(2)}) %all-to-all-start.4) | async-done | bytes 1048608 | tf_op jit(solution)/shard_map/all_to_all | solution.py:310
  496.6 7.4 fusion.62
  509.7 8.9 %collective-permute-done = bf16[2,480,256]{2,1,0:T(8,128)(2,1)S(1)} collective-permute-done((bf16[2,480,256]{2,1,0:T(8,128)(2,1)S(1)}, bf16[2,480,256]{2,1,0:T(8,128)(2,1)S(1)}, u32[]{:S(2)}, u32[]{:S(2)}) %collective-permute-start) | collective-permute-done | bytes 491552 | tf_op jit(solution)/shard_map/ppermute | solution.py:79
  520.2 7.5 collective-permute-done.8
  530.7 11.1 %collective-permute-done.16 = bf16[2,480,256]{2,1,0:T(8,128)(2,1)S(1)} collective-permute-done((bf16[2,480,256]{2,1,0:T(8,128)(2,1)S(1)}, bf16[2,480,256]{2,1,0:T(8,128)(2,1)S(1)}, u32[]{:S(2)}, u32[]{:S(2)}) %collective-permute-start.16) | collective-permute-done | bytes 491552 | tf_op jit(solution)/shard_map/ppermute | solution.py:79
  562.7 26.9 %collective-permute-done.6 = bf16[480,256]{1,0:T(8,128)(2,1)S(1)} collective-permute-done((bf16[480,256]{1,0:T(8,128)(2,1)S(1)}, bf16[480,256]{1,0:T(8,128)(2,1)S(1)}, u32[]{:S(2)}, u32[]{:S(2)}) %collective-permute-start.6) | collective-permute-done | bytes 245792 | tf_op jit(solution)/shard_map/ppermute | solution.py:79
  611.6 9.0 %collective-permute-done.49 = bf16[2,2,96,768]{3,2,0,1:T(8,128)(2,1)S(1)} collective-permute-done((bf16[2,2,96,768]{3,2,0,1:T(8,128)(2,1)S(1)}, bf16[2,2,96,768]{3,2,0,1:T(8,128)(2,1)S(1)}, u32[]{:S(2)}, u32[]{:S(2)}) %collective-permute-start.49) | collective-permute-done | bytes 589856 | tf_op jit(solution)/shard_map/ppermute | solution.py:79
  622.6 10.5 %collective-permute-done.37 = bf16[2,2,24,3072]{3,2,0,1:T(8,128)(2,1)S(1)} collective-permute-done((bf16[2,2,24,3072]{3,2,0,1:T(8,128)(2,1)S(1)}, bf16[2,2,24,3072]{3,2,0,1:T(8,128)(2,1)S(1)}, u32[]{:S(2)}, u32[]{:S(2)}) %collective-permute-start.37) | collective-permute-done | bytes 589856 | tf_op jit(solution)/shard_map/ppermute | solution.py:79
  639.1 23.7 %collective-permute-done.40 = bf16[2,24,3072]{2,1,0:T(8,128)(2,1)S(1)} collective-permute-done((bf16[2,24,3072]{2,1,0:T(8,128)(2,1)S(1)}, bf16[2,24,3072]{2,1,0:T(8,128)(2,1)S(1)}, u32[]{:S(2)}, u32[]{:S(2)}) %collective-permute-start.40) | collective-permute-done | bytes 294944 | tf_op jit(solution)/shard_map/ppermute | solution.py:79
  663.6 8.5 %collective-permute-done.38 = bf16[2,24,3072]{2,1,0:T(8,128)(2,1)S(1)} collective-permute-done((bf16[2,24,3072]{2,1,0:T(8,128)(2,1)S(1)}, bf16[2,24,3072]{2,1,0:T(8,128)(2,1)S(1)}, u32[]{:S(2)}, u32[]{:S(2)}) %collective-permute-start.38) | collective-permute-done | bytes 294944 | tf_op jit(solution)/shard_map/ppermute | solution.py:79
  674.4 7.7 collective-permute-done.50
  694.0 9.1 %collective-permute-done.19 = bf16[2,480,256]{2,1,0:T(8,128)(2,1)S(1)} collective-permute-done((bf16[2,480,256]{2,1,0:T(8,128)(2,1)S(1)}, bf16[2,480,256]{2,1,0:T(8,128)(2,1)S(1)}, u32[]{:S(2)}, u32[]{:S(2)}) %collective-permute-start.19) | collective-permute-done | bytes 491552 | tf_op jit(solution)/shard_map/ppermute | solution.py:79
  731.9 13.6 %collective-permute-done.47 = bf16[24,1536]{1,0:T(8,128)(2,1)S(1)} collective-permute-done((bf16[24,1536]{1,0:T(8,128)(2,1)S(1)}, bf16[24,1536]{1,0:T(8,128)(2,1)S(1)}, u32[]{:S(2)}, u32[]{:S(2)}) %collective-permute-start.47) | collective-permute-done | bytes 73760 | tf_op jit(solution)/shard_map/ppermute | solution.py:79
  (615 shorter events, 373.5 us)
Async XLA Ops:
  40.7 76.3 %all-to-all-start.1 = ((bf16[8,256,768]{2,1,0:T(8,128)(2,1)}), bf16[8,256,768]{2,1,0:T(8,128)(2,1)}, u32[]{:S(2)}, u32[]{:S(2)}) async-start(bf16[8,256,768]{2,1,0:T(8,128)(2,1)} %broadcast_select_fusion), calls=%async_computation.1 | async-start | bytes 6291456 | tf_op jit(solution)/shard_map/all_to_all | solution.py:217
  392.9 150.7 %collective-permute-start.48 = (bf16[4,384,768]{2,1,0:T(8,128)(2,1)}, bf16[4,384,768]{2,1,0:T(8,128)(2,1)}, u32[]{:S(2)}, u32[]{:S(2)}) collective-permute-start(bf16[4,384,768]{2,1,0:T(8,128)(2,1)} %dynamic-slice_bitcast_fusion.2), channel_id=1, source_target_pairs={{0,1},{1,0},{2,3},{3,2},{4,5},{5,4},{6,7},{7,6},{8,9},{9,8},{10,11... | collective-permute-start | bytes 7077896 | tf_op jit(solution)/shard_map/ppermute | solution.py:79
  394.6 153.0 %collective-permute-start.36 = (bf16[4,96,3072]{2,1,0:T(8,128)(2,1)}, bf16[4,96,3072]{2,1,0:T(8,128)(2,1)}, u32[]{:S(2)}, u32[]{:S(2)}) collective-permute-start(bf16[4,96,3072]{2,1,0:T(8,128)(2,1)} %dynamic-slice_bitcast_fusion.3), channel_id=1, source_target_pairs={{0,1},{1,0},{2,3},{3,2},{4,5},{5,4},{6,7},{7,6},{8,9},{9,8},{10,11... | collective-permute-start | bytes 7077896 | tf_op jit(solution)/shard_map/ppermute | solution.py:79
  403.4 31.1 %all-to-all-start.2 = ((bf16[8,256,256]{2,1,0:T(8,128)(2,1)}), bf16[8,256,256]{2,1,0:T(8,128)(2,1)}, u32[]{:S(2)}, u32[]{:S(2)}) async-start(bf16[8,256,256]{2,1,0:T(8,128)(2,1)} %bitcast.34), calls=%async_computation.2 | async-start | bytes 2097152 | tf_op jit(solution)/shard_map/all_to_all | solution.py:310
  434.4 30.8 %all-to-all-start.3 = ((bf16[8,256,256]{2,1,0:T(8,128)(2,1)}), bf16[8,256,256]{2,1,0:T(8,128)(2,1)}, u32[]{:S(2)}, u32[]{:S(2)}) async-start(bf16[8,256,256]{2,1,0:T(8,128)(2,1)} %bitcast.54), calls=%async_computation.3 | async-start | bytes 2097152 | tf_op jit(solution)/shard_map/all_to_all | solution.py:310
  445.4 189.8 %collective-permute-start.24 = (bf16[4,128,3072]{2,1,0:T(8,128)(2,1)}, bf16[4,128,3072]{2,1,0:T(8,128)(2,1)}, u32[]{:S(2)}, u32[]{:S(2)}) collective-permute-start(bf16[4,128,3072]{2,1,0:T(8,128)(2,1)} %dynamic-slice_bitcast_fusion.1), channel_id=1, source_target_pairs={{0,1},{1,0},{2,3},{3,2},{4,5},{5,4},{6,7},{7,6},{8,9},{9,8},{10,11... | collective-permute-start | bytes 9437192 | tf_op jit(solution)/shard_map/ppermute | solution.py:79
  465.3 31.3 %all-to-all-start.4 = ((bf16[8,256,256]{2,1,0:T(8,128)(2,1)}), bf16[8,256,256]{2,1,0:T(8,128)(2,1)}, u32[]{:S(2)}, u32[]{:S(2)}) async-start(bf16[8,256,256]{2,1,0:T(8,128)(2,1)} %bitcast.74), calls=%async_computation.4 | async-start | bytes 2097152 | tf_op jit(solution)/shard_map/all_to_all | solution.py:310
  472.5 31.8 %collective-permute-start.4 = (bf16[2,480,256]{2,1,0:T(8,128)(2,1)}, bf16[2,480,256]{2,1,0:T(8,128)(2,1)}, u32[]{:S(2)}, u32[]{:S(2)}) collective-permute-start(bf16[2,480,256]{2,1,0:T(8,128)(2,1)} %dynamic-slice_bitcast_fusion.9), channel_id=1, source_target_pairs={{0,16},{8,24},{16,0},{24,8},{1,17},{9,25},{17,1},{25,9},{2,18},{10... | collective-permute-start | bytes 1474568 | tf_op jit(solution)/shard_map/ppermute | solution.py:79
  483.2 23.9 %collective-permute-start.12 = (bf16[2,480,256]{2,1,0:T(8,128)(2,1)}, bf16[2,480,256]{2,1,0:T(8,128)(2,1)}, u32[]{:S(2)}, u32[]{:S(2)}) collective-permute-start(bf16[2,480,256]{2,1,0:T(8,128)(2,1)} %dynamic-slice_bitcast_fusion.7), channel_id=1, source_target_pairs={{0,16},{8,24},{16,0},{24,8},{1,17},{9,25},{17,1},{25,9},{2,18},{10... | collective-permute-start | bytes 1474568 | tf_op jit(solution)/shard_map/ppermute | solution.py:79
  504.4 14.2 %collective-permute-start = (bf16[2,480,256]{2,1,0:T(8,128)(2,1)S(1)}, bf16[2,480,256]{2,1,0:T(8,128)(2,1)S(1)}, u32[]{:S(2)}, u32[]{:S(2)}) collective-permute-start(bf16[2,480,256]{2,1,0:T(8,128)(2,1)S(1)} %dynamic-slice_bitcast_fusion.10), channel_id=1, source_target_pairs={{0,8},{8,0},{16,24},{24,16},{1,9},{9,1},{17,25},{25,17},{2,10},{10... | collective-permute-start | bytes 1474568 | tf_op jit(solution)/shard_map/ppermute | solution.py:79
  507.1 20.6 %collective-permute-start.8 = (bf16[2,480,256]{2,1,0:T(8,128)(2,1)S(1)}, bf16[2,480,256]{2,1,0:T(8,128)(2,1)S(1)}, u32[]{:S(2)}, u32[]{:S(2)}) collective-permute-start(bf16[2,480,256]{2,1,0:T(8,128)(2,1)S(1)} %dynamic-slice_bitcast_fusion.8), channel_id=1, source_target_pairs={{0,8},{8,0},{16,24},{24,16},{1,9},{9,1},{17,25},{25,17},{2,10},{10... | collective-permute-start | bytes 1474568 | tf_op jit(solution)/shard_map/ppermute | solution.py:79
  529.4 22.0 %collective-permute-start.5 = (bf16[480,256]{1,0:T(8,128)(2,1)S(1)}, bf16[480,256]{1,0:T(8,128)(2,1)S(1)}, u32[]{:S(2)}, u32[]{:S(2)}) collective-permute-start(bf16[480,256]{1,0:T(8,128)(2,1)S(1)} %dynamic-slice_bitcast_fusion.21), channel_id=1, source_target_pairs={{0,8},{8,0},{16,24},{24,16},{1,9},{9,1},{17,25},{25,17},{2,10},{10... | collective-permute-start | bytes 737288 | tf_op jit(solution)/shard_map/ppermute | solution.py:79
  553.8 56.0 %collective-permute-start.51 = (bf16[2,2,96,768]{3,2,0,1:T(8,128)(2,1)S(1)}, bf16[2,2,96,768]{3,2,0,1:T(8,128)(2,1)S(1)}, u32[]{:S(2)}, u32[]{:S(2)}) collective-permute-start(bf16[2,2,96,768]{3,2,0,1:T(8,128)(2,1)S(1)} %bitcast.717), channel_id=1, source_target_pairs={{0,16},{8,24},{16,0},{24,8},{1,17},{9,25},{17,1},{25,9},{2,18},{10... | collective-permute-start | bytes 1769480 | tf_op jit(solution)/shard_map/ppermute | solution.py:79
  556.6 53.6 %collective-permute-start.39 = (bf16[2,2,24,3072]{3,2,0,1:T(8,128)(2,1)S(1)}, bf16[2,2,24,3072]{3,2,0,1:T(8,128)(2,1)S(1)}, u32[]{:S(2)}, u32[]{:S(2)}) collective-permute-start(bf16[2,2,24,3072]{3,2,0,1:T(8,128)(2,1)S(1)} %bitcast.716), channel_id=1, source_target_pairs={{0,16},{8,24},{16,0},{24,8},{1,17},{9,25},{17,1},{25,9},{2,18},{10... | collective-permute-start | bytes 1769480 | tf_op jit(solution)/shard_map/ppermute | solution.py:79
  557.8 31.8 %collective-permute-start.6 = (bf16[480,256]{1,0:T(8,128)(2,1)S(1)}, bf16[480,256]{1,0:T(8,128)(2,1)S(1)}, u32[]{:S(2)}, u32[]{:S(2)}) collective-permute-start(bf16[480,256]{1,0:T(8,128)(2,1)S(1)} %fusion.133), channel_id=1, source_target_pairs={{0,16},{8,24},{16,0},{24,8},{1,17},{9,25},{17,1},{25,9},{2,18},{10... | collective-permute-start | bytes 737288 | tf_op jit(solution)/shard_map/ppermute | solution.py:79
  561.8 28.6 %collective-permute-start.2 = (bf16[480,256]{1,0:T(8,128)(2,1)S(1)}, bf16[480,256]{1,0:T(8,128)(2,1)S(1)}, u32[]{:S(2)}, u32[]{:S(2)}) collective-permute-start(bf16[480,256]{1,0:T(8,128)(2,1)S(1)} %fusion.134), channel_id=1, source_target_pairs={{0,8},{8,0},{16,24},{24,16},{1,9},{9,1},{17,25},{25,17},{2,10},{10... | collective-permute-start | bytes 737288 | tf_op jit(solution)/shard_map/ppermute | solution.py:79
  604.1 16.5 %collective-permute-start.49 = (bf16[2,2,96,768]{3,2,0,1:T(8,128)(2,1)S(1)}, bf16[2,2,96,768]{3,2,0,1:T(8,128)(2,1)S(1)}, u32[]{:S(2)}, u32[]{:S(2)}) collective-permute-start(bf16[2,2,96,768]{3,2,0,1:T(8,128)(2,1)S(1)} %bitcast.715), channel_id=1, source_target_pairs={{0,8},{8,0},{16,24},{24,16},{1,9},{9,1},{17,25},{25,17},{2,10},{10... | collective-permute-start | bytes 1769480 | tf_op jit(solution)/shard_map/ppermute | solution.py:79
  607.9 25.3 %collective-permute-start.37 = (bf16[2,2,24,3072]{3,2,0,1:T(8,128)(2,1)S(1)}, bf16[2,2,24,3072]{3,2,0,1:T(8,128)(2,1)S(1)}, u32[]{:S(2)}, u32[]{:S(2)}) collective-permute-start(bf16[2,2,24,3072]{3,2,0,1:T(8,128)(2,1)S(1)} %bitcast.714), channel_id=1, source_target_pairs={{0,8},{8,0},{16,24},{24,16},{1,9},{9,1},{17,25},{25,17},{2,10},{10... | collective-permute-start | bytes 1769480 | tf_op jit(solution)/shard_map/ppermute | solution.py:79
  609.8 76.1 %collective-permute-start.7 = (bf16[2,480,256]{2,1,0:T(8,128)(2,1)S(1)}, bf16[2,480,256]{2,1,0:T(8,128)(2,1)S(1)}, u32[]{:S(2)}, u32[]{:S(2)}) collective-permute-start(bf16[2,480,256]{2,1,0:T(8,128)(2,1)S(1)} %pad_maximum_fusion.5), channel_id=1, source_target_pairs={{0,8},{8,0},{16,24},{24,16},{1,9},{9,1},{17,25},{25,17},{2,10},{10... | collective-permute-start | bytes 1474568 | tf_op jit(solution)/shard_map/ppermute | solution.py:79
  610.2 73.6 %collective-permute-start.3 = (bf16[2,480,256]{2,1,0:T(8,128)(2,1)S(1)}, bf16[2,480,256]{2,1,0:T(8,128)(2,1)S(1)}, u32[]{:S(2)}, u32[]{:S(2)}) collective-permute-start(bf16[2,480,256]{2,1,0:T(8,128)(2,1)S(1)} %pad_maximum_fusion.4), channel_id=1, source_target_pairs={{0,16},{8,24},{16,0},{24,8},{1,17},{9,25},{17,1},{25,9},{2,18},{10... | collective-permute-start | bytes 1474568 | tf_op jit(solution)/shard_map/ppermute | solution.py:79
  620.5 72.6 %collective-permute-start.15 = (bf16[2,480,256]{2,1,0:T(8,128)(2,1)S(1)}, bf16[2,480,256]{2,1,0:T(8,128)(2,1)S(1)}, u32[]{:S(2)}, u32[]{:S(2)}) collective-permute-start(bf16[2,480,256]{2,1,0:T(8,128)(2,1)S(1)} %pad_maximum_fusion.7), channel_id=1, source_target_pairs={{0,8},{8,0},{16,24},{24,16},{1,9},{9,1},{17,25},{25,17},{2,10},{10... | collective-permute-start | bytes 1474568 | tf_op jit(solution)/shard_map/ppermute | solution.py:79
  633.2 40.1 %collective-permute-start.52 = (bf16[2,96,768]{2,1,0:T(8,128)(2,1)S(1)}, bf16[2,96,768]{2,1,0:T(8,128)(2,1)S(1)}, u32[]{:S(2)}, u32[]{:S(2)}) collective-permute-start(bf16[2,96,768]{2,1,0:T(8,128)(2,1)S(1)} %dynamic-slice_bitcast_fusion.13), channel_id=1, source_target_pairs={{0,8},{8,0},{16,24},{24,16},{1,9},{9,1},{17,25},{25,17},{2,10},{10... | collective-permute-start | bytes 884744 | tf_op jit(solution)/shard_map/ppermute | solution.py:79
  635.2 27.5 %collective-permute-start.40 = (bf16[2,24,3072]{2,1,0:T(8,128)(2,1)S(1)}, bf16[2,24,3072]{2,1,0:T(8,128)(2,1)S(1)}, u32[]{:S(2)}, u32[]{:S(2)}) collective-permute-start(bf16[2,24,3072]{2,1,0:T(8,128)(2,1)S(1)} %dynamic-slice_bitcast_fusion.15), channel_id=1, source_target_pairs={{0,8},{8,0},{16,24},{24,16},{1,9},{9,1},{17,25},{25,17},{2,10},{10... | collective-permute-start | bytes 884744 | tf_op jit(solution)/shard_map/ppermute | solution.py:79
  673.3 19.3 %collective-permute-start.11 = (bf16[2,480,256]{2,1,0:T(8,128)(2,1)S(1)}, bf16[2,480,256]{2,1,0:T(8,128)(2,1)S(1)}, u32[]{:S(2)}, u32[]{:S(2)}) collective-permute-start(bf16[2,480,256]{2,1,0:T(8,128)(2,1)S(1)} %pad_maximum_fusion.6), channel_id=1, source_target_pairs={{0,16},{8,24},{16,0},{24,8},{1,17},{9,25},{17,1},{25,9},{2,18},{10... | collective-permute-start | bytes 1474568 | tf_op jit(solution)/shard_map/ppermute | solution.py:79
  682.0 21.7 %collective-permute-start.23 = (bf16[2,480,256]{2,1,0:T(8,128)(2,1)S(1)}, bf16[2,480,256]{2,1,0:T(8,128)(2,1)S(1)}, u32[]{:S(2)}, u32[]{:S(2)}) collective-permute-start(bf16[2,480,256]{2,1,0:T(8,128)(2,1)S(1)} %pad_maximum_fusion.9), channel_id=1, source_target_pairs={{0,8},{8,0},{16,24},{24,16},{1,9},{9,1},{17,25},{25,17},{2,10},{10... | collective-permute-start | bytes 1474568 | tf_op jit(solution)/shard_map/ppermute | solution.py:79
  683.8 19.3 %collective-permute-start.19 = (bf16[2,480,256]{2,1,0:T(8,128)(2,1)S(1)}, bf16[2,480,256]{2,1,0:T(8,128)(2,1)S(1)}, u32[]{:S(2)}, u32[]{:S(2)}) collective-permute-start(bf16[2,480,256]{2,1,0:T(8,128)(2,1)S(1)} %pad_maximum_fusion.8), channel_id=1, source_target_pairs={{0,16},{8,24},{16,0},{24,8},{1,17},{9,25},{17,1},{25,9},{2,18},{10... | collective-permute-start | bytes 1474568 | tf_op jit(solution)/shard_map/ppermute | solution.py:79
  685.9 60.9 %collective-permute-start.27 = (bf16[2,2,32,3072]{3,2,1,0:T(8,128)(2,1)S(1)}, bf16[2,2,32,3072]{3,2,1,0:T(8,128)(2,1)S(1)}, u32[]{:S(2)}, u32[]{:S(2)}) collective-permute-start(bf16[2,2,32,3072]{3,2,1,0:T(8,128)(2,1)S(1)} %dynamic-slice_bitcast_fusion.4), channel_id=1, source_target_pairs={{0,16},{8,24},{16,0},{24,8},{1,17},{9,25},{17,1},{25,9},{2,18},{10... | collective-permute-start | bytes 2359304 | tf_op jit(solution)/shard_map/ppermute | solution.py:79
  692.6 23.4 %collective-permute-start.53 = (bf16[96,768]{1,0:T(8,128)(2,1)S(1)}, bf16[96,768]{1,0:T(8,128)(2,1)S(1)}, u32[]{:S(2)}, u32[]{:S(2)}) collective-permute-start(bf16[96,768]{1,0:T(8,128)(2,1)S(1)} %get-tuple-element.306), channel_id=1, source_target_pairs={{0,2},{1,3},{2,4},{3,5},{4,6},{5,7},{6,0},{7,1},{8,10},{9,11},{10,... | collective-permute-start | bytes 442376 | tf_op jit(solution)/shard_map/ppermute | solution.py:133
  727.7 19.4 %collective-permute-start.25 = (bf16[2,2,32,3072]{3,2,0,1:T(8,128)(2,1)S(1)}, bf16[2,2,32,3072]{3,2,0,1:T(8,128)(2,1)S(1)}, u32[]{:S(2)}, u32[]{:S(2)}) collective-permute-start(bf16[2,2,32,3072]{3,2,0,1:T(8,128)(2,1)S(1)} %bitcast.713), channel_id=1, source_target_pairs={{0,8},{8,0},{16,24},{24,16},{1,9},{9,1},{17,25},{25,17},{2,10},{10... | collective-permute-start | bytes 2359304 | tf_op jit(solution)/shard_map/ppermute | solution.py:79
  727.8 32.7 %collective-permute-start.57 = (bf16[96,384]{1,0:T(8,128)(2,1)S(1)}, bf16[96,384]{1,0:T(8,128)(2,1)S(1)}, u32[]{:S(2)}, u32[]{:S(2)}) collective-permute-start(bf16[96,384]{1,0:T(8,128)(2,1)S(1)} %slice.331), channel_id=1, source_target_pairs={{0,16},{8,24},{16,0},{24,8},{1,17},{9,25},{17,1},{25,9},{2,18},{10... | collective-permute-start | bytes 221192 | tf_op jit(solution)/shard_map/ppermute | solution.py:79
  729.7 30.8 %collective-permute-start.59 = (bf16[96,384]{1,0:T(8,128)(2,1)S(1)}, bf16[96,384]{1,0:T(8,128)(2,1)S(1)}, u32[]{:S(2)}, u32[]{:S(2)}) collective-permute-start(bf16[96,384]{1,0:T(8,128)(2,1)S(1)} %slice.332), channel_id=1, source_target_pairs={{0,8},{8,0},{16,24},{24,16},{1,9},{9,1},{17,25},{25,17},{2,10},{10... | collective-permute-start | bytes 221192 | tf_op jit(solution)/shard_map/ppermute | solution.py:79
  730.9 14.6 %collective-permute-start.47 = (bf16[24,1536]{1,0:T(8,128)(2,1)S(1)}, bf16[24,1536]{1,0:T(8,128)(2,1)S(1)}, u32[]{:S(2)}, u32[]{:S(2)}) collective-permute-start(bf16[24,1536]{1,0:T(8,128)(2,1)S(1)} %slice.327), channel_id=1, source_target_pairs={{0,8},{8,0},{16,24},{24,16},{1,9},{9,1},{17,25},{25,17},{2,10},{10... | collective-permute-start | bytes 221192 | tf_op jit(solution)/shard_map/ppermute | solution.py:79
  (143 other events, 1190.7 us)

commit v2 on v1

--- a/solution.py
+++ b/solution.py
@@ -3,6 +3,8 @@
 import jax
 import jax.numpy as jnp
 from jax import lax
+from jax.experimental import pallas as pl
+from jax.experimental.pallas import tpu as pltpu
 from jax.sharding import PartitionSpec as P
 
 HEADS = 12
@@ -166,6 +168,414 @@
     b = reorder(last, last_x[0], last_y, last_x[1])
     parts = [p for group in (a, b) for line in group for p in line]
     return jnp.concatenate(parts, 0).astype(jnp.float32)
+
+
+MESH = pl.DeviceIdType.MESH
+BF = jnp.bfloat16
+F32 = jnp.float32
+
+
+def flipped(index, bits):
+    out = 0
+    for place in range(3):
+        bit = lax.rem(lax.div(index, 1 << place), 2)
+        out = out + (1 << place) * (1 - bit if (bits >> place) & 1 else bit)
+    return out
+
+
+ORDER = (6, 7, 4, 5, 2, 3, 1)
+
+
+def tail_kernel(
+    demb, slot, asked, small, normed, mixed, gfirst, dq, dk, dv,
+    word, packed,
+    og, inc, hits, dense, r1a, r1b, r2a, r2b,
+    ops, turned, wbuf, wcore, w1a, w1b, w2a, w2b, wz, wown,
+    load_sem, z_send, z_recv, d_send, d_recv, w_send, w_recv, own_sem,
+):
+    owners, cap = og.shape[1], og.shape[2]
+    chunks, cols = og.shape[0], og.shape[3]
+    tokens = demb.shape[0]
+    part = dense.shape[4]
+    me = lax.axis_index("vocab")
+    spot = lax.axis_index("dp")
+    core, place = lax.rem(me, 2), lax.div(me, 2)
+    xb, yb = lax.rem(spot, 2), lax.div(spot, 2)
+    across_x = {"dp": spot + 1 - 2 * xb}
+    across_y = {"dp": spot + 2 - 4 * yb}
+
+    loads = [
+        pltpu.make_async_copy(ref, ops.at[i], load_sem.at[i])
+        for i, ref in enumerate((normed, dq, dk, dv, mixed, gfirst))
+    ]
+    for load in loads:
+        load.start()
+    barrier = pltpu.get_barrier_semaphore()
+    for k in ORDER:
+        pl.semaphore_signal(barrier, inc=1, device_id={"vocab": flipped(me, k)}, device_id_type=MESH)
+    for peer in (across_x, across_y):
+        pl.semaphore_signal(barrier, inc=1, device_id=peer, device_id_type=MESH)
+    pl.semaphore_wait(barrier, len(ORDER) + 2)
+
+    def remote(src, dst, send, recv, peer):
+        return pltpu.make_async_remote_copy(
+            src_ref=src, dst_ref=dst, send_sem=send, recv_sem=recv, device_id=peer, device_id_type=MESH
+        )
+
+    def row_copy(c, k):
+        peer = flipped(me, k)
+        return remote(
+            og.at[c, peer], inc.at[c, me], z_send.at[c, k], z_recv.at[c, k], {"vocab": peer}
+        )
+
+    def slots_of(peer):
+        wanted = lax.broadcasted_iota(jnp.int32, (cap, tokens), 0) + peer * cap
+        hot = jnp.where(wanted == slot[...], 1.0, 0.0).astype(BF)
+        return jnp.dot(hot, demb[...], preferred_element_type=F32).astype(BF)
+
+    for k in ORDER:
+        peer = flipped(me, k)
+        rows = slots_of(peer)
+        for c in range(chunks):
+            og[c, peer] = rows[:, c * cols : (c + 1) * cols]
+        row_copy(0, k).start()
+    rows = slots_of(me)
+    for c in range(chunks):
+        inc[c, me] = rows[:, c * cols : (c + 1) * cols]
+
+    width = demb.shape[1]
+    per = width // owners
+    block = 256
+
+    def turn(which):
+        for i in range(tokens // block):
+            for j in range(width // block):
+                turned[pl.ds(j * block, block), pl.ds(i * block, block)] = ops[
+                    which, pl.ds(i * block, block), pl.ds(j * block, block)
+                ].T
+
+    def weight(which, at):
+        def one(n, carry):
+            there = pl.multiple_of(n * block, block)
+            out = jnp.dot(turned[...], ops[which, :, pl.ds(there, block)], preferred_element_type=F32).astype(BF)
+            there = pl.multiple_of(at * width + n * block, block)
+            for v in range(owners):
+                wbuf[v // 2, v % 2, pl.ds(0, per), pl.ds(there, block)] = out[v * per : (v + 1) * per]
+            return carry
+
+        lax.fori_loop(0, width // block, one, 0)
+
+    loads[0].wait()
+    turn(0)
+    for i in range(3):
+        loads[1 + i].wait()
+        weight(1 + i, i)
+    loads[4].wait()
+    turn(4)
+    loads[5].wait()
+    weight(5, 3)
+    half = tokens // 2
+    lines = half // owners // 4
+    for v in range(owners):
+        for j in range(4):
+            at = v * (half // owners) + j * lines
+            total = demb[pl.ds(at, lines), :].astype(F32) + demb[pl.ds(half + at, lines), :].astype(F32)
+            wbuf[v // 2, v % 2, pl.ds(per, lines), pl.ds(j * width, width)] = total.astype(BF)
+        wbuf[v // 2, v % 2, pl.ds(per + lines, 16), :] = jnp.zeros((16, 4 * width), BF)
+        wbuf[v // 2, v % 2, pl.ds(per + lines, 16), pl.ds(0, 128)] = jnp.pad(
+            small[:, v * per : (v + 1) * per], ((0, 0), (0, 128 - per))
+        ).astype(BF)
+    partner = {"vocab": flipped(me, 1)}
+    core_copy = remote(wbuf.at[:, 1 - core], wcore, w_send.at[0], w_recv.at[0], partner)
+    core_copy.start()
+
+    tile = 240
+    rows_local = 8 * part
+
+    def match(t, carry):
+        at = pl.multiple_of(t * tile, tile)
+        row = lax.broadcasted_iota(jnp.int32, (tile, owners * cap), 0) + at
+        hits[pl.ds(at, tile), :] = jnp.where(row == asked[...], 1.0, 0.0).astype(BF)
+        return carry
+
+    lax.fori_loop(0, rows_local // tile, match, 0)
+
+    quarter = wown.shape[0]
+    def w_view(z, x, y):
+        return wbuf.at[z, core, pl.ds(pl.multiple_of((2 * x + y) * quarter, quarter), quarter), :]
+
+    def w_half(z, x):
+        return wbuf.at[z, core, pl.ds(pl.multiple_of(2 * x * quarter, quarter), 2 * quarter), :]
+
+    def core_sum(i, carry):
+        z = lax.div(i, 4)
+        at = pl.multiple_of(lax.rem(i, 4) * quarter, quarter)
+        mine = wbuf[z, core, pl.ds(at, quarter), :].astype(F32)
+        wbuf[z, core, pl.ds(at, quarter), :] = (mine + wcore[z, pl.ds(at, quarter), :].astype(F32)).astype(BF)
+        return carry
+
+    def first_weights():
+        copies = []
+        for z in range(2):
+            copies.append(remote(w_half(z, 1 - xb), w1a.at[z], w_send.at[1 + z], w_recv.at[1 + z], across_x))
+            for x in range(2):
+                at = 2 * z + x
+                copies.append(
+                    remote(w_view(2 + z, x, 1 - yb), w1b.at[z, x], w_send.at[3 + at], w_recv.at[3 + at], across_y)
+                )
+        return copies
+
+    def add_to(z, x, y, value):
+        view = w_view(z, x, y)
+        view[...] = (view[...].astype(F32) + value.astype(F32)).astype(BF)
+
+    def second_weights():
+        copies = []
+        for z in range(2):
+            copies.append(remote(w_view(z, xb, 1 - yb), w2a.at[z], w_send.at[7 + z], w_recv.at[7 + z], across_y))
+            copies.append(remote(w_view(2 + z, 1 - xb, yb), w2b.at[z], w_send.at[9 + z], w_recv.at[9 + z], across_x))
+        return copies
+
+    def place_copy(k):
+        to = flipped(place, k)
+        return remote(
+            w_view(to, xb, yb), wz.at[k - 1], w_send.at[10 + k], w_recv.at[10 + k], {"vocab": 2 * to + core}
+        )
+
+    def third_weights():
+        return [place_copy(k) for k in (3, 2, 1)]
+
+    def own_weights():
+        return pltpu.make_async_copy(wown, packed.at[xb, yb], own_sem.at[0])
+
+    def fourth_weights():
+        return [
+            remote(wown, packed.at[xb, yb], w_send.at[14], w_recv.at[14], across_x),
+            remote(wown, packed.at[xb, yb], w_send.at[15], w_recv.at[15], across_y),
+        ]
+
+    wide = 2 * width
+
+    def fifth_weights():
+        left, right = pl.ds(0, wide), pl.ds(wide, wide)
+        return [
+            remote(
+                packed.at[1 - xb, yb, :, left], packed.at[1 - xb, yb, :, left], w_send.at[16], w_recv.at[16], across_y
+            ),
+            remote(
+                packed.at[xb, 1 - yb, :, right], packed.at[xb, 1 - yb, :, right], w_send.at[17], w_recv.at[17], across_x
+            ),
+        ]
+
+    def first_rows(c):
+        return [
+            remote(dense.at[c, 0, 1 - xb], r1a.at[c], d_send.at[c, 0], d_recv.at[c, 0], across_x),
+            remote(dense.at[c, 1, :, 1 - yb], r1b.at[c], d_send.at[c, 1], d_recv.at[c, 1], across_y),
+        ]
+
+    def second_rows(c):
+        return [
+            remote(dense.at[c, 0, xb, 1 - yb], r2a.at[c], d_send.at[c, 2], d_recv.at[c, 2], across_y),
+            remote(dense.at[c, 1, 1 - xb, yb], r2b.at[c], d_send.at[c, 3], d_recv.at[c, 3], across_x),
+        ]
+
+    def spread(c):
+        return pl.ds(c * cols, cols)
+
+    def own_rows(c):
+        return [
+            pltpu.make_async_copy(dense.at[c, h, xb, yb], word.at[h, xb, yb, :, spread(c)], own_sem.at[1 + 2 * c + h])
+            for h in range(2)
+        ]
+
+    def third_rows(c):
+        return [
+            remote(dense.at[c, 0, xb, yb], word.at[0, xb, yb, :, spread(c)], d_send.at[c, 4], d_recv.at[c, 4], across_x),
+            remote(dense.at[c, 1, xb, yb], word.at[1, xb, yb, :, spread(c)], d_send.at[c, 5], d_recv.at[c, 5], across_y),
+        ]
+
+    def fourth_rows(c):
+        return [
+            remote(
+                word.at[0, :, yb, :, spread(c)], word.at[0, :, yb, :, spread(c)], d_send.at[c, 6], d_recv.at[c, 6], across_y
+            ),
+            remote(
+                word.at[1, xb, :, :, spread(c)], word.at[1, xb, :, :, spread(c)], d_send.at[c, 7], d_recv.at[c, 7], across_x
+            ),
+        ]
+
+    def start(copies):
+        for copy in copies:
+            copy.start()
+
+    def arrived(copies):
+        for copy in copies:
+            copy.wait_recv()
+
+    def gone(copies):
+        for copy in copies:
+            copy.wait_send()
+
+    def arrive_slots(c):
+        for k in ORDER:
+            row_copy(c, k).wait_recv()
+
+    def sum_slots(c):
+        def one(t, carry):
+            h, x, y = lax.div(t, 4), lax.rem(lax.div(t, 2), 2), lax.rem(t, 2)
+            at = pl.multiple_of(t * part, part)
+            total = jnp.zeros((part, cols), F32)
+            for p in range(owners):
+                total = total + jnp.dot(
+                    hits[pl.ds(at, part), pl.ds(p * cap, cap)], inc[c, p], preferred_element_type=F32
+                )
+            dense[c, h, x, y] = total.astype(BF)
+            return carry
+
+        lax.fori_loop(0, 8, one, 0)
+
+    def add_rows(c, h, x, y, value):
+        dense[c, h, x, y] = (dense[c, h, x, y].astype(F32) + value.astype(F32)).astype(BF)
+
+    def add_first(c):
+        arrived(first_rows(c))
+        for i in range(2):
+            add_rows(c, 0, xb, i, r1a[c, i])
+            add_rows(c, 1, i, yb, r1b[c, i])
+        start(second_rows(c))
+
+    def add_second(c):
+        arrived(second_rows(c))
+        add_rows(c, 0, xb, yb, r2a[c])
+        add_rows(c, 1, xb, yb, r2b[c])
+        start(third_rows(c))
+        start(own_rows(c))
+
+    def pass_on(c):
+        for copy in own_rows(c):
+            copy.wait()
+        arrived(third_rows(c))
+        start(fourth_rows(c))
+
+    core_copy.wait_recv()
+    core_copy.wait_send()
+    lax.fori_loop(0, 16, core_sum, 0)
+    start(first_weights())
+
+    arrive_slots(0)
+    for k in ORDER:
+        row_copy(1, k).start()
+    sum_slots(0)
+    start(first_rows(0))
+
+    arrived(first_weights())
+    for z in range(2):
+        for i in range(2):
+            add_to(z, xb, i, w1a[z, pl.ds(i * quarter, quarter), :])
+            add_to(2 + z, i, yb, w1b[z, i])
+    start(second_weights())
+
+    add_first(0)
+    arrive_slots(1)
+    for k in ORDER:
+        row_copy(2, k).start()
+    sum_slots(1)
+    start(first_rows(1))
+    add_second(0)
+
+    arrived(second_weights())
+    for z in range(2):
+        add_to(z, xb, yb, w2a[z])
+        add_to(2 + z, xb, yb, w2b[z])
+    start(third_weights())
+
+    pass_on(0)
+    add_first(1)
+    arrive_slots(2)
+    sum_slots(2)
+    start(first_rows(2))
+    add_second(1)
+
+    arrived(third_weights())
+    mine = w_view(place, xb, yb)[...].astype(F32)
+    for k in range(3):
+        mine = mine + wz[k].astype(F32)
+    wown[...] = mine.astype(BF)
+    start(fourth_weights())
+    own_weights().start()
+
+    add_first(2)
+    pass_on(1)
+    own_weights().wait()
+    arrived(fourth_weights())
+    start(fifth_weights())
+    add_second(2)
+    pass_on(2)
+
+    for c in range(chunks):
+        arrived(fourth_rows(c))
+    arrived(fifth_weights())
+    for c in range(chunks):
+        for k in ORDER:
+            row_copy(c, k).wait_send()
+        for step in (first_rows, second_rows, third_rows, fourth_rows):
+            gone(step(c))
+    for step in (first_weights, second_weights, third_weights, fourth_weights, fifth_weights):
+        gone(step())
+
+
+def tail(demb, slot, asked, small, normed, mixed, gfirst, dq, dk, dv, rows_local, owners):
+    tokens, width = demb.shape
+    cap = asked.size // owners
+    chunks = 3
+    cols = width // chunks
+    part = rows_local // 8
+    lines = 128
+    wide = 4 * width
+    vmem = pl.BlockSpec(memory_space=pltpu.VMEM)
+    hbm = pl.BlockSpec(memory_space=pl.ANY)
+    word, packed = pl.pallas_call(
+        tail_kernel,
+        out_shape=(
+            jax.ShapeDtypeStruct((2, 2, 2, part, width), BF),
+            jax.ShapeDtypeStruct((2, 2, lines // 4, wide), BF),
+        ),
+        in_specs=[vmem] * 4 + [hbm] * 6,
+        out_specs=(hbm, hbm),
+        scratch_shapes=[
+            pltpu.VMEM((chunks, owners, cap, cols), BF),
+            pltpu.VMEM((chunks, owners, cap, cols), BF),
+            pltpu.VMEM((rows_local, owners * cap), BF),
+            pltpu.VMEM((chunks, 2, 2, 2, part, cols), BF),
+            pltpu.VMEM((chunks, 2, part, cols), BF),
+            pltpu.VMEM((chunks, 2, part, cols), BF),
+            pltpu.VMEM((chunks, part, cols), BF),
+            pltpu.VMEM((chunks, part, cols), BF),
+            pltpu.VMEM((6, tokens, width), BF),
+            pltpu.VMEM((width, tokens), BF),
+            pltpu.VMEM((4, 2, lines, wide), BF),
+            pltpu.VMEM((4, lines, wide), BF),
+            pltpu.VMEM((2, lines // 2, wide), BF),
+            pltpu.VMEM((2, 2, lines // 4, wide), BF),
+            pltpu.VMEM((2, lines // 4, wide), BF),
+            pltpu.VMEM((2, lines // 4, wide), BF),
+            pltpu.VMEM((3, lines // 4, wide), BF),
+            pltpu.VMEM((lines // 4, wide), BF),
+            pltpu.SemaphoreType.DMA((6,)),
+            pltpu.SemaphoreType.DMA((chunks, owners)),
+            pltpu.SemaphoreType.DMA((chunks, owners)),
+            pltpu.SemaphoreType.DMA((chunks, 8)),
+            pltpu.SemaphoreType.DMA((chunks, 8)),
+            pltpu.SemaphoreType.DMA((18,)),
+            pltpu.SemaphoreType.DMA((18,)),
+            pltpu.SemaphoreType.DMA((7,)),
+        ],
+        compiler_params=pltpu.CompilerParams(
+            collective_id=1, has_side_effects=True, vmem_limit_bytes=62 * 1024 * 1024
+        ),
+        name="tail",
+    )(demb, slot.reshape(1, tokens), asked.reshape(1, owners * cap), small, normed, mixed, gfirst, dq, dk, dv)
+    return word.reshape(rows_local, width), packed.reshape(lines, wide)
 
 
 def local(
@@ -299,24 +709,6 @@
     per = width // owners
     grad_down_all = sum_over_all(grad_down.astype(bf))
     grad_up_all = sum_over_all(grad_up.astype(bf))
-    places = slot[None, :] == jnp.arange(owners * capacity)[:, None]
-    outgoing = matmul(
-        places.astype(bf), embedding_output_gradient.reshape(tokens, width).astype(bf)
-    ).astype(bf)
-    hits = (jnp.arange(rows_local)[:, None] == asked.reshape(-1)[None, :]).astype(bf)
-    pieces = []
-    step = 256
-    for start in range(0, width, step):
-        incoming = lax.all_to_all(
-            outgoing[:, start : start + step].reshape(owners, capacity, step),
-            "vocab",
-            split_axis=0,
-            concat_axis=0,
-            tiled=True,
-        )
-        dense = matmul(hits, incoming.reshape(owners * capacity, step)).astype(bf)
-        pieces.append(sum_over_dp(dense))
-    grad_word = jnp.concatenate(pieces, 1)
     small = jnp.stack(
         [
             grad_query_bias,
@@ -333,31 +725,76 @@
             token_type_gradient[1],
         ]
     )
-    small = small.reshape(12, owners, per).transpose(1, 0, 2).reshape(owners, 12 * per)
-    small = jnp.concatenate([small, grad_up_bias.reshape(owners, 4 * per)], 1)
-    wide = 4 * width
-    lines = (seq_len // owners) * width // wide
-    rest = per // 3 - lines
-    small_lines = jnp.pad(small, ((0, 0), (0, rest * wide - 16 * per))).reshape(owners, rest, wide)
-    mixed_grads = jnp.concatenate(
-        [grad_query_weight, grad_key_weight, grad_value_weight, grad_out_weight], 1
-    ).astype(bf)
-    packed = jnp.concatenate(
-        [
-            mixed_grads.reshape(owners, per, wide),
-            grad_pos.astype(bf).reshape(owners, lines, wide),
-            small_lines.astype(bf),
-        ],
-        1,
-    )
-    packed = sum_over_all(packed.reshape(-1, wide))
-    weights = packed[:per]
-    grad_query_weight = weights[:, :width]
-    grad_key_weight = weights[:, width : 2 * width]
-    grad_value_weight = weights[:, 2 * width : 3 * width]
-    grad_out_weight = weights[:, 3 * width :]
-    grad_pos = packed[per : per + lines].reshape(seq_len // owners, width)
-    small = packed[per + lines :].reshape(-1)[: 16 * per].reshape(16, per)
+    if owners == 8 and lax.axis_size("dp") == 4:
+        ups = grad_up_bias.reshape(owners, 4, per).transpose(1, 0, 2).reshape(4, width)
+        word_low, packed = tail(
+            embedding_output_gradient.reshape(tokens, width).astype(bf),
+            slot,
+            asked,
+            jnp.concatenate([small, ups], 0),
+            normed_low,
+            mixed_low,
+            grad_first_low,
+            grad_query_low,
+            grad_keys_low,
+            grad_values_low,
+            rows_local,
+            owners,
+        )
+        grad_word = word_low.astype(jnp.float32)
+        packed = packed.astype(jnp.float32)
+        grad_query_weight, grad_key_weight, grad_value_weight, grad_out_weight = [
+            packed[:per, i * width : (i + 1) * width] for i in range(4)
+        ]
+        lines = seq_len // owners // 4
+        grad_pos = (
+            packed[per : per + lines].reshape(lines, 4, width).transpose(1, 0, 2).reshape(4 * lines, width)
+        )
+        small = packed[per + lines :, :per]
+    else:
+        places = slot[None, :] == jnp.arange(owners * capacity)[:, None]
+        outgoing = matmul(
+            places.astype(bf), embedding_output_gradient.reshape(tokens, width).astype(bf)
+        ).astype(bf)
+        hits = (jnp.arange(rows_local)[:, None] == asked.reshape(-1)[None, :]).astype(bf)
+        pieces = []
+        step = 256
+        for start in range(0, width, step):
+            incoming = lax.all_to_all(
+                outgoing[:, start : start + step].reshape(owners, capacity, step),
+                "vocab",
+                split_axis=0,
+                concat_axis=0,
+                tiled=True,
+            )
+            dense = matmul(hits, incoming.reshape(owners * capacity, step)).astype(bf)
+            pieces.append(sum_over_dp(dense))
+        grad_word = jnp.concatenate(pieces, 1)
+        small = small.reshape(12, owners, per).transpose(1, 0, 2).reshape(owners, 12 * per)
+        small = jnp.concatenate([small, grad_up_bias.reshape(owners, 4 * per)], 1)
+        wide = 4 * width
+        lines = (seq_len // owners) * width // wide
+        rest = per // 3 - lines
+        small_lines = jnp.pad(small, ((0, 0), (0, rest * wide - 16 * per))).reshape(owners, rest, wide)
+        mixed_grads = jnp.concatenate(
+            [grad_query_weight, grad_key_weight, grad_value_weight, grad_out_weight], 1
+        ).astype(bf)
+        packed = jnp.concatenate(
+            [
+                mixed_grads.reshape(owners, per, wide),
+                grad_pos.astype(bf).reshape(owners, lines, wide),
+                small_lines.astype(bf),
+            ],
+            1,
+        )
+        packed = sum_over_all(packed.reshape(-1, wide))
+        weights = packed[:per]
+        grad_query_weight = weights[:, :width]
+        grad_key_weight = weights[:, width : 2 * width]
+        grad_value_weight = weights[:, 2 * width : 3 * width]
+        grad_out_weight = weights[:, 3 * width :]
+        grad_pos = packed[per : per + lines].reshape(seq_len // owners, width)
+        small = packed[per + lines :].reshape(-1)[: 16 * per].reshape(16, per)
     (
         grad_query_bias,
         grad_value_bias,

time: 790 us -> 659 us (0.83)
  waiting for transfers between devices: 288 us -> 107 us
  Pallas kernels: 0 us -> 157 us
  starting transfers between devices: 87 us -> 29.8 us
  matrix products: 200 us -> 160 us
  other arithmetic: 86.7 us -> 78.5 us
    pallas_call x0 -> x1, Pallas kernels: none -> 157 us  [tail(): pl.pallas_call(tail_kernel, out_shape=(jax.ShapeDtypeStruct((2, 2, 2, par...]
    ppermute x51 -> x18, waiting for transfers between devices: 172 us -> 25.7 us  [swap(): return lax.ppermute(value, axis_name, [(i, i ^ bit) for i in range(size)])]
    ppermute x51 -> x18, starting transfers between devices: 55.3 us -> 17.7 us  [swap(): return lax.ppermute(value, axis_name, [(i, i ^ bit) for i in range(size)])]
    all_to_all x3 -> x0, waiting for transfers between devices: 34.7 us -> none  [local(): lax.all_to_all(outgoing[:, start:start + step].reshape(owners, capacity,...]
    dot_general x10 -> x6, matrix products: 78.4 us -> 50.2 us  [matmul(): return jnp.dot(left, right, preferred_element_type=jnp.float32)]
    all_to_all x3 -> x0, starting transfers between devices: 13.4 us -> none  [local(): lax.all_to_all(outgoing[:, start:start + step].reshape(owners, capacity,...]
    convert_element_type x0 -> x3, other arithmetic: none -> 13.3 us  [the longest x1 8.77 us: local(): grad_word = word_low.astype(jnp.float32)]
    dot_general x6 -> x2, matrix products: 29.6 us -> 18.4 us  [matmul_tn(): lax.dot_general(left, right, (((0,), (0,)), ((), ())), preferred_element_...]
  transfers between devices with their start and end apart: 64 -> 25, of which waited for: 34 -> 10; matrix products, arithmetic and copies ran while one was open for 11% -> 5% of each run, Pallas kernels for 0% -> 24%
where the time goes in v2:
time: 659 us; the launch traced here: 654 us
  matrix products  160 us (24%)
  Pallas kernels  157 us (24%)
  local copies, waits for them, and re-layouts  107 us (16%)
  waiting for transfers between devices  107 us (16%)
  other arithmetic  78.5 us (12%)
  starting transfers between devices  29.8 us (5%)
  blocking collectives  11.7 us (2%)
    pallas_call x1, Pallas kernels, tail(): pl.pallas_call(tail_kernel, out_shape=(jax.ShapeDtypeStruct((2, 2, 2, par...  157 us
    all_to_all x1, waiting for transfers between devices, local(): lax.all_to_all(found, 'vocab', split_axis=0, concat_axis=0, tiled=True)  68.7 us
    dot_general x6, matrix products, matmul(): return jnp.dot(left, right, preferred_element_type=jnp.float32)  50.2 us
    dot_general x6, matrix products, matmul_nt(): lax.dot_general(left, right, (((1,), (1,)), ((), ())), preferred_element_...  35 us
    ppermute x18, waiting for transfers between devices, swap(): return lax.ppermute(value, axis_name, [(i, i ^ bit) for i in range(size)])  25.7 us
    dot_general x2, matrix products, matmul_tn(): lax.dot_general(left, right, (((0,), (0,)), ((), ())), preferred_element_...  18.4 us
    ppermute x18, starting transfers between devices, swap(): return lax.ppermute(value, axis_name, [(i, i ^ bit) for i in range(size)])  17.7 us
    convert_element_type x2, other arithmetic, attend_backward(): grad_scores = (probs * (grad_probs - inner)).astype(jnp.bfloat16)  14.8 us
  transfers between devices with their start and end apart: 25, of which 10 were waited for; matrix products, arithmetic and copies ran while one was open for 5% of the time, Pallas kernels for 24%

profile of v2, /device:TPU:0, one launch (start us, length us, event | category | flops | bytes accessed | tf_op | source)
XLA Modules:
  0.0 654.5 jit_solution(9603458763570377955)
XLA Ops:
  7.2 4.3 scatter_custom_fusion
  11.5 11.7 %all_to_all.14 = s32[8,1,256]{2,1,0:T(1,128)S(1)} all-to-all(s32[8,1,256]{2,1,0:T(1,128)S(1)} %bitcast.423), channel_id=1, replica_groups=mesh['dp'=4,'vocab'=8] {'vocab'}, dimensions={0} | all-to-all | bytes 16384 | tf_op jit(solution)/shard_map/all_to_all | solution.py:623
  23.3 13.5 %gather_fusion = bf16[2048,768]{1,0:T(8,128)(2,1)} fusion(bf16[3840,768]{1,0:T(8,128)(2,1)} %param.31, s32[2048]{0:T(1024)S(1)} %broadcast_clamp_fusion), kind=kCustom, calls=%fused_computation | custom fusion | bytes 6299648 | tf_op jit(solution)/shard_map/gather | solution.py:625
  40.1 4.8 all-to-all-start.1
  47.7 68.7 %all-to-all-done.1 = bf16[8,256,768]{2,1,0:T(8,128)(2,1)} async-done(((bf16[8,256,768]{2,1,0:T(8,128)(2,1)}), bf16[8,256,768]{2,1,0:T(8,128)(2,1)}, u32[]{:S(2)}, u32[]{:S(2)}) %all-to-all-start.1) | async-done | bytes 3145760 | tf_op jit(solution)/shard_map/all_to_all | solution.py:627
  116.4 8.0 %gather_fusion.1 = bf16[1024,768]{1,0:T(8,128)(2,1)} fusion(bf16[2048,768]{1,0:T(8,128)(2,1)} %bitcast.25, s32[1024]{0:T(1024)S(1)} %broadcast_clamp_fusion.1), kind=kCustom, calls=%fused_computation.1 | custom fusion | bytes 3149824 | tf_op jit(solution)/shard_map/gather | solution.py:628
  162.4 25.6 %while.26 = (s32[]{:T(128)}, bf16[2,512,12,64]{1,3,2,0:T(8,128)(2,1)}, f32[2,12,512,1]{2,1,3,0:T(8,128)}, bf16[2,512,12,64]{1,3,2,0:T(8,128)(2,1)}, s32[2]{0:T(1...) while((s32[]{:T(128)}, ...), condition=%wide.region_9.10_spmd, body=%wide.region_6.9_spmd.sunk | while | flops 843442688 | bytes 47411840 | solution.py:651
  163.8 4.1 fusion.179
  171.1 4.1 fusion.181
  176.5 4.1 fusion.179
  183.8 4.2 fusion.181
  196.5 35.4 %multiply_convert_fusion.1 = (bf16[1024,3072]{1,0:T(8,128)(2,1)S(1)}, f32[1024,3072]{1,0:T(8,128)}, f32[1024,3072]{1,0:T(8,128)}) fusion(f32[3072]{0:T(1024)S(1)} %copy-done.70, bf16[768,3072]{1,0:T(8,128)(2,1)S(1)} %bitcast.432, f32[1024,768]{1,0:T(8,128)S(1)} %get-tuple-element.293, f32[768]{0:T(1024)S(1)} %copy-done.75, f32[768]{0:T(1024)S(1)} %copy-done.62, ...), kind=kOutput, calls=%fused_computation.62 | convolution fusion | flops 5043388416 | bytes 39348224 | tf_op jit(solution)/shard_map/dot_general | solution.py:25
  231.9 5.5 fusion.132
  243.4 7.6 %convolution_convert_fusion = bf16[3072,768]{1,0:T(8,128)(2,1)} fusion(bf16[1024,3072]{1,0:T(8,128)(2,1)S(1)} %get-tuple-element.235, f32[1024,768]{1,0:T(8,128)S(1)} %get-tuple-element.234, f32[1024]{0:T(1024)S(1)} %negate_multiply_fusion.3), kind=kOutput, calls=%fused_computation.77 | convolution fusion | flops 4835770368 | bytes 14159872 | tf_op jit(solution)/shard_map/dot_general | solution.py:29
  251.0 19.4 %fusion.134 = (f32[3072]{0:T(1024)}, bf16[1024,3072]{1,0:T(8,128)(2,1)}) fusion(f32[1024,3072]{1,0:T(8,128)} %get-tuple-element.236, bf16[3072,768]{1,0:T(8,128)(2,1)} %param.47, f32[1024,768]{1,0:T(8,128)} %copy-done.19, f32[1024]{0:T(1024)S(1)} %negate_multiply_fusion.3, f32[1024,3072]{1,0:T(8,128)} %get-tuple-element.294, f32[3072]{0:T(1024)S(1)} %copy-done.70), kind=kOutput, calls=%fused_computation.303 | convolution fusion | flops 4883739648 | bytes 39350272 | tf_op jit(solution)/shard_map/dot_general | solution.py:35
  270.4 10.8 %convolution_convert_fusion.1 = bf16[768,3072]{1,0:T(8,128)(2,1)} fusion(bf16[1024,3072]{1,0:T(8,128)(2,1)} %get-tuple-element.301, f32[1024,768]{1,0:T(8,128)} %copy-done.17, f32[768]{0:T(1024)S(1)} %copy-done.75, f32[768]{0:T(1024)S(1)} %copy-done.62, f32[1024]{0:T(1024)S(1)} %fusion.115, f32[1024]{0:T(1024)S(1)} %broadcast_multiply_fusion.1), kind=kOutput, calls=%fused_computation.78 | convolution fusion | flops 4838129664 | bytes 14170112 | tf_op jit(solution)/shard_map/dot_general | solution.py:29
  281.3 9.0 %multiply_reduce_fusion.2 = (f32[768]{0:T(1024)}, f32[1024]{0:T(1024)S(1)}, f32[768]{0:T(1024)}, f32[1024,768]{1,0:T(8,128)S(1)}) fusion(f32[1024,768]{1,0:T(8,128)S(1)} %copy-done.18, f32[1024]{0:T(1024)S(1)} %fusion.115, f32[1024]{0:T(1024)S(1)} %broadcast_multiply_fusion.1, f32[768]{0:T(1024)S(1)} %copy-done.62, bf16[768,3072]{1,0:T(8,128)(2,1)} %param.45, ...), kind=kOutput, calls=%fused_computation.99 | convolution fusion | flops 4839699456 | bytes 20472832 | tf_op jit(solution)/shard_map/dot_general | solution.py:35
  299.5 4.0 reshape.506
  306.4 55.9 %while.27 = (s32[]{:T(128)}, f32[2,512,12,64]{1,3,2,0:T(8,128)}, bf16[2,512,12,64]{1,3,2,0:T(8,128)(2,1)}, f32[2,512,12,64]{1,3,2,0:T(8,128)}, bf16[2,512,12,64]...) while((s32[]{:T(128)}, f32[2,512,12,64]{1,3,2,0:T(8,128)}, ...), condition=%wide.region_20.21_spmd, body=%wide.region_18.20_spmd.sunk | while | flops 2061232640 | bytes 161414480 | solution.py:679
  311.3 7.3 %multiply_reduce_fusion.9 = (f32[12,512]{1,0:T(8,128)S(1)}, f32[12,512,512]{1,2,0:T(8,128)}) fusion(f32[12,512,512]{1,2,0:T(8,128)S(1)} %fusion.190, f32[12,512]{1,0:T(8,128)S(1)} %dynamic-slice_bitcast_fusion.8, pred[512]{0:T(512)(128)(4,1)S(1)} %iota_compare_fusion.10, bf16[2,512,12,64]{1,3,2,0:T(8,128)(2,1)S(1)} %copy-done.11, ...), kind=kOutput, calls=%fused_computation.26.clone.1 | convolution fusion | flops 418375680 | bytes 26797568 | tf_op jit(solution)/shard_map/while/body/eval_jaxpr/qhd,khd->hqk/dot_general | solution.py:66
  318.6 7.4 %multiply_convert_fusion.3 = bf16[12,512,512]{1,2,0:T(8,128)(2,1)S(1)} fusion(f32[12,512,512]{1,2,0:T(8,128)} %get-tuple-element.416, f32[12,512,512]{1,2,0:T(8,128)S(1)} %fusion.190, f32[12,512]{1,0:T(8,128)S(1)} %get-tuple-element.417, f32[12,512]{1,0:T(8,128)S(1)} %dynamic-slice_bitcast_fusion.8, pred[512]{0:T(512)(128)(4,1)S(1)} %iota_compare_fusion.10), kind=kLoop, calls=%fused_computation.25.clone.1 | loop fusion | flops 18874368 | bytes 31506944 | tf_op jit(solution)/shard_map/while/body/eval_jaxpr/convert_element_type | solution.py:68
  330.6 3.9 bitcast_dynamic-update-slice_fusion.11
  338.9 7.3 %multiply_reduce_fusion.9 = (f32[12,512]{1,0:T(8,128)S(1)}, f32[12,512,512]{1,2,0:T(8,128)}) fusion(f32[12,512,512]{1,2,0:T(8,128)S(1)} %fusion.190, f32[12,512]{1,0:T(8,128)S(1)} %dynamic-slice_bitcast_fusion.8, pred[512]{0:T(512)(128)(4,1)S(1)} %iota_compare_fusion.10, bf16[2,512,12,64]{1,3,2,0:T(8,128)(2,1)S(1)} %copy-done.11, ...), kind=kOutput, calls=%fused_computation.26.clone.1 | convolution fusion | flops 418375680 | bytes 26797568 | tf_op jit(solution)/shard_map/while/body/eval_jaxpr/qhd,khd->hqk/dot_general | solution.py:66
  346.3 7.4 %multiply_convert_fusion.3 = bf16[12,512,512]{1,2,0:T(8,128)(2,1)S(1)} fusion(f32[12,512,512]{1,2,0:T(8,128)} %get-tuple-element.416, f32[12,512,512]{1,2,0:T(8,128)S(1)} %fusion.190, f32[12,512]{1,0:T(8,128)S(1)} %get-tuple-element.417, f32[12,512]{1,0:T(8,128)S(1)} %dynamic-slice_bitcast_fusion.8, pred[512]{0:T(512)(128)(4,1)S(1)} %iota_compare_fusion.10), kind=kLoop, calls=%fused_computation.25.clone.1 | loop fusion | flops 18874368 | bytes 31506944 | tf_op jit(solution)/shard_map/while/body/eval_jaxpr/convert_element_type | solution.py:68
  362.4 5.5 fusion.125
  410.4 157.1 %tail.1 = (bf16[2,2,2,480,768]{4,3,2,1,0:T(8,128)(2,1)}, bf16[2,2,32,3072]{3,2,1,0:T(8,128)(2,1)}) custom-call(bf16[1024,768]{1,0:T(8,128)(2,1)} %bitcast.393, s32[1,1024]{1,0:T(1,128)} %fusion.109.slot, s32[1,2048]{1,0:T(1,128)} %bitcast.414, f32[16,768]{1,0:T(8,128)} %concatenate.15.small, bf16[1024,768]{1,0:T(8,128)(2,1)} %copy-done.26, ...), custom_call_target="tpu_custom_call" | custom-call | tf_op jit(solution)/shard_map/tail/pallas_call | solution.py:537
  569.8 8.8 %bitcast_convert_fusion = f32[3840,768]{1,0:T(8,128)} fusion(bf16[2,2,2,480,768]{4,3,2,1,0:T(8,128)(2,1)} %get-tuple-element.120), kind=kLoop, calls=%fused_computation.76 | loop fusion | flops 2949120 | bytes 17694720 | tf_op jit(solution)/shard_map/convert_element_type | solution.py:744
  588.9 8.8 %collective-permute-done.15 = bf16[2,2,96,768]{3,2,0,1:T(8,128)(2,1)S(1)} collective-permute-done((bf16[2,2,96,768]{3,2,0,1:T(8,128)(2,1)S(1)}, bf16[2,2,96,768]{3,2,0,1:T(8,128)(2,1)S(1)}, u32[]{:S(2)}, u32[]{:S(2)}) %collective-permute-start.15) | collective-permute-done | bytes 589856 | tf_op jit(solution)/shard_map/ppermute | solution.py:81
  600.2 10.1 %collective-permute-done.3 = bf16[2,2,24,3072]{3,2,0,1:T(8,128)(2,1)S(1)} collective-permute-done((bf16[2,2,24,3072]{3,2,0,1:T(8,128)(2,1)S(1)}, bf16[2,2,24,3072]{3,2,0,1:T(8,128)(2,1)S(1)}, u32[]{:S(2)}, u32[]{:S(2)}) %collective-permute-start.3) | collective-permute-done | bytes 589856 | tf_op jit(solution)/shard_map/ppermute | solution.py:81
  612.9 5.2 collective-permute-done.16
  628.1 5.2 collective-permute-done.18
  635.6 5.3 collective-permute-done.6
  (416 shorter events, 192.7 us)
Async XLA Ops:
  0.7 191.4 %copy-start = (bf16[768,768]{1,0:T(8,128)(2,1)S(1)}, bf16[768,768]{1,0:T(8,128)(2,1)}, u32[]{:S(2)}) copy-start(bf16[768,768]{1,0:T(8,128)(2,1)} %param.41) | copy-start | bytes 3538948
  23.3 13.5 %copy-start.41 = (s32[8,1,256]{2,1,0:T(1,128)}, s32[8,1,256]{2,1,0:T(1,128)S(1)}, u32[]{:S(2)}) copy-start(s32[8,1,256]{2,1,0:T(1,128)S(1)} %all_to_all.14) | copy-start | bytes 24580
  40.1 76.3 %all-to-all-start.1 = ((bf16[8,256,768]{2,1,0:T(8,128)(2,1)}), bf16[8,256,768]{2,1,0:T(8,128)(2,1)}, u32[]{:S(2)}, u32[]{:S(2)}) async-start(bf16[8,256,768]{2,1,0:T(8,128)(2,1)} %broadcast_select_fusion), calls=%async_computation.1 | async-start | bytes 6291456 | tf_op jit(solution)/shard_map/all_to_all | solution.py:627
  192.1 39.7 %slice-start.4 = ((s8[4718592]{0:T(1024)(128)(4,1)}), s8[4194304]{0:T(1024)(128)(4,1)S(1)}, s32[]{:S(2)}) async-start(s8[4718592]{0:T(1024)(128)(4,1)} %bitcast.429), calls=%async_computation.6 | async-start | bytes 8388608
  193.8 38.0 %copy-start.17 = (f32[1024,768]{1,0:T(8,128)}, f32[1024,768]{1,0:T(8,128)S(1)}, u32[]{:S(2)}) copy-start(f32[1024,768]{1,0:T(8,128)S(1)} %get-tuple-element.293) | copy-start | bytes 9437188
  196.5 35.4 %slice-start.5 = ((s8[4718592]{0:T(1024)(128)(4,1)}), s8[524288]{0:T(1024)(128)(4,1)S(1)}, s32[]{:S(2)}) async-start(s8[4718592]{0:T(1024)(128)(4,1)} %bitcast.429), calls=%async_computation.7 | async-start | bytes 1048576
  196.5 35.4 %copy-start.74 = (f32[768]{0:T(1024)S(1)}, f32[768]{0:T(1024)}, u32[]{:S(2)}) copy-start(f32[768]{0:T(1024)} %param.48) | copy-start | bytes 9220
  270.4 10.8 %copy-start.78 = (bf16[1024,3072]{1,0:T(8,128)(2,1)S(1)}, bf16[1024,3072]{1,0:T(8,128)(2,1)}, u32[]{:S(2)}) copy-start(bf16[1024,3072]{1,0:T(8,128)(2,1)} %get-tuple-element.301) | copy-start | bytes 18874372
  404.9 173.7 %collective-permute-start.12 = (bf16[4,384,768]{2,1,0:T(8,128)(2,1)}, bf16[4,384,768]{2,1,0:T(8,128)(2,1)}, u32[]{:S(2)}, u32[]{:S(2)}) collective-permute-start(bf16[4,384,768]{2,1,0:T(8,128)(2,1)} %dynamic-slice_bitcast_fusion.1), channel_id=1, source_target_pairs={{0,1},{1,0},{2,3},{3,2},{4,5},{5,4},{6,7},{7,6},{8,9},{9,8},{10,11... | collective-permute-start | bytes 7077896 | tf_op jit(solution)/shard_map/ppermute | solution.py:81
  408.2 175.5 %collective-permute-start = (bf16[4,96,3072]{2,1,0:T(8,128)(2,1)}, bf16[4,96,3072]{2,1,0:T(8,128)(2,1)}, u32[]{:S(2)}, u32[]{:S(2)}) collective-permute-start(bf16[4,96,3072]{2,1,0:T(8,128)(2,1)} %dynamic-slice_bitcast_fusion.2), channel_id=1, source_target_pairs={{0,1},{1,0},{2,3},{3,2},{4,5},{5,4},{6,7},{7,6},{8,9},{9,8},{10,11... | collective-permute-start | bytes 7077896 | tf_op jit(solution)/shard_map/ppermute | solution.py:81
  581.4 16.3 %collective-permute-start.15 = (bf16[2,2,96,768]{3,2,0,1:T(8,128)(2,1)S(1)}, bf16[2,2,96,768]{3,2,0,1:T(8,128)(2,1)S(1)}, u32[]{:S(2)}, u32[]{:S(2)}) collective-permute-start(bf16[2,2,96,768]{3,2,0,1:T(8,128)(2,1)S(1)} %bitcast.410), channel_id=1, source_target_pairs={{0,16},{8,24},{16,0},{24,8},{1,17},{9,25},{17,1},{25,9},{2,18},{10... | collective-permute-start | bytes 1769480 | tf_op jit(solution)/shard_map/ppermute | solution.py:81
  582.8 16.4 %collective-permute-start.13 = (bf16[2,2,96,768]{3,2,0,1:T(8,128)(2,1)S(1)}, bf16[2,2,96,768]{3,2,0,1:T(8,128)(2,1)S(1)}, u32[]{:S(2)}, u32[]{:S(2)}) collective-permute-start(bf16[2,2,96,768]{3,2,0,1:T(8,128)(2,1)S(1)} %bitcast.409), channel_id=1, source_target_pairs={{0,8},{8,0},{16,24},{24,16},{1,9},{9,1},{17,25},{25,17},{2,10},{10... | collective-permute-start | bytes 1769480 | tf_op jit(solution)/shard_map/ppermute | solution.py:81
  586.6 23.8 %collective-permute-start.3 = (bf16[2,2,24,3072]{3,2,0,1:T(8,128)(2,1)S(1)}, bf16[2,2,24,3072]{3,2,0,1:T(8,128)(2,1)S(1)}, u32[]{:S(2)}, u32[]{:S(2)}) collective-permute-start(bf16[2,2,24,3072]{3,2,0,1:T(8,128)(2,1)S(1)} %bitcast.412), channel_id=1, source_target_pairs={{0,16},{8,24},{16,0},{24,8},{1,17},{9,25},{17,1},{25,9},{2,18},{10... | collective-permute-start | bytes 1769480 | tf_op jit(solution)/shard_map/ppermute | solution.py:81
  588.0 23.8 %collective-permute-start.1 = (bf16[2,2,24,3072]{3,2,0,1:T(8,128)(2,1)S(1)}, bf16[2,2,24,3072]{3,2,0,1:T(8,128)(2,1)S(1)}, u32[]{:S(2)}, u32[]{:S(2)}) collective-permute-start(bf16[2,2,24,3072]{3,2,0,1:T(8,128)(2,1)S(1)} %bitcast.411), channel_id=1, source_target_pairs={{0,8},{8,0},{16,24},{24,16},{1,9},{9,1},{17,25},{25,17},{2,10},{10... | collective-permute-start | bytes 1769480 | tf_op jit(solution)/shard_map/ppermute | solution.py:81
  597.9 20.2 %collective-permute-start.16 = (bf16[2,96,768]{2,1,0:T(8,128)(2,1)S(1)}, bf16[2,96,768]{2,1,0:T(8,128)(2,1)S(1)}, u32[]{:S(2)}, u32[]{:S(2)}) collective-permute-start(bf16[2,96,768]{2,1,0:T(8,128)(2,1)S(1)} %dynamic-slice_bitcast_fusion.3), channel_id=1, source_target_pairs={{0,8},{8,0},{16,24},{24,16},{1,9},{9,1},{17,25},{25,17},{2,10},{10... | collective-permute-start | bytes 884744 | tf_op jit(solution)/shard_map/ppermute | solution.py:81
  599.3 18.8 %collective-permute-start.14 = (bf16[2,96,768]{2,1,0:T(8,128)(2,1)S(1)}, bf16[2,96,768]{2,1,0:T(8,128)(2,1)S(1)}, u32[]{:S(2)}, u32[]{:S(2)}) collective-permute-start(bf16[2,96,768]{2,1,0:T(8,128)(2,1)S(1)} %dynamic-slice_bitcast_fusion.4), channel_id=1, source_target_pairs={{0,16},{8,24},{16,0},{24,8},{1,17},{9,25},{17,1},{25,9},{2,18},{10... | collective-permute-start | bytes 884744 | tf_op jit(solution)/shard_map/ppermute | solution.py:81
  610.5 12.7 %collective-permute-start.4 = (bf16[2,24,3072]{2,1,0:T(8,128)(2,1)S(1)}, bf16[2,24,3072]{2,1,0:T(8,128)(2,1)S(1)}, u32[]{:S(2)}, u32[]{:S(2)}) collective-permute-start(bf16[2,24,3072]{2,1,0:T(8,128)(2,1)S(1)} %dynamic-slice_bitcast_fusion.5), channel_id=1, source_target_pairs={{0,8},{8,0},{16,24},{24,16},{1,9},{9,1},{17,25},{25,17},{2,10},{10... | collective-permute-start | bytes 884744 | tf_op jit(solution)/shard_map/ppermute | solution.py:81
  612.0 11.3 %collective-permute-start.2 = (bf16[2,24,3072]{2,1,0:T(8,128)(2,1)S(1)}, bf16[2,24,3072]{2,1,0:T(8,128)(2,1)S(1)}, u32[]{:S(2)}, u32[]{:S(2)}) collective-permute-start(bf16[2,24,3072]{2,1,0:T(8,128)(2,1)S(1)} %dynamic-slice_bitcast_fusion.6), channel_id=1, source_target_pairs={{0,16},{8,24},{16,0},{24,8},{1,17},{9,25},{17,1},{25,9},{2,18},{10... | collective-permute-start | bytes 884744 | tf_op jit(solution)/shard_map/ppermute | solution.py:81
  618.4 8.8 %collective-permute-start.17 = (bf16[96,768]{1,0:T(8,128)(2,1)S(1)}, bf16[96,768]{1,0:T(8,128)(2,1)S(1)}, u32[]{:S(2)}, u32[]{:S(2)}) collective-permute-start(bf16[96,768]{1,0:T(8,128)(2,1)S(1)} %get-tuple-element.278), channel_id=1, source_target_pairs={{0,2},{1,3},{2,4},{3,5},{4,6},{5,7},{6,0},{7,1},{8,10},{9,11},{10,... | collective-permute-start | bytes 442376 | tf_op jit(solution)/shard_map/ppermute | solution.py:135
  619.3 14.1 %collective-permute-start.18 = (bf16[96,768]{1,0:T(8,128)(2,1)S(1)}, bf16[96,768]{1,0:T(8,128)(2,1)S(1)}, u32[]{:S(2)}, u32[]{:S(2)}) collective-permute-start(bf16[96,768]{1,0:T(8,128)(2,1)S(1)} %get-tuple-element.279), channel_id=1, source_target_pairs={{0,4},{1,5},{2,6},{3,7},{4,0},{5,1},{6,2},{7,3},{8,12},{9,13},{10,... | collective-permute-start | bytes 442376 | tf_op jit(solution)/shard_map/ppermute | solution.py:135
  621.6 11.7 %collective-permute-start.19 = (bf16[96,768]{1,0:T(8,128)(2,1)S(1)}, bf16[96,768]{1,0:T(8,128)(2,1)S(1)}, u32[]{:S(2)}, u32[]{:S(2)}) collective-permute-start(bf16[96,768]{1,0:T(8,128)(2,1)S(1)} %get-tuple-element.280), channel_id=1, source_target_pairs={{0,6},{1,7},{2,0},{3,1},{4,2},{5,3},{6,4},{7,5},{8,14},{9,15},{10,... | collective-permute-start | bytes 442376 | tf_op jit(solution)/shard_map/ppermute | solution.py:135
  623.6 12.0 %collective-permute-start.5 = (bf16[24,3072]{1,0:T(8,128)(2,1)S(1)}, bf16[24,3072]{1,0:T(8,128)(2,1)S(1)}, u32[]{:S(2)}, u32[]{:S(2)}) collective-permute-start(bf16[24,3072]{1,0:T(8,128)(2,1)S(1)} %get-tuple-element.285), channel_id=1, source_target_pairs={{0,2},{1,3},{2,4},{3,5},{4,6},{5,7},{6,0},{7,1},{8,10},{9,11},{10,... | collective-permute-start | bytes 442376 | tf_op jit(solution)/shard_map/ppermute | solution.py:135
  624.1 16.8 %collective-permute-start.6 = (bf16[24,3072]{1,0:T(8,128)(2,1)S(1)}, bf16[24,3072]{1,0:T(8,128)(2,1)S(1)}, u32[]{:S(2)}, u32[]{:S(2)}) collective-permute-start(bf16[24,3072]{1,0:T(8,128)(2,1)S(1)} %get-tuple-element.286), channel_id=1, source_target_pairs={{0,4},{1,5},{2,6},{3,7},{4,0},{5,1},{6,2},{7,3},{8,12},{9,13},{10,... | collective-permute-start | bytes 442376 | tf_op jit(solution)/shard_map/ppermute | solution.py:135
  627.2 13.7 %collective-permute-start.7 = (bf16[24,3072]{1,0:T(8,128)(2,1)S(1)}, bf16[24,3072]{1,0:T(8,128)(2,1)S(1)}, u32[]{:S(2)}, u32[]{:S(2)}) collective-permute-start(bf16[24,3072]{1,0:T(8,128)(2,1)S(1)} %get-tuple-element.287), channel_id=1, source_target_pairs={{0,6},{1,7},{2,0},{3,1},{4,2},{5,3},{6,4},{7,5},{8,14},{9,15},{10,... | collective-permute-start | bytes 442376 | tf_op jit(solution)/shard_map/ppermute | solution.py:135
  633.5 9.7 %collective-permute-start.20 = (bf16[96,768]{1,0:T(8,128)(2,1)S(1)}, bf16[96,768]{1,0:T(8,128)(2,1)S(1)}, u32[]{:S(2)}, u32[]{:S(2)}) collective-permute-start(bf16[96,768]{1,0:T(8,128)(2,1)S(1)} %fusion.82), channel_id=1, source_target_pairs={{0,8},{8,0},{16,24},{24,16},{1,9},{9,1},{17,25},{25,17},{2,10},{10... | collective-permute-start | bytes 442376 | tf_op jit(solution)/shard_map/ppermute | solution.py:81
  634.1 12.3 %collective-permute-start.22 = (bf16[96,768]{1,0:T(8,128)(2,1)S(1)}, bf16[96,768]{1,0:T(8,128)(2,1)S(1)}, u32[]{:S(2)}, u32[]{:S(2)}) collective-permute-start(bf16[96,768]{1,0:T(8,128)(2,1)S(1)} %fusion.82), channel_id=1, source_target_pairs={{0,16},{8,24},{16,0},{24,8},{1,17},{9,25},{17,1},{25,9},{2,18},{10... | collective-permute-start | bytes 442376 | tf_op jit(solution)/shard_map/ppermute | solution.py:81
  641.1 6.9 %collective-permute-start.8 = (bf16[24,3072]{1,0:T(8,128)(2,1)S(1)}, bf16[24,3072]{1,0:T(8,128)(2,1)S(1)}, u32[]{:S(2)}, u32[]{:S(2)}) collective-permute-start(bf16[24,3072]{1,0:T(8,128)(2,1)S(1)} %fusion.85), channel_id=1, source_target_pairs={{0,8},{8,0},{16,24},{24,16},{1,9},{9,1},{17,25},{25,17},{2,10},{10... | collective-permute-start | bytes 442376 | tf_op jit(solution)/shard_map/ppermute | solution.py:81
  641.6 6.9 %collective-permute-start.10 = (bf16[24,3072]{1,0:T(8,128)(2,1)S(1)}, bf16[24,3072]{1,0:T(8,128)(2,1)S(1)}, u32[]{:S(2)}, u32[]{:S(2)}) collective-permute-start(bf16[24,3072]{1,0:T(8,128)(2,1)S(1)} %fusion.85), channel_id=1, source_target_pairs={{0,16},{8,24},{16,0},{24,8},{1,17},{9,25},{17,1},{25,9},{2,18},{10... | collective-permute-start | bytes 442376 | tf_op jit(solution)/shard_map/ppermute | solution.py:81
  643.2 7.0 %collective-permute-start.21 = (bf16[96,384]{1,0:T(8,128)(2,1)S(1)}, bf16[96,384]{1,0:T(8,128)(2,1)S(1)}, u32[]{:S(2)}, u32[]{:S(2)}) collective-permute-start(bf16[96,384]{1,0:T(8,128)(2,1)S(1)} %slice.165), channel_id=1, source_target_pairs={{0,16},{8,24},{16,0},{24,8},{1,17},{9,25},{17,1},{25,9},{2,18},{10... | collective-permute-start | bytes 221192 | tf_op jit(solution)/shard_map/ppermute | solution.py:81
  646.4 4.4 collective-permute-start.23
  648.0 4.4 collective-permute-start.9
  648.6 4.4 collective-permute-start.11
  (88 other events, 320.7 us)

commit v3 on v2

--- a/solution.py
+++ b/solution.py
@@ -35,45 +35,6 @@
     return lax.dot_general(
         left, right, (((1,), (1,)), ((), ())), preferred_element_type=jnp.float32
     )
-
-
-def masked_scores(query, keys, length):
-    scores = jnp.einsum("qhd,khd->hqk", query, keys, preferred_element_type=jnp.float32) * HEAD ** (
-        -0.5
-    )
-    visible = jnp.arange(L) < length
-    return jnp.where(visible[None, None, :], scores, -1000000000.0)
-
-
-def attend_forward(block):
-    query, keys, values, length = block
-    scores = masked_scores(query, keys, length)
-    highest = jnp.max(scores, -1, keepdims=True)
-    expd = jnp.exp(scores - highest)
-    totals = jnp.sum(expd, -1, keepdims=True)
-    probs_low = (expd / totals).astype(jnp.bfloat16)
-    mixed = jnp.einsum("hqk,khd->qhd", probs_low, values, preferred_element_type=jnp.float32)
-    return (mixed.astype(jnp.bfloat16), highest + jnp.log(totals))
-
-
-def attend_backward(block):
-    query, keys, values, grad_mixed, logsum, length = block
-    probs = jnp.exp(masked_scores(query, keys, length) - logsum)
-    probs_low = probs.astype(jnp.bfloat16)
-    grad_values = jnp.einsum(
-        "hqk,qhd->khd", probs_low, grad_mixed, preferred_element_type=jnp.float32
-    )
-    grad_probs = jnp.einsum("qhd,khd->hqk", grad_mixed, values, preferred_element_type=jnp.float32)
-    inner = jnp.sum(grad_probs * probs, -1, keepdims=True)
-    grad_scores = (probs * (grad_probs - inner)).astype(jnp.bfloat16)
-    scale = HEAD ** (-0.5)
-    grad_query = (
-        jnp.einsum("hqk,khd->qhd", grad_scores, keys, preferred_element_type=jnp.float32) * scale
-    )
-    grad_keys = (
-        jnp.einsum("hqk,qhd->khd", grad_scores, query, preferred_element_type=jnp.float32) * scale
-    )
-    return (grad_query, grad_keys, grad_values)
 
 
 def swap(value, axis_name, bit):
@@ -170,9 +131,323 @@
     return jnp.concatenate(parts, 0).astype(jnp.float32)
 
 
-MESH = pl.DeviceIdType.MESH
 BF = jnp.bfloat16
 F32 = jnp.float32
+MIB = 1024 * 1024
+
+
+def dot_nt(left, right):
+    return lax.dot_general(left, right, (((1,), (1,)), ((), ())), preferred_element_type=F32)
+
+
+def dot_nn(left, right):
+    return jnp.dot(left, right, preferred_element_type=F32)
+
+
+def stats(values):
+    center = values - jnp.mean(values, -1, keepdims=True)
+    inverse = lax.rsqrt(jnp.mean(center * center, -1, keepdims=True) + EPSILON)
+    return center * inverse, inverse
+
+
+def norm_back(grad, gain, unit, inverse):
+    scaled = grad * gain
+    return inverse * (
+        scaled
+        - jnp.mean(scaled, -1, keepdims=True)
+        - unit * jnp.mean(scaled * unit, -1, keepdims=True)
+    )
+
+
+def column_sum(values):
+    return jnp.sum(values, 0, keepdims=True)
+
+
+TAIL_SCALE = 0.33
+TAIL_TERMS = (
+    -0.13534782292195252,
+    0.4602463244004558,
+    -0.3511662200543899,
+    0.4085159085223644,
+    0.04721176063633592,
+    0.2012267561020528,
+    0.1829554472050349,
+    0.1863578383326851,
+)
+
+
+def normal_parts(u):
+    t = 1.0 / (1.0 + (TAIL_SCALE * 0.5**0.5) * jnp.abs(u))
+    poly = TAIL_TERMS[0]
+    for term in TAIL_TERMS[1:]:
+        poly = poly * t + term
+    bell = jnp.exp(u * u * -0.5)
+    below = (0.5 * t) * poly * bell
+    return jnp.where(u >= 0, 1.0 - below, below), bell * 0.3989422804014327
+
+
+def attend_kernel(
+    lengths, normed, wq, wk, wv, wo, query_bias, value_bias, out_bias,
+    low, q_out, k_out, v_out, mixed_out, first_out, probs_out, bias,
+):
+    tokens, width = normed.shape
+    tile = 256
+    low[...] = normed[...].astype(BF)
+
+    def project(n, carry):
+        at = pl.ds(pl.multiple_of(n * tile, tile), tile)
+        x = low[...]
+        query = (dot_nn(x, wq[:, at]) + query_bias[:, at]).astype(BF)
+        q_out[:, at] = query * BF(HEAD**-0.5)
+        k_out[:, at] = dot_nn(x, wk[:, at]).astype(BF)
+        v_out[:, at] = (dot_nn(x, wv[:, at]) + value_bias[:, at]).astype(BF)
+        return carry
+
+    lax.fori_loop(0, width // tile, project, 0)
+    seen = lax.broadcasted_iota(jnp.int32, bias.shape, 0) < lengths[pl.program_id(0)]
+    bias[...] = jnp.where(seen, 0.0, -1000000000.0)
+
+    def pair(j, carry):
+        at = pl.ds(pl.multiple_of(j * 2 * HEAD, 2 * HEAD), 2 * HEAD)
+        q, k, turned = q_out[:, at], k_out[:, at], v_out[:, at].T
+        lane = lax.broadcasted_iota(jnp.int32, k.shape, 1)
+        parts = []
+        for side in range(2):
+            mine = (lane >= HEAD) if side else (lane < HEAD)
+            scores = dot_nt(jnp.where(mine, k, jnp.zeros_like(k)), q)
+            scores = scores + jnp.concatenate([bias[...]] * (tokens // 128), 1)
+            expd = jnp.exp(scores - jnp.max(scores, 0, keepdims=True))
+            probs = (expd * (1.0 / jnp.sum(expd, 0, keepdims=True))).astype(BF)
+            probs_out[0, 2 * j + side] = probs
+            parts.append(dot_nn(turned[side * HEAD : (side + 1) * HEAD], probs))
+        mixed_out[:, at] = jnp.concatenate(parts, 0).T.astype(BF)
+        return carry
+
+    lax.fori_loop(0, HEADS // 2, pair, 0)
+
+    def close(n, carry):
+        at = pl.ds(pl.multiple_of(n * tile, tile), tile)
+        first_out[:, at] = normed[:, at] + dot_nn(mixed_out[...], wo[:, at]) + out_bias[:, at]
+        return carry
+
+    lax.fori_loop(0, width // tile, close, 0)
+
+
+def fixed(shape):
+    return pl.BlockSpec(shape, lambda i, *_: (0,) * len(shape), pipeline_mode=pl.Buffered(1))
+
+
+def rows_of(rows, width):
+    return pl.BlockSpec((rows, width), lambda i, *_: (i, 0))
+
+
+def row(vector):
+    return vector.reshape(1, -1)
+
+
+def attend(lengths, normed, wq, wk, wv, wo, query_bias, value_bias, out_bias):
+    tokens, width = normed.shape
+    seqs = lengths.shape[0]
+    size = tokens // seqs
+    low = jax.ShapeDtypeStruct((tokens, width), BF)
+    part = rows_of(size, width)
+    return pl.pallas_call(
+        attend_kernel,
+        grid_spec=pltpu.PrefetchScalarGridSpec(
+            num_scalar_prefetch=1,
+            grid=(seqs,),
+            in_specs=[part] + [fixed((width, width))] * 4 + [fixed((1, width))] * 3,
+            out_specs=[part] * 6 + [pl.BlockSpec((1, HEADS, size, size), lambda i, *_: (i, 0, 0, 0))],
+            scratch_shapes=[pltpu.VMEM((size, 128), F32)],
+        ),
+        out_shape=[low] * 5
+        + [jax.ShapeDtypeStruct((tokens, width), F32), jax.ShapeDtypeStruct((seqs, HEADS, size, size), BF)],
+        compiler_params=pltpu.CompilerParams(vmem_limit_bytes=60 * MIB),
+        cost_estimate=pl.CostEstimate(flops=20 * 10**9, bytes_accessed=30 * 10**6, transcendentals=0),
+        name="attend",
+    )(lengths, normed, wq, wk, wv, wo, row(query_bias), row(value_bias), row(out_bias))
+
+
+def feed_kernel(
+    first, cotangent, up, down, up_bias, down_bias, attn_gain, attn_bias, final_gain, final_bias,
+    encoded, active, second_low, hidden_low, upper_low, first_grad, sums, up_sum,
+    slope,
+):
+    width = first.shape[1]
+    units = up.shape[1]
+    block = 768
+    unit, inverse = stats(first[...])
+    hidden = unit * attn_gain[...] + attn_bias[...]
+    hidden_low[...] = hidden.astype(BF)
+    total = hidden + down_bias[...]
+    for n in range(units // block):
+        at = pl.ds(n * block, block)
+        upper = dot_nn(hidden_low[...], up[:, at]) + up_bias[:, at]
+        below, density = normal_parts(upper)
+        active[:, at] = (upper * below).astype(BF)
+        slope[:, at] = below + upper * density
+        total = total + dot_nn(active[:, at], down[at, :])
+    unit_out, inverse_out = stats(total)
+    encoded[...] = unit_out * final_gain[...] + final_bias[...]
+    grad = cotangent[...].astype(F32)
+    grad_second = norm_back(grad, final_gain[...], unit_out, inverse_out)
+    second_low[...] = grad_second.astype(BF)
+
+    @pl.when(pl.program_id(0) == 0)
+    def _():
+        sums[...] = jnp.zeros_like(sums)
+        up_sum[...] = jnp.zeros_like(up_sum)
+
+    sums[0:1, :] += column_sum(grad * unit_out)
+    sums[1:2, :] += column_sum(grad)
+    sums[2:3, :] += column_sum(grad_second)
+    total = grad_second
+    for n in range(units // block):
+        at = pl.ds(n * block, block)
+        grad_upper = dot_nt(second_low[...], down[at, :]) * slope[:, at]
+        up_sum[:, at] += column_sum(grad_upper)
+        upper_low[:, at] = grad_upper.astype(BF)
+        total = total + dot_nt(upper_low[:, at], up[:, at])
+    grad_first = norm_back(total, attn_gain[...], unit, inverse)
+    sums[3:4, :] += column_sum(total * unit)
+    sums[4:5, :] += column_sum(total)
+    sums[5:6, :] += column_sum(grad_first)
+    first_grad[...] = grad_first
+
+
+def feed(first, cotangent, up, down, up_bias, down_bias, attn_gain, attn_bias, final_gain, final_bias):
+    tokens, width = first.shape
+    units = up.shape[1]
+    tile = 256
+    part, wide = rows_of(tile, width), rows_of(tile, units)
+    vector = fixed((1, width))
+    return pl.pallas_call(
+        feed_kernel,
+        grid=(tokens // tile,),
+        in_specs=[part, part, fixed((width, units)), fixed((units, width)), fixed((1, units))] + [vector] * 5,
+        out_specs=[part, wide, part, part, wide, part, fixed((8, width)), fixed((1, units))],
+        out_shape=[
+            jax.ShapeDtypeStruct((tokens, width), F32),
+            jax.ShapeDtypeStruct((tokens, units), BF),
+            jax.ShapeDtypeStruct((tokens, width), BF),
+            jax.ShapeDtypeStruct((tokens, width), BF),
+            jax.ShapeDtypeStruct((tokens, units), BF),
+            jax.ShapeDtypeStruct((tokens, width), F32),
+            jax.ShapeDtypeStruct((8, width), F32),
+            jax.ShapeDtypeStruct((1, units), F32),
+        ],
+        scratch_shapes=[pltpu.VMEM((tile, units), F32)],
+        compiler_params=pltpu.CompilerParams(vmem_limit_bytes=60 * MIB),
+        cost_estimate=pl.CostEstimate(flops=40 * 10**9, bytes_accessed=40 * 10**6, transcendentals=0),
+        name="feed",
+    )(
+        first, cotangent, up, down, row(up_bias), row(down_bias), row(attn_gain), row(attn_bias),
+        row(final_gain), row(final_bias),
+    )
+
+
+def attend_back_kernel(
+    grad_first, embedded, kinds, q_in, k_in, v_in, probs_in, wq, wk, wv, wo, emb_gain,
+    first_low, dq, dk, dv, emb_low, sums,
+    grad_mixed, total,
+):
+    tokens, width = grad_first.shape
+    tile = 256
+
+    @pl.when(pl.program_id(0) == 0)
+    def _():
+        sums[...] = jnp.zeros_like(sums)
+
+    first_low[...] = grad_first[...].astype(BF)
+
+    def open_(n, carry):
+        at = pl.ds(pl.multiple_of(n * tile, tile), tile)
+        grad_mixed[:, at] = dot_nt(first_low[...], wo[at, :]).astype(BF)
+        return carry
+
+    lax.fori_loop(0, width // tile, open_, 0)
+
+    def pair(j, carry):
+        at = pl.ds(pl.multiple_of(j * 2 * HEAD, 2 * HEAD), 2 * HEAD)
+        q, k, v, grad = q_in[:, at], k_in[:, at], v_in[:, at], grad_mixed[:, at]
+        turned = k.T
+        lane = lax.broadcasted_iota(jnp.int32, k.shape, 1)
+        parts = []
+        grad_k = jnp.zeros(k.shape, F32)
+        grad_v = jnp.zeros(k.shape, F32)
+        for side in range(2):
+            mine = (lane >= HEAD) if side else (lane < HEAD)
+            none = jnp.zeros_like(k)
+            probs = probs_in[0, 2 * j + side]
+            grad_probs = dot_nt(jnp.where(mine, v, none), grad)
+            grad_v = grad_v + dot_nn(probs, jnp.where(mine, grad, none))
+            wide = probs.astype(F32)
+            both = wide * grad_probs
+            scores = (both - wide * jnp.sum(both, 0, keepdims=True)).astype(BF)
+            grad_k = grad_k + dot_nn(scores, jnp.where(mine, q, none))
+            parts.append(dot_nn(turned[side * HEAD : (side + 1) * HEAD], scores))
+        grad_q = jnp.concatenate(parts, 0).T * HEAD**-0.5
+        dq[:, at] = grad_q.astype(BF)
+        dk[:, at] = grad_k.astype(BF)
+        dv[:, at] = grad_v.astype(BF)
+        sums[0:1, at] += column_sum(grad_q)
+        sums[1:2, at] += column_sum(grad_v)
+        return carry
+
+    lax.fori_loop(0, HEADS // 2, pair, 0)
+
+    def close(n, carry):
+        at = pl.ds(pl.multiple_of(n * tile, tile), tile)
+        total[:, at] = (
+            grad_first[:, at]
+            + dot_nt(dq[...], wq[at, :])
+            + dot_nt(dk[...], wk[at, :])
+            + dot_nt(dv[...], wv[at, :])
+        )
+        return carry
+
+    lax.fori_loop(0, width // tile, close, 0)
+    rows = 128
+
+    def last(n, carry):
+        at = pl.ds(pl.multiple_of(n * rows, rows), rows)
+        unit, inverse = stats(embedded[at, :])
+        grad = total[at, :]
+        grad_emb = norm_back(grad, emb_gain[...], unit, inverse)
+        emb_low[at, :] = grad_emb.astype(BF)
+        sums[2:3, :] += column_sum(grad * unit)
+        sums[3:4, :] += column_sum(grad)
+        kind = kinds[at, :]
+        for t in range(2):
+            sums[4 + t : 5 + t, :] += column_sum(jnp.where(kind == t, grad_emb, 0.0))
+        return carry
+
+    lax.fori_loop(0, tokens // rows, last, 0)
+
+
+def attend_back(grad_first, embedded, kinds, q, k, v, probs, wq, wk, wv, wo, emb_gain):
+    tokens, width = grad_first.shape
+    seqs, _, size, _ = probs.shape
+    part = rows_of(size, width)
+    low = jax.ShapeDtypeStruct((tokens, width), BF)
+    return pl.pallas_call(
+        attend_back_kernel,
+        grid=(seqs,),
+        in_specs=[part, part, rows_of(size, 1)]
+        + [part] * 3
+        + [pl.BlockSpec((1, HEADS, size, size), lambda i: (i, 0, 0, 0))]
+        + [fixed((width, width))] * 4
+        + [fixed((1, width))],
+        out_specs=[part] * 5 + [fixed((8, width))],
+        out_shape=[low] * 5 + [jax.ShapeDtypeStruct((8, width), F32)],
+        scratch_shapes=[pltpu.VMEM((size, width), BF), pltpu.VMEM((size, width), F32)],
+        compiler_params=pltpu.CompilerParams(vmem_limit_bytes=60 * MIB),
+        cost_estimate=pl.CostEstimate(flops=30 * 10**9, bytes_accessed=40 * 10**6, transcendentals=0),
+        name="attend_back",
+    )(grad_first, embedded, kinds.reshape(tokens, 1), q, k, v, probs, wq, wk, wv, wo, row(emb_gain))
+
+
+MESH = pl.DeviceIdType.MESH
 
 
 def flipped(index, bits):
@@ -639,72 +914,46 @@
         + pos_table.astype(jnp.float32)[None]
         + type_rows
     )
-    normed = layer_norm(embedded, emb_gain, emb_bias).reshape(tokens, width)
-    normed_low = normed.astype(jnp.bfloat16)
-    query = (matmul(normed_low, query_weight) + query_bias).astype(jnp.bfloat16)
-    keys = matmul(normed_low, key_weight).astype(jnp.bfloat16)
-    values = (matmul(normed_low, value_weight) + value_bias).astype(jnp.bfloat16)
-    split_shape = (seq_count, seq_len, HEADS, HEAD)
-    query_split = query.reshape(split_shape)
-    keys_split = keys.reshape(split_shape)
-    values_split = values.reshape(split_shape)
-    mixed, logsum = lax.map(attend_forward, (query_split, keys_split, values_split, lengths))
-    mixed_low = mixed.reshape(tokens, width)
-    first = normed + matmul(mixed_low, out_weight) + out_bias
-    hidden = layer_norm(first, attn_gain, attn_bias)
-    hidden_reduced_precision = hidden.astype(jnp.bfloat16)
-    upper = matmul(hidden_reduced_precision, up_weight) + up_bias
-    active_low = jax.nn.gelu(upper, approximate=False).astype(jnp.bfloat16)
-    second = hidden + matmul(active_low, down_weight) + down_bias
-    encoded = layer_norm(second, final_gain, final_bias)
-    grad_out = cotangent.reshape(tokens, width).astype(jnp.float32)
-    _, final_pull = jax.vjp(layer_norm, second, final_gain, final_bias)
-    grad_second, grad_final_gain, grad_final_bias = final_pull(grad_out)
-    grad_down_bias = jnp.sum(grad_second, 0)
-    second_matmul_gradient_reduced = grad_second.astype(jnp.bfloat16)
-    grad_down = matmul_tn(active_low, second_matmul_gradient_reduced)
-    grad_active = matmul_nt(second_matmul_gradient_reduced, down_weight)
-    _, gelu_pull = jax.vjp(partial(jax.nn.gelu, approximate=False), upper)
-    (grad_upper,) = gelu_pull(grad_active)
-    grad_up_bias = jnp.sum(grad_upper, 0)
-    grad_upper_low = grad_upper.astype(jnp.bfloat16)
-    grad_up = matmul_tn(hidden_reduced_precision, grad_upper_low)
-    grad_hidden = grad_second + matmul_nt(grad_upper_low, up_weight)
-    _, attn_pull = jax.vjp(layer_norm, first, attn_gain, attn_bias)
-    grad_first, grad_attn_gain, grad_attn_bias = attn_pull(grad_hidden)
-    grad_out_bias = jnp.sum(grad_first, 0)
-    grad_first_low = grad_first.astype(jnp.bfloat16)
-    grad_out_weight = matmul_tn(mixed_low, grad_first_low)
-    grad_mixed = matmul_nt(grad_first_low, out_weight).astype(jnp.bfloat16)
-    grad_query, grad_keys, grad_values = lax.map(
-        attend_backward,
-        (query_split, keys_split, values_split, grad_mixed.reshape(split_shape), logsum, lengths),
-    )
-    grad_query = grad_query.reshape(tokens, width)
-    grad_keys = grad_keys.reshape(tokens, width)
-    grad_values = grad_values.reshape(tokens, width)
-    grad_query_bias = jnp.sum(grad_query, 0)
-    grad_value_bias = jnp.sum(grad_values, 0)
-    grad_query_low = grad_query.astype(jnp.bfloat16)
-    grad_keys_low = grad_keys.astype(jnp.bfloat16)
-    grad_values_low = grad_values.astype(jnp.bfloat16)
-    grad_query_weight = matmul_tn(normed_low, grad_query_low)
-    grad_key_weight = matmul_tn(normed_low, grad_keys_low)
-    grad_value_weight = matmul_tn(normed_low, grad_values_low)
-    grad_normed = (
-        grad_first
-        + matmul_nt(grad_query_low, query_weight)
-        + matmul_nt(grad_keys_low, key_weight)
-        + matmul_nt(grad_values_low, value_weight)
-    )
-    _, emb_pull = jax.vjp(layer_norm, embedded, emb_gain, emb_bias)
-    embedding_output_gradient, grad_emb_gain, grad_emb_bias = emb_pull(
-        grad_normed.reshape(seq_count, seq_len, width)
-    )
-    grad_pos = jnp.sum(embedding_output_gradient, 0)
-    token_type_gradient = jnp.einsum(
-        "nox,noh->xh", selection_matrix, embedding_output_gradient, precision=lax.Precision.HIGHEST
-    )
+    embedded = embedded.reshape(tokens, width)
+    normed = layer_norm(embedded, emb_gain, emb_bias)
+    normed_low, query, keys, values, mixed_low, first, probs = attend(
+        lengths, normed, query_weight, key_weight, value_weight, out_weight, query_bias, value_bias, out_bias
+    )
+    encoded, active_low, grad_second_low, hidden_low, grad_upper_low, grad_first, sums, grad_up_bias = feed(
+        first,
+        cotangent.reshape(tokens, width),
+        up_weight,
+        down_weight,
+        up_bias,
+        down_bias,
+        attn_gain,
+        attn_bias,
+        final_gain,
+        final_bias,
+    )
+    grad_final_gain, grad_final_bias, grad_down_bias, grad_attn_gain, grad_attn_bias, grad_out_bias = [
+        sums[i] for i in range(6)
+    ]
+    grad_up_bias = grad_up_bias[0]
+    grad_down = matmul_tn(active_low, grad_second_low)
+    grad_up = matmul_tn(hidden_low, grad_upper_low)
+    grad_first_low, grad_query_low, grad_keys_low, grad_values_low, embedding_output_gradient, sums = attend_back(
+        grad_first,
+        embedded,
+        type_ids,
+        query,
+        keys,
+        values,
+        probs,
+        query_weight,
+        key_weight,
+        value_weight,
+        out_weight,
+        emb_gain,
+    )
+    grad_query_bias, grad_value_bias, grad_emb_gain, grad_emb_bias = [sums[i] for i in range(4)]
+    token_type_gradient = sums[4:6]
+    grad_pos = jnp.sum(embedding_output_gradient.astype(jnp.float32).reshape(seq_count, seq_len, width), 0)
     bf = jnp.bfloat16
     per = width // owners
     grad_down_all = sum_over_all(grad_down.astype(bf))
@@ -776,6 +1025,10 @@
         lines = (seq_len // owners) * width // wide
         rest = per // 3 - lines
         small_lines = jnp.pad(small, ((0, 0), (0, rest * wide - 16 * per))).reshape(owners, rest, wide)
+        grad_query_weight, grad_key_weight, grad_value_weight = [
+            matmul_tn(normed_low, g) for g in (grad_query_low, grad_keys_low, grad_values_low)
+        ]
+        grad_out_weight = matmul_tn(mixed_low, grad_first_low)
         mixed_grads = jnp.concatenate(
             [grad_query_weight, grad_key_weight, grad_value_weight, grad_out_weight], 1
         ).astype(bf)

time: 659 us -> 511 us (0.78)
  matrix products: 160 us -> 16.5 us
  Pallas kernels: 157 us -> 271 us
  local copies, waits for them, and re-layouts: 107 us -> 42.1 us
  other arithmetic: 78.5 us -> 32.8 us
  waiting for transfers between devices: 107 us -> 100 us
    dot_general x27 -> x0, matrix products: 140 us -> none  [the longest x6 50.2 us: matmul(): return jnp.dot(left, right, preferred_element_type=jnp.float32)]
    pallas_call x0 -> x3, Pallas kernels: none -> 114 us  [the longest x1 42.3 us: feed(): pl.pallas_call(feed_kernel, grid=(tokens // tile,), in_specs=[part, part,...]
    reduce_sum x11 -> x0, other arithmetic: 22.4 us -> none  [the longest x3 6.39 us: layer_norm(): center = values - jnp.mean(values, -1, keepdims=True)]
    convert_element_type x10 -> x0, local copies, waits for them, and re-layouts: 19.5 us -> none  [the longest x2 4.34 us: local(): grad_keys_low = grad_keys.astype(jnp.bfloat16)]
    convert_element_type x4 -> x0, other arithmetic: 18.3 us -> none  [the longest x2 14.8 us: attend_backward(): grad_scores = (probs * (grad_probs - inner)).astype(jnp.bfloat16)]
    while x37 -> x0, local copies, waits for them, and re-layouts: 17.3 us -> none  [the longest x4 11.5 us: local(): lax.map(attend_forward, (query_split, keys_split, values_split, lengths))]
    reshape x9 -> x8, local copies, waits for them, and re-layouts: 14.9 us -> 4.68 us  [row(): return vector.reshape(1, -1)]
    unnamed x168 -> x60, local copies, waits for them, and re-layouts: 13.8 us -> 4.48 us
  transfers between devices with their start and end apart: 25 -> 25, of which waited for: 10 -> 10; matrix products, arithmetic and copies ran while one was open for 5% -> 8% of each run, Pallas kernels for 24% -> 39%
where the time goes in v3:
time: 511 us; the launch traced here: 504 us
  Pallas kernels  271 us (53%)
  waiting for transfers between devices  100 us (20%)
  local copies, waits for them, and re-layouts  42.1 us (8%)
  other arithmetic  32.8 us (6%)
  starting transfers between devices  28.5 us (6%)
  matrix products  16.5 us (3%)
  blocking collectives  11.7 us (2%)
    pallas_call x1, Pallas kernels, tail(): pl.pallas_call(tail_kernel, out_shape=(jax.ShapeDtypeStruct((2, 2, 2, par...  157 us
    all_to_all x1, waiting for transfers between devices, local(): lax.all_to_all(found, 'vocab', split_axis=0, concat_axis=0, tiled=True)  61.9 us
    pallas_call x1, Pallas kernels, feed(): pl.pallas_call(feed_kernel, grid=(tokens // tile,), in_specs=[part, part,...  42.3 us
    pallas_call x1, Pallas kernels, attend_back(): pl.pallas_call(attend_back_kernel, grid=(seqs,), in_specs=[part, part, ro...  39.6 us
    pallas_call x1, Pallas kernels, attend(): pl.pallas_call(attend_kernel, grid_spec=pltpu.PrefetchScalarGridSpec(num_...  32 us
    ppermute x18, waiting for transfers between devices, swap(): return lax.ppermute(value, axis_name, [(i, i ^ bit) for i in range(size)])  25.6 us
    ppermute x18, starting transfers between devices, swap(): return lax.ppermute(value, axis_name, [(i, i ^ bit) for i in range(size)])  17.6 us
    dot_general x2, matrix products, matmul_tn(): lax.dot_general(left, right, (((0,), (0,)), ((), ())), preferred_element_...  13.7 us
  transfers between devices with their start and end apart: 25, of which 10 were waited for; matrix products, arithmetic and copies ran while one was open for 8% of the time, Pallas kernels for 39%

profile of v3, /device:TPU:0, one launch (start us, length us, event | category | flops | bytes accessed | tf_op | source)
XLA Modules:
  0.0 504.3 jit_solution(4132573098651586683)
XLA Ops:
  3.5 2.3 reduce-window.6
  7.1 4.3 scatter_custom_fusion
  11.4 11.7 %all_to_all.14 = s32[8,1,256]{2,1,0:T(1,128)S(1)} all-to-all(s32[8,1,256]{2,1,0:T(1,128)S(1)} %bitcast.251), channel_id=1, replica_groups=mesh['dp'=4,'vocab'=8] {'vocab'}, dimensions={0} | all-to-all | bytes 16384 | tf_op jit(solution)/shard_map/all_to_all | solution.py:898
  23.2 11.9 %gather_fusion = bf16[2048,768]{1,0:T(8,128)(2,1)S(1)} fusion(bf16[3840,768]{1,0:T(8,128)(2,1)} %param.27, s32[2048]{0:T(1024)S(1)} %broadcast_clamp_fusion), kind=kCustom, calls=%fused_computation | custom fusion | bytes 6299648 | tf_op jit(solution)/shard_map/gather | solution.py:900
  35.1 1.9 broadcast_select_fusion
  37.0 3.7 all-to-all-start.1
  40.9 2.4 convert_element_type.208
  50.2 61.9 %all-to-all-done.1 = bf16[8,256,768]{2,1,0:T(8,128)(2,1)S(1)} async-done(((bf16[8,256,768]{2,1,0:T(8,128)(2,1)}), bf16[8,256,768]{2,1,0:T(8,128)(2,1)S(1)}, u32[]{:S(2)}, u32[]{:S(2)}) %all-to-all-start.1) | async-done | bytes 3145760 | tf_op jit(solution)/shard_map/all_to_all | solution.py:902
  112.1 5.2 %gather_fusion.1 = bf16[1024,768]{1,0:T(8,128)(2,1)} fusion(bf16[2048,768]{1,0:T(8,128)(2,1)S(1)} %bitcast.219, s32[1024]{0:T(1024)S(1)} %broadcast_clamp_fusion.1), kind=kCustom, calls=%fused_computation.1 | custom fusion | bytes 3149824 | tf_op jit(solution)/shard_map/gather | solution.py:903
  117.3 2.7 fusion.55
  120.8 2.2 multiply_add_fusion.normed
  123.0 32.0 %attend.1 = (bf16[1024,768]{1,0:T(8,128)(2,1)}, bf16[1024,768]{1,0:T(8,128)(2,1)}, bf16[1024,768]{1,0:T(8,128)(2,1)}, bf16[1024,768]{1,0:T(8,128)(2,1)}, bf16[10...) custom-call(s32[2]{0:T(128)} %lengths.1, f32[1024,768]{1,0:T(8,128)} %multiply_add_fusion.normed, ...), custom_call_target="tpu_custom_call" | custom-call | flops 20000000000 | bytes 30000000 | tf_op jit(solution)/shard_map/attend/pallas_call | solution.py:254
  154.9 42.3 %feed.1 = (f32[1024,768]{1,0:T(8,128)}, bf16[1024,3072]{1,0:T(8,128)(2,1)}, bf16[1024,768]{1,0:T(8,128)(2,1)}, bf16[1024,768]{1,0:T(8,128)(2,1)}, bf16[1024,3072...) custom-call(f32[1024,768]{1,0:T(8,128)} %get-tuple-element.44.first, ...), custom_call_target="tpu_custom_call" | custom-call | flops 40000000000 | bytes 40000000 | tf_op jit(solution)/shard_map/feed/pallas_call | solution.py:324
  197.3 7.9 %convolution_convert_fusion = bf16[3072,768]{1,0:T(8,128)(2,1)S(1)} fusion(bf16[1024,3072]{1,0:T(8,128)(2,1)} %get-tuple-element.65, bf16[1024,768]{1,0:T(8,128)(2,1)} %get-tuple-element.66), kind=kOutput, calls=%fused_computation.4 | convolution fusion | flops 4834197504 | bytes 12582912 | tf_op jit(solution)/shard_map/dot_general | solution.py:29
  205.2 1.5 dynamic-slice_bitcast_fusion
  208.0 5.9 %convolution_convert_fusion.1 = bf16[768,3072]{1,0:T(8,128)(2,1)S(1)} fusion(bf16[1024,768]{1,0:T(8,128)(2,1)S(1)} %copy-done.20, bf16[1024,3072]{1,0:T(8,128)(2,1)S(1)} %copy-done.19), kind=kOutput, calls=%fused_computation.5 | convolution fusion | flops 4834197504 | bytes 12582912 | tf_op jit(solution)/shard_map/dot_general | solution.py:29
  213.9 1.7 dynamic-slice_bitcast_fusion.1
  217.2 39.6 %attend_back.1 = (bf16[1024,768]{1,0:T(8,128)(2,1)}, bf16[1024,768]{1,0:T(8,128)(2,1)}, bf16[1024,768]{1,0:T(8,128)(2,1)}, bf16[1024,768]{1,0:T(8,128)(2,1)}, bf...) custom-call(f32[1024,768]{1,0:T(8,128)} %get-tuple-element.46.grad_first, f32[1024,768]{1,0:T(8,128)} %bitcast.220, ...), custom_call_target="tpu_custom_call" | custom-call | flops 30000001024 | bytes 40000000 | tf_op jit(solution)/shard_map/attend_back/pallas_call | solution.py:433
  260.4 156.9 %tail.1 = (bf16[2,2,2,480,768]{4,3,2,1,0:T(8,128)(2,1)}, bf16[2,2,32,3072]{3,2,1,0:T(8,128)(2,1)}) custom-call(bf16[1024,768]{1,0:T(8,128)(2,1)} %get-tuple-element.51.demb, s32[1,1024]{1,0:T(1,128)} %fusion.42.slot, s32[1,2048]{1,0:T(1,128)} %bitcast.242, f32[16,768]{1,0:T(8,128)} %concatenate.15.small, bf16[1024,768]{1,0:T(8,128)(2,1)} %get-tuple-element.55.normed, ...), custom_call_target="tpu_custom_call" | custom-call | tf_op jit(solution)/shard_map/tail/pallas_call | solution.py:812
  419.6 8.8 %bitcast_convert_fusion = f32[3840,768]{1,0:T(8,128)} fusion(bf16[2,2,2,480,768]{4,3,2,1,0:T(8,128)(2,1)} %get-tuple-element.61), kind=kLoop, calls=%fused_computation.3 | loop fusion | flops 2949120 | bytes 17694720 | tf_op jit(solution)/shard_map/convert_element_type | solution.py:993
  428.4 2.4 fusion
  433.5 2.6 fusion.1
  438.7 8.8 %collective-permute-done.15 = bf16[2,2,96,768]{3,2,0,1:T(8,128)(2,1)S(1)} collective-permute-done((bf16[2,2,96,768]{3,2,0,1:T(8,128)(2,1)S(1)}, bf16[2,2,96,768]{3,2,0,1:T(8,128)(2,1)S(1)}, u32[]{:S(2)}, u32[]{:S(2)}) %collective-permute-start.15) | collective-permute-done | bytes 589856 | tf_op jit(solution)/shard_map/ppermute | solution.py:42
  450.0 10.1 %collective-permute-done.3 = bf16[2,2,24,3072]{3,2,0,1:T(8,128)(2,1)S(1)} collective-permute-done((bf16[2,2,24,3072]{3,2,0,1:T(8,128)(2,1)S(1)}, bf16[2,2,24,3072]{3,2,0,1:T(8,128)(2,1)S(1)}, u32[]{:S(2)}, u32[]{:S(2)}) %collective-permute-start.3) | collective-permute-done | bytes 589856 | tf_op jit(solution)/shard_map/ppermute | solution.py:42
  462.7 5.1 %collective-permute-done.16 = bf16[2,96,768]{2,1,0:T(8,128)(2,1)S(1)} collective-permute-done((bf16[2,96,768]{2,1,0:T(8,128)(2,1)S(1)}, bf16[2,96,768]{2,1,0:T(8,128)(2,1)S(1)}, u32[]{:S(2)}, u32[]{:S(2)}) %collective-permute-start.16) | collective-permute-done | bytes 294944 | tf_op jit(solution)/shard_map/ppermute | solution.py:42
  469.1 2.3 collective-permute-start.18
  475.0 2.0 collective-permute-done.17
  477.8 5.4 %collective-permute-done.18 = bf16[96,768]{1,0:T(8,128)(2,1)S(1)} collective-permute-done((bf16[96,768]{1,0:T(8,128)(2,1)S(1)}, bf16[96,768]{1,0:T(8,128)(2,1)S(1)}, u32[]{:S(2)}, u32[]{:S(2)}) %collective-permute-start.18) | collective-permute-done | bytes 147488 | tf_op jit(solution)/shard_map/ppermute | solution.py:96
  483.9 1.5 collective-permute-start.22
  485.4 5.3 %collective-permute-done.6 = bf16[24,3072]{1,0:T(8,128)(2,1)S(1)} collective-permute-done((bf16[24,3072]{1,0:T(8,128)(2,1)S(1)}, bf16[24,3072]{1,0:T(8,128)(2,1)S(1)}, u32[]{:S(2)}, u32[]{:S(2)}) %collective-permute-start.6) | collective-permute-done | bytes 147488 | tf_op jit(solution)/shard_map/ppermute | solution.py:96
  496.2 1.6 collective-permute-start.23
  498.4 1.6 collective-permute-start.11
  (186 shorter events, 47.1 us)
Async XLA Ops:
  0.7 116.7 %copy-start = (bf16[2,768]{1,0:T(2,128)(2,1)S(1)}, bf16[2,768]{1,0:T(2,128)(2,1)}, u32[]{:S(2)}) copy-start(bf16[2,768]{1,0:T(2,128)(2,1)} %param.29) | copy-start | bytes 9220
  23.2 11.9 %copy-start.5 = (s32[8,1,256]{2,1,0:T(1,128)}, s32[8,1,256]{2,1,0:T(1,128)S(1)}, u32[]{:S(2)}) copy-start(s32[8,1,256]{2,1,0:T(1,128)S(1)} %all_to_all.14) | copy-start | bytes 24580
  37.0 75.1 %all-to-all-start.1 = ((bf16[8,256,768]{2,1,0:T(8,128)(2,1)}), bf16[8,256,768]{2,1,0:T(8,128)(2,1)S(1)}, u32[]{:S(2)}, u32[]{:S(2)}) async-start(bf16[8,256,768]{2,1,0:T(8,128)(2,1)} %broadcast_select_fusion), calls=%async_computation.1 | async-start | bytes 6291456 | tf_op jit(solution)/shard_map/all_to_all | solution.py:902
  40.8 8.2 %copy-start.6 = (f32[768]{0:T(1024)S(1)}, f32[768]{0:T(1024)}, u32[]{:S(2)}) copy-start(f32[768]{0:T(1024)} %param.30) | copy-start | bytes 9220
  197.3 10.8 %copy-start.19 = (bf16[1024,3072]{1,0:T(8,128)(2,1)S(1)}, bf16[1024,3072]{1,0:T(8,128)(2,1)}, u32[]{:S(2)}) copy-start(bf16[1024,3072]{1,0:T(8,128)(2,1)} %get-tuple-element.64) | copy-start | bytes 18874372
  208.0 220.4 %collective-permute-start.12 = (bf16[4,384,768]{2,1,0:T(8,128)(2,1)}, bf16[4,384,768]{2,1,0:T(8,128)(2,1)}, u32[]{:S(2)}, u32[]{:S(2)}) collective-permute-start(bf16[4,384,768]{2,1,0:T(8,128)(2,1)} %dynamic-slice_bitcast_fusion), channel_id=1, source_target_pairs={{0,1},{1,0},{2,3},{3,2},{4,5},{5,4},{6,7},{7,6},{8,9},{9,8},{10,11... | collective-permute-start | bytes 7077896 | tf_op jit(solution)/shard_map/ppermute | solution.py:42
  216.7 216.8 %collective-permute-start = (bf16[4,96,3072]{2,1,0:T(8,128)(2,1)}, bf16[4,96,3072]{2,1,0:T(8,128)(2,1)}, u32[]{:S(2)}, u32[]{:S(2)}) collective-permute-start(bf16[4,96,3072]{2,1,0:T(8,128)(2,1)} %dynamic-slice_bitcast_fusion.1), channel_id=1, source_target_pairs={{0,1},{1,0},{2,3},{3,2},{4,5},{5,4},{6,7},{7,6},{8,9},{9,8},{10,11... | collective-permute-start | bytes 7077896 | tf_op jit(solution)/shard_map/ppermute | solution.py:42
  217.2 41.0 %copy-start.9 = (f32[1,3072]{1,0:T(1,128)S(1)}, f32[1,3072]{1,0:T(1,128)}, u32[]{:S(2)}) copy-start(f32[1,3072]{1,0:T(1,128)} %get-tuple-element.54) | copy-start | bytes 36868
  418.6 9.8 %slice-start.2 = ((s8[4718592]{0:T(1024)(128)(4,1)}), s8[4194304]{0:T(1024)(128)(4,1)S(1)}, s32[]{:S(2)}) async-start(s8[4718592]{0:T(1024)(128)(4,1)} %bitcast.228), calls=%async_computation.4 | async-start | bytes 8388608
  419.6 8.8 %slice-start.3 = ((s8[4718592]{0:T(1024)(128)(4,1)}), s8[524288]{0:T(1024)(128)(4,1)S(1)}, s32[]{:S(2)}) async-start(s8[4718592]{0:T(1024)(128)(4,1)} %bitcast.228), calls=%async_computation.5 | async-start | bytes 1048576
  431.2 16.3 %collective-permute-start.15 = (bf16[2,2,96,768]{3,2,0,1:T(8,128)(2,1)S(1)}, bf16[2,2,96,768]{3,2,0,1:T(8,128)(2,1)S(1)}, u32[]{:S(2)}, u32[]{:S(2)}) collective-permute-start(bf16[2,2,96,768]{3,2,0,1:T(8,128)(2,1)S(1)} %bitcast.237), channel_id=1, source_target_pairs={{0,16},{8,24},{16,0},{24,8},{1,17},{9,25},{17,1},{25,9},{2,18},{10... | collective-permute-start | bytes 1769480 | tf_op jit(solution)/shard_map/ppermute | solution.py:42
  432.5 16.4 %collective-permute-start.13 = (bf16[2,2,96,768]{3,2,0,1:T(8,128)(2,1)S(1)}, bf16[2,2,96,768]{3,2,0,1:T(8,128)(2,1)S(1)}, u32[]{:S(2)}, u32[]{:S(2)}) collective-permute-start(bf16[2,2,96,768]{3,2,0,1:T(8,128)(2,1)S(1)} %bitcast.236), channel_id=1, source_target_pairs={{0,8},{8,0},{16,24},{24,16},{1,9},{9,1},{17,25},{25,17},{2,10},{10... | collective-permute-start | bytes 1769480 | tf_op jit(solution)/shard_map/ppermute | solution.py:42
  436.4 23.8 %collective-permute-start.3 = (bf16[2,2,24,3072]{3,2,0,1:T(8,128)(2,1)S(1)}, bf16[2,2,24,3072]{3,2,0,1:T(8,128)(2,1)S(1)}, u32[]{:S(2)}, u32[]{:S(2)}) collective-permute-start(bf16[2,2,24,3072]{3,2,0,1:T(8,128)(2,1)S(1)} %bitcast.239), channel_id=1, source_target_pairs={{0,16},{8,24},{16,0},{24,8},{1,17},{9,25},{17,1},{25,9},{2,18},{10... | collective-permute-start | bytes 1769480 | tf_op jit(solution)/shard_map/ppermute | solution.py:42
  437.7 23.8 %collective-permute-start.1 = (bf16[2,2,24,3072]{3,2,0,1:T(8,128)(2,1)S(1)}, bf16[2,2,24,3072]{3,2,0,1:T(8,128)(2,1)S(1)}, u32[]{:S(2)}, u32[]{:S(2)}) collective-permute-start(bf16[2,2,24,3072]{3,2,0,1:T(8,128)(2,1)S(1)} %bitcast.238), channel_id=1, source_target_pairs={{0,8},{8,0},{16,24},{24,16},{1,9},{9,1},{17,25},{25,17},{2,10},{10... | collective-permute-start | bytes 1769480 | tf_op jit(solution)/shard_map/ppermute | solution.py:42
  447.7 20.1 %collective-permute-start.16 = (bf16[2,96,768]{2,1,0:T(8,128)(2,1)S(1)}, bf16[2,96,768]{2,1,0:T(8,128)(2,1)S(1)}, u32[]{:S(2)}, u32[]{:S(2)}) collective-permute-start(bf16[2,96,768]{2,1,0:T(8,128)(2,1)S(1)} %dynamic-slice_bitcast_fusion.2), channel_id=1, source_target_pairs={{0,8},{8,0},{16,24},{24,16},{1,9},{9,1},{17,25},{25,17},{2,10},{10... | collective-permute-start | bytes 884744 | tf_op jit(solution)/shard_map/ppermute | solution.py:42
  449.1 18.8 %collective-permute-start.14 = (bf16[2,96,768]{2,1,0:T(8,128)(2,1)S(1)}, bf16[2,96,768]{2,1,0:T(8,128)(2,1)S(1)}, u32[]{:S(2)}, u32[]{:S(2)}) collective-permute-start(bf16[2,96,768]{2,1,0:T(8,128)(2,1)S(1)} %dynamic-slice_bitcast_fusion.3), channel_id=1, source_target_pairs={{0,16},{8,24},{16,0},{24,8},{1,17},{9,25},{17,1},{25,9},{2,18},{10... | collective-permute-start | bytes 884744 | tf_op jit(solution)/shard_map/ppermute | solution.py:42
  460.3 12.6 %collective-permute-start.4 = (bf16[2,24,3072]{2,1,0:T(8,128)(2,1)S(1)}, bf16[2,24,3072]{2,1,0:T(8,128)(2,1)S(1)}, u32[]{:S(2)}, u32[]{:S(2)}) collective-permute-start(bf16[2,24,3072]{2,1,0:T(8,128)(2,1)S(1)} %dynamic-slice_bitcast_fusion.4), channel_id=1, source_target_pairs={{0,8},{8,0},{16,24},{24,16},{1,9},{9,1},{17,25},{25,17},{2,10},{10... | collective-permute-start | bytes 884744 | tf_op jit(solution)/shard_map/ppermute | solution.py:42
  461.7 11.2 %collective-permute-start.2 = (bf16[2,24,3072]{2,1,0:T(8,128)(2,1)S(1)}, bf16[2,24,3072]{2,1,0:T(8,128)(2,1)S(1)}, u32[]{:S(2)}, u32[]{:S(2)}) collective-permute-start(bf16[2,24,3072]{2,1,0:T(8,128)(2,1)S(1)} %dynamic-slice_bitcast_fusion.5), channel_id=1, source_target_pairs={{0,16},{8,24},{16,0},{24,8},{1,17},{9,25},{17,1},{25,9},{2,18},{10... | collective-permute-start | bytes 884744 | tf_op jit(solution)/shard_map/ppermute | solution.py:42
  468.2 8.7 %collective-permute-start.17 = (bf16[96,768]{1,0:T(8,128)(2,1)S(1)}, bf16[96,768]{1,0:T(8,128)(2,1)S(1)}, u32[]{:S(2)}, u32[]{:S(2)}) collective-permute-start(bf16[96,768]{1,0:T(8,128)(2,1)S(1)} %get-tuple-element.97), channel_id=1, source_target_pairs={{0,2},{1,3},{2,4},{3,5},{4,6},{5,7},{6,0},{7,1},{8,10},{9,11},{10,... | collective-permute-start | bytes 442376 | tf_op jit(solution)/shard_map/ppermute | solution.py:96
  469.1 14.1 %collective-permute-start.18 = (bf16[96,768]{1,0:T(8,128)(2,1)S(1)}, bf16[96,768]{1,0:T(8,128)(2,1)S(1)}, u32[]{:S(2)}, u32[]{:S(2)}) collective-permute-start(bf16[96,768]{1,0:T(8,128)(2,1)S(1)} %get-tuple-element.98), channel_id=1, source_target_pairs={{0,4},{1,5},{2,6},{3,7},{4,0},{5,1},{6,2},{7,3},{8,12},{9,13},{10,... | collective-permute-start | bytes 442376 | tf_op jit(solution)/shard_map/ppermute | solution.py:96
  471.4 11.8 %collective-permute-start.19 = (bf16[96,768]{1,0:T(8,128)(2,1)S(1)}, bf16[96,768]{1,0:T(8,128)(2,1)S(1)}, u32[]{:S(2)}, u32[]{:S(2)}) collective-permute-start(bf16[96,768]{1,0:T(8,128)(2,1)S(1)} %get-tuple-element.99), channel_id=1, source_target_pairs={{0,6},{1,7},{2,0},{3,1},{4,2},{5,3},{6,4},{7,5},{8,14},{9,15},{10,... | collective-permute-start | bytes 442376 | tf_op jit(solution)/shard_map/ppermute | solution.py:96
  473.3 12.2 %collective-permute-start.5 = (bf16[24,3072]{1,0:T(8,128)(2,1)S(1)}, bf16[24,3072]{1,0:T(8,128)(2,1)S(1)}, u32[]{:S(2)}, u32[]{:S(2)}) collective-permute-start(bf16[24,3072]{1,0:T(8,128)(2,1)S(1)} %get-tuple-element.104), channel_id=1, source_target_pairs={{0,2},{1,3},{2,4},{3,5},{4,6},{5,7},{6,0},{7,1},{8,10},{9,11},{10,... | collective-permute-start | bytes 442376 | tf_op jit(solution)/shard_map/ppermute | solution.py:96
  473.9 16.9 %collective-permute-start.6 = (bf16[24,3072]{1,0:T(8,128)(2,1)S(1)}, bf16[24,3072]{1,0:T(8,128)(2,1)S(1)}, u32[]{:S(2)}, u32[]{:S(2)}) collective-permute-start(bf16[24,3072]{1,0:T(8,128)(2,1)S(1)} %get-tuple-element.105), channel_id=1, source_target_pairs={{0,4},{1,5},{2,6},{3,7},{4,0},{5,1},{6,2},{7,3},{8,12},{9,13},{10,... | collective-permute-start | bytes 442376 | tf_op jit(solution)/shard_map/ppermute | solution.py:96
  476.9 13.8 %collective-permute-start.7 = (bf16[24,3072]{1,0:T(8,128)(2,1)S(1)}, bf16[24,3072]{1,0:T(8,128)(2,1)S(1)}, u32[]{:S(2)}, u32[]{:S(2)}) collective-permute-start(bf16[24,3072]{1,0:T(8,128)(2,1)S(1)} %get-tuple-element.106), channel_id=1, source_target_pairs={{0,6},{1,7},{2,0},{3,1},{4,2},{5,3},{6,4},{7,5},{8,14},{9,15},{10,... | collective-permute-start | bytes 442376 | tf_op jit(solution)/shard_map/ppermute | solution.py:96
  483.3 9.7 %collective-permute-start.20 = (bf16[96,768]{1,0:T(8,128)(2,1)S(1)}, bf16[96,768]{1,0:T(8,128)(2,1)S(1)}, u32[]{:S(2)}, u32[]{:S(2)}) collective-permute-start(bf16[96,768]{1,0:T(8,128)(2,1)S(1)} %fusion.13), channel_id=1, source_target_pairs={{0,8},{8,0},{16,24},{24,16},{1,9},{9,1},{17,25},{25,17},{2,10},{10... | collective-permute-start | bytes 442376 | tf_op jit(solution)/shard_map/ppermute | solution.py:42
  483.9 12.3 %collective-permute-start.22 = (bf16[96,768]{1,0:T(8,128)(2,1)S(1)}, bf16[96,768]{1,0:T(8,128)(2,1)S(1)}, u32[]{:S(2)}, u32[]{:S(2)}) collective-permute-start(bf16[96,768]{1,0:T(8,128)(2,1)S(1)} %fusion.13), channel_id=1, source_target_pairs={{0,16},{8,24},{16,0},{24,8},{1,17},{9,25},{17,1},{25,9},{2,18},{10... | collective-permute-start | bytes 442376 | tf_op jit(solution)/shard_map/ppermute | solution.py:42
  490.9 6.9 %collective-permute-start.8 = (bf16[24,3072]{1,0:T(8,128)(2,1)S(1)}, bf16[24,3072]{1,0:T(8,128)(2,1)S(1)}, u32[]{:S(2)}, u32[]{:S(2)}) collective-permute-start(bf16[24,3072]{1,0:T(8,128)(2,1)S(1)} %fusion.16), channel_id=1, source_target_pairs={{0,8},{8,0},{16,24},{24,16},{1,9},{9,1},{17,25},{25,17},{2,10},{10... | collective-permute-start | bytes 442376 | tf_op jit(solution)/shard_map/ppermute | solution.py:42
  491.5 6.9 %collective-permute-start.10 = (bf16[24,3072]{1,0:T(8,128)(2,1)S(1)}, bf16[24,3072]{1,0:T(8,128)(2,1)S(1)}, u32[]{:S(2)}, u32[]{:S(2)}) collective-permute-start(bf16[24,3072]{1,0:T(8,128)(2,1)S(1)} %fusion.16), channel_id=1, source_target_pairs={{0,16},{8,24},{16,0},{24,8},{1,17},{9,25},{17,1},{25,9},{2,18},{10... | collective-permute-start | bytes 442376 | tf_op jit(solution)/shard_map/ppermute | solution.py:42
  493.0 7.0 %collective-permute-start.21 = (bf16[96,384]{1,0:T(8,128)(2,1)S(1)}, bf16[96,384]{1,0:T(8,128)(2,1)S(1)}, u32[]{:S(2)}, u32[]{:S(2)}) collective-permute-start(bf16[96,384]{1,0:T(8,128)(2,1)S(1)} %slice.203), channel_id=1, source_target_pairs={{0,16},{8,24},{16,0},{24,8},{1,17},{9,25},{17,1},{25,9},{2,18},{10... | collective-permute-start | bytes 221192 | tf_op jit(solution)/shard_map/ppermute | solution.py:42
  496.2 4.4 collective-permute-start.23
  497.8 4.4 collective-permute-start.9
  498.4 4.4 collective-permute-start.11
  (18 other events, 70.4 us)

commit v4 on v3

--- a/solution.py
+++ b/solution.py
@@ -450,6 +450,382 @@
 MESH = pl.DeviceIdType.MESH
 
 
+def mid_kernel(
+    active, upper_low, second_low, hidden_low, grad_first, embedded, q_in, k_in, v_in, probs_in, wq, wk, wv, wo,
+    kinds, emb_gain,
+    first_out, dq_out, dk_out, dv_out, raw_out, pos_out, feed_out, sums,
+    stage, lhs, turned, grads, core_in, in_1a, in_1b, in_2a, in_2b, in_z, kept,
+    first, low, grad_mixed, q, k, v, dq, dk, dv, weights, table, raw, pos, probs,
+    load, stage_sem, probs_sem, out_sem, send, recv,
+):
+    tokens, width = lhs.shape
+    size = probs.shape[2]
+    seqs = tokens // size
+    per = grads.shape[3]
+    me = lax.axis_index("vocab")
+    spot = lax.axis_index("dp")
+    core, place = lax.rem(me, 2), lax.div(me, 2)
+    xb, yb = lax.rem(spot, 2), lax.div(spot, 2)
+    across_x = {"dp": spot + 1 - 2 * xb}
+    across_y = {"dp": spot + 2 - 4 * yb}
+    partner = {"vocab": me + 1 - 2 * core}
+    block = 768
+    blocks = active.shape[1] // block
+
+    def stage_copy(n):
+        source = active if n < blocks else upper_low
+        at = pl.ds((n % blocks) * block, block)
+        return pltpu.make_async_copy(source.at[:, at], stage.at[n % 2], stage_sem.at[n % 2])
+
+    def probs_copy(n):
+        return pltpu.make_async_copy(
+            probs_in.at[lax.div(n, HEADS // 2), pl.ds(2 * lax.rem(n, HEADS // 2), 2)],
+            probs.at[lax.rem(n, 2)],
+            probs_sem.at[lax.rem(n, 2)],
+        )
+
+    second_copy = pltpu.make_async_copy(second_low, lhs, load.at[0])
+    hidden_copy = pltpu.make_async_copy(hidden_low, lhs, load.at[1])
+    second_copy.start()
+    stage_copy(0).start()
+    stage_copy(1).start()
+    loads = [
+        pltpu.make_async_copy(source, target, load.at[2 + i])
+        for i, (source, target) in enumerate(
+            (
+                (grad_first, first),
+                (wo, weights.at[3]),
+                (q_in, q),
+                (k_in, k),
+                (v_in, v),
+                (wq, weights.at[0]),
+                (wk, weights.at[1]),
+                (wv, weights.at[2]),
+                (embedded, table),
+            )
+        )
+    ]
+    barrier = pltpu.get_barrier_semaphore()
+    places = [{"vocab": 2 * flipped(place, k) + core} for k in (1, 2, 3)]
+    for peer in [partner, across_x, across_y] + places:
+        pl.semaphore_signal(barrier, inc=1, device_id=peer, device_id_type=MESH)
+    pl.semaphore_wait(barrier, 6)
+
+    def remote(src, dst, at, peer):
+        return pltpu.make_async_remote_copy(
+            src_ref=src, dst_ref=dst, send_sem=send.at[at], recv_sem=recv.at[at], device_id=peer, device_id_type=MESH
+        )
+
+    def core_copy(g):
+        return remote(grads.at[g, :, 1 - core], core_in.at[g], 5 * g, partner)
+
+    half = 2 * width
+
+    def wide(b):
+        return pl.ds(pl.multiple_of(b * half, half), half)
+
+    def narrow(b, c):
+        return pl.ds(pl.multiple_of(b * half + c * width, width), width)
+
+    def first_copies(g):
+        return [
+            remote(grads.at[g, pl.ds(0, 2), core, :, wide(1 - xb)], in_1a.at[g], 5 * g + 1, across_x),
+            remote(grads.at[g, pl.ds(2, 2), core, :, wide(1 - yb)], in_1b.at[g], 5 * g + 2, across_y),
+        ]
+
+    def second_copies(g):
+        return [
+            remote(grads.at[g, pl.ds(0, 2), core, :, narrow(xb, 1 - yb)], in_2a.at[g], 5 * g + 3, across_y),
+            remote(grads.at[g, pl.ds(2, 2), core, :, narrow(yb, 1 - xb)], in_2b.at[g], 5 * g + 4, across_x),
+        ]
+
+    def add(view, value):
+        view[...] = (view[...].astype(F32) + value.astype(F32)).astype(BF)
+
+    def core_step(g):
+        core_copy(g).wait_recv()
+        rows = per // 2
+
+        def one(i, carry):
+            z = lax.div(i, 2)
+            at = pl.ds(pl.multiple_of(lax.rem(i, 2) * rows, rows), rows)
+            add(grads.at[g, z, core, at, :], core_in[g, z, at, :])
+            return carry
+
+        lax.fori_loop(0, 8, one, 0)
+        for copy in first_copies(g):
+            copy.start()
+
+    def first_step(g):
+        for copy in first_copies(g):
+            copy.wait_recv()
+
+        def one(z, carry):
+            add(grads.at[g, z, core, :, wide(xb)], in_1a[g, z])
+            add(grads.at[g, 2 + z, core, :, wide(yb)], in_1b[g, z])
+            return carry
+
+        lax.fori_loop(0, 2, one, 0)
+        for copy in second_copies(g):
+            copy.start()
+
+    def owned(g, z):
+        at = 2 * xb + yb + lax.div(z, 2) * (yb - xb)
+        return grads.at[g, z, core, :, pl.ds(pl.multiple_of(at * width, width), width)]
+
+    def place_copies(g):
+        return [
+            remote(owned(g, flipped(place, k)), in_z.at[g, k - 1], 10 + 3 * g + k - 1, places[k - 1]) for k in (3, 2, 1)
+        ]
+
+    def place_step(g):
+        for copy in place_copies(g):
+            copy.wait_recv()
+        total = owned(g, place)[...].astype(F32)
+        for k in range(3):
+            total = total + in_z[g, k].astype(F32)
+        kept[pl.ds(g * per, per), :] = total.astype(BF)
+
+    def second_step(g):
+        for copy in second_copies(g):
+            copy.wait_recv()
+        for z in range(2):
+            add(grads.at[g, z, core, :, narrow(xb, yb)], in_2a[g, z])
+            add(grads.at[g, 2 + z, core, :, narrow(yb, xb)], in_2b[g, z])
+        for copy in place_copies(g):
+            copy.start()
+
+    corner = 256
+
+    def turn():
+        def one(i, carry):
+            at = pl.ds(pl.multiple_of(i * corner, corner), corner)
+            for j in range(width // corner):
+                there = pl.ds(j * corner, corner)
+                turned[there, at] = lhs[at, there].T
+            return carry
+
+        lax.fori_loop(0, tokens // corner, one, 0)
+
+    second_copy.wait()
+    turn()
+    hidden_copy.start()
+    share = block // 2
+    for n in range(blocks):
+        stage_copy(n).wait()
+        for c in range(2):
+            out = dot_nn(turned[...], stage[n % 2, :, c * share : (c + 1) * share]).astype(BF)
+            for j in range(8):
+                grads[0, n, c, :, j * share : (j + 1) * share] = out[j * per : (j + 1) * per]
+        stage_copy(n + 2).start()
+        if n == 0:
+            for copy in loads[:5]:
+                copy.start()
+            probs_copy(0).start()
+    core_copy(0).start()
+    hidden_copy.wait()
+    turn()
+    for n in range(blocks, 2 * blocks):
+        stage_copy(n).wait()
+        for c in range(2):
+            out = dot_nn(turned[...], stage[n % 2, :, c * share : (c + 1) * share]).astype(BF)
+            at = (n - blocks) * block + c * share
+            for j in range(8):
+                grads[1, j // 2, j % 2, :, at : at + share] = out[j * per : (j + 1) * per]
+        if n + 2 < 2 * blocks:
+            stage_copy(n + 2).start()
+        if n == blocks:
+            for copy in loads[5:]:
+                copy.start()
+    core_copy(1).start()
+    core_step(0)
+
+    for copy in loads:
+        copy.wait()
+    sums[...] = jnp.zeros_like(sums)
+    low[...] = first[...].astype(BF)
+    first_copy = pltpu.make_async_copy(low, first_out, out_sem.at[4])
+    first_copy.start()
+    tile = 256
+
+    def open_(n, carry):
+        at = pl.ds(pl.multiple_of(n * tile, tile), tile)
+        grad_mixed[:, at] = dot_nt(low[...], weights[3, at, :]).astype(BF)
+        return carry
+
+    lax.fori_loop(0, width // tile, open_, 0)
+
+    def pair(n, carry):
+        @pl.when(n + 1 < seqs * (HEADS // 2))
+        def _():
+            probs_copy(n + 1).start()
+
+        probs_copy(n).wait()
+        slot = lax.rem(n, 2)
+        rows = pl.ds(pl.multiple_of(lax.div(n, HEADS // 2) * size, size), size)
+        at = pl.ds(pl.multiple_of(lax.rem(n, HEADS // 2) * 2 * HEAD, 2 * HEAD), 2 * HEAD)
+        q2, k2, v2, grad = q[rows, at], k[rows, at], v[rows, at], grad_mixed[rows, at]
+        across = k2.T
+        lane = lax.broadcasted_iota(jnp.int32, k2.shape, 1)
+        parts = []
+        grad_k = jnp.zeros(k2.shape, F32)
+        grad_v = jnp.zeros(k2.shape, F32)
+        for side in range(2):
+            mine = (lane >= HEAD) if side else (lane < HEAD)
+            none = jnp.zeros_like(k2)
+            chances = probs[slot, side]
+            grad_probs = dot_nt(jnp.where(mine, v2, none), grad)
+            grad_v = grad_v + dot_nn(chances, jnp.where(mine, grad, none))
+            full = chances.astype(F32)
+            both = full * grad_probs
+            scores = (both - full * jnp.sum(both, 0, keepdims=True)).astype(BF)
+            grad_k = grad_k + dot_nn(scores, jnp.where(mine, q2, none))
+            parts.append(dot_nn(across[side * HEAD : (side + 1) * HEAD], scores))
+        grad_q = jnp.concatenate(parts, 0).T * HEAD**-0.5
+        dq[rows, at] = grad_q.astype(BF)
+        dk[rows, at] = grad_k.astype(BF)
+        dv[rows, at] = grad_v.astype(BF)
+        sums[0:1, at] += column_sum(grad_q)
+        sums[1:2, at] += column_sum(grad_v)
+        return carry
+
+    lax.fori_loop(0, 2, pair, 0)
+    core_step(1)
+    lax.fori_loop(2, 5, pair, 0)
+    first_step(0)
+    lax.fori_loop(5, 8, pair, 0)
+    second_step(0)
+    first_step(1)
+    lax.fori_loop(8, 11, pair, 0)
+    second_step(1)
+    lax.fori_loop(11, 12, pair, 0)
+    out_copies = [
+        pltpu.make_async_copy(source, target, out_sem.at[5 + i])
+        for i, (source, target) in enumerate(((dq, dq_out), (dk, dk_out), (dv, dv_out)))
+    ]
+    for copy in out_copies:
+        copy.start()
+
+    def close(n, carry):
+        at = pl.ds(pl.multiple_of(n * tile, tile), tile)
+        first[:, at] = (
+            first[:, at]
+            + dot_nt(dq[...], weights[0, at, :])
+            + dot_nt(dk[...], weights[1, at, :])
+            + dot_nt(dv[...], weights[2, at, :])
+        )
+        return carry
+
+    lax.fori_loop(0, width // tile, close, 0)
+    few = 128
+    lane = lax.broadcasted_iota(jnp.int32, (few, 128), 1)
+
+    def back(at):
+        unit, inverse = stats(table[at, :])
+        grad = first[at, :]
+        grad_emb = norm_back(grad, emb_gain[...], unit, inverse)
+        sums[2:3, :] += column_sum(grad * unit)
+        sums[3:4, :] += column_sum(grad)
+        kind = kinds[at, :]
+        for t in range(2):
+            sums[4 + t : 5 + t, :] += column_sum(jnp.where(kind == t, grad_emb, 0.0))
+        return grad_emb
+
+    def last(n, carry):
+        at = pl.ds(pl.multiple_of(n * few, few), few)
+        left = back(at)
+        right = back(pl.ds(pl.multiple_of(size + n * few, few), few))
+        pos[at, :] = (left + right).astype(BF)
+        for t in range(width // 128):
+            one, two = left[:, t * 128 : (t + 1) * 128], right[:, t * 128 : (t + 1) * 128]
+            q = 2 * (t % 2)
+            raw[t // 2, q, at, :] = jnp.where(lane < 64, one, pltpu.roll(two, 64, 1)).astype(BF)
+            raw[t // 2, q + 1, at, :] = jnp.where(lane < 64, pltpu.roll(one, 64, 1), two).astype(BF)
+        return carry
+
+    lax.fori_loop(0, size // few, last, 0)
+    raw_copy = pltpu.make_async_copy(raw, raw_out, out_sem.at[0])
+    raw_copy.start()
+    pos_copy = pltpu.make_async_copy(pos, pos_out, out_sem.at[1])
+    pos_copy.start()
+    for g in range(2):
+        place_step(g)
+    feed_copy = pltpu.make_async_copy(kept, feed_out, out_sem.at[2])
+    feed_copy.start()
+    for copy in [first_copy, raw_copy, pos_copy, feed_copy] + out_copies:
+        copy.wait()
+    for g in range(2):
+        for copy in [core_copy(g)] + first_copies(g) + second_copies(g) + place_copies(g):
+            copy.wait_send()
+
+
+def mid(
+    active, upper_low, second_low, hidden_low, grad_first, embedded, q, k, v, probs, wq, wk, wv, wo, kinds, emb_gain
+):
+    tokens, width = grad_first.shape
+    seqs, heads, size, _ = probs.shape
+    units = active.shape[1]
+    per = width // 8
+    wide = 4 * width
+    vmem = pl.BlockSpec(memory_space=pltpu.VMEM)
+    hbm = pl.BlockSpec(memory_space=pl.ANY)
+    low = jax.ShapeDtypeStruct((tokens, width), BF)
+    small = pltpu.VMEM((tokens, width), BF)
+    large = pltpu.VMEM((tokens, width), F32)
+    return pl.pallas_call(
+        mid_kernel,
+        out_shape=[low] * 4
+        + [
+            jax.ShapeDtypeStruct((3, 4, size, 128), BF),
+            jax.ShapeDtypeStruct((size, width), BF),
+            jax.ShapeDtypeStruct((2 * per, width), BF),
+            jax.ShapeDtypeStruct((8, width), F32),
+        ],
+        in_specs=[hbm] * 14 + [vmem] * 2,
+        out_specs=[hbm] * 7 + [vmem],
+        scratch_shapes=[
+            pltpu.VMEM((2, tokens, 768), BF),
+            small,
+            pltpu.VMEM((width, tokens), BF),
+            pltpu.VMEM((2, 4, 2, per, wide), BF),
+            pltpu.VMEM((2, 4, per, wide), BF),
+            pltpu.VMEM((2, 2, per, wide // 2), BF),
+            pltpu.VMEM((2, 2, per, wide // 2), BF),
+            pltpu.VMEM((2, 2, per, width), BF),
+            pltpu.VMEM((2, 2, per, width), BF),
+            pltpu.VMEM((2, 3, per, width), BF),
+            pltpu.VMEM((2 * per, width), BF),
+            large,
+            small,
+            small,
+            small,
+            small,
+            small,
+            small,
+            small,
+            small,
+            pltpu.VMEM((4, width, width), BF),
+            large,
+            pltpu.VMEM((3, 4, size, 128), BF),
+            pltpu.VMEM((size, width), BF),
+            pltpu.VMEM((2, 2, size, size), BF),
+            pltpu.SemaphoreType.DMA((11,)),
+            pltpu.SemaphoreType.DMA((2,)),
+            pltpu.SemaphoreType.DMA((2,)),
+            pltpu.SemaphoreType.DMA((9,)),
+            pltpu.SemaphoreType.DMA((16,)),
+            pltpu.SemaphoreType.DMA((16,)),
+        ],
+        compiler_params=pltpu.CompilerParams(
+            collective_id=2, has_side_effects=True, vmem_limit_bytes=62 * MIB
+        ),
+        name="mid",
+    )(
+        active, upper_low, second_low, hidden_low, grad_first, embedded, q, k, v, probs, wq, wk, wv, wo,
+        kinds.reshape(tokens, 1), row(emb_gain),
+    )
+
+
 def flipped(index, bits):
     out = 0
     for place in range(3):
@@ -462,16 +838,15 @@
 
 
 def tail_kernel(
-    demb, slot, asked, small, normed, mixed, gfirst, dq, dk, dv,
-    word, packed,
-    og, inc, hits, dense, r1a, r1b, r2a, r2b,
-    ops, turned, wbuf, wcore, w1a, w1b, w2a, w2b, wz, wown,
-    load_sem, z_send, z_recv, d_send, d_recv, w_send, w_recv, own_sem,
+    slots, asked, asked_columns, pos, small, raw, normed, mixed, gfirst, dq, dk, dv, feed_own,
+    word, packed, feed_out, small_out,
+    tok, og, inc, rhs, dense, ops, turned, wbuf, wcore, w1a, w1b, w2a, w2b, wz, wown, small_by, small_in, small_dp,
+    load_sem, t_send, t_recv, z_send, z_recv, d_send, d_recv, w_send, w_recv, s_send, s_recv, own_sem,
 ):
-    owners, cap = og.shape[1], og.shape[2]
-    chunks, cols = og.shape[0], og.shape[3]
-    tokens = demb.shape[0]
-    part = dense.shape[4]
+    chunks, owners, sources, pairs, lanes = og.shape
+    half, width = pos.shape
+    tokens = 2 * half
+    tall = dense.shape[1]
     me = lax.axis_index("vocab")
     spot = lax.axis_index("dp")
     core, place = lax.rem(me, 2), lax.div(me, 2)
@@ -479,378 +854,485 @@
     across_x = {"dp": spot + 1 - 2 * xb}
     across_y = {"dp": spot + 2 - 4 * yb}
 
+    barrier = pltpu.get_barrier_semaphore()
+    for k in ORDER:
+        pl.semaphore_signal(barrier, inc=1, device_id={"vocab": flipped(me, k)}, device_id_type=MESH)
+    for k in (1, 2, 3):
+        pl.semaphore_signal(barrier, inc=1, device_id={"dp": flipped(spot, k)}, device_id_type=MESH)
     loads = [
         pltpu.make_async_copy(ref, ops.at[i], load_sem.at[i])
         for i, ref in enumerate((normed, dq, dk, dv, mixed, gfirst))
     ]
     for load in loads:
         load.start()
-    barrier = pltpu.get_barrier_semaphore()
-    for k in ORDER:
-        pl.semaphore_signal(barrier, inc=1, device_id={"vocab": flipped(me, k)}, device_id_type=MESH)
-    for peer in (across_x, across_y):
-        pl.semaphore_signal(barrier, inc=1, device_id=peer, device_id_type=MESH)
-    pl.semaphore_wait(barrier, len(ORDER) + 2)
+    for v in range(owners):
+        per = width // owners
+        small_by[v] = jnp.pad(small[:, v * per : (v + 1) * per], ((0, 0), (0, 128 - per)))
+    pl.semaphore_wait(barrier, len(ORDER) + 3)
 
     def remote(src, dst, send, recv, peer):
         return pltpu.make_async_remote_copy(
             src_ref=src, dst_ref=dst, send_sem=send, recv_sem=recv, device_id=peer, device_id_type=MESH
         )
 
-    def row_copy(c, k):
-        peer = flipped(me, k)
-        return remote(
-            og.at[c, peer], inc.at[c, me], z_send.at[c, k], z_recv.at[c, k], {"vocab": peer}
+    def start(copies):
+        for copy in copies:
+            copy.start()
+
+    def arrived(copies):
+        for copy in copies:
+            copy.wait_recv()
+
+    def gone(copies):
+        for copy in copies:
+            copy.wait_send()
+
+    def token_copies(c):
+        copies = []
+        for k in (3, 1, 2):
+            peer = flipped(spot, k)
+            copies.append(remote(raw.at[c, peer], tok.at[c, spot], t_send.at[c, k], t_recv.at[c, k], {"dp": peer}))
+        return copies
+
+    def token_own(c):
+        return pltpu.make_async_copy(raw.at[c, spot], tok.at[c, spot], own_sem.at[c])
+
+    for c in range(chunks):
+        start(token_copies(c))
+        token_own(c).start()
+
+    def row_copy(c, k, peer):
+        return remote(og.at[c, peer], inc.at[c, me], z_send.at[c, k], z_recv.at[c, k], {"vocab": peer})
+
+    def row_copies(c):
+        return [row_copy(c, k, flipped(me, k)) for k in ORDER]
+
+    def fill(c, peer, target):
+        def one(d, carry):
+            lane = lax.broadcasted_iota(jnp.int32, (pairs, lanes), 1)
+            wanted = lax.broadcasted_iota(jnp.int32, (2 * pairs, half), 0) + peer * (2 * pairs)
+            tokens_in = tok[c, d]
+            early = jnp.where(wanted == slots[d, :, :half], 1.0, 0.0).astype(BF)
+            late = jnp.where(wanted == slots[d, :, half:], 1.0, 0.0).astype(BF)
+            early = dot_nn(early, tokens_in)
+            late = dot_nn(late, tokens_in)
+            straight = jnp.where(lane < 64, early[:pairs], late[pairs:])
+            crossed = jnp.where(lane < 64, early[pairs:], late[:pairs])
+            target[d] = (straight + pltpu.roll(crossed, 64, 1)).astype(BF)
+            return carry
+
+        lax.fori_loop(0, sources, one, 0)
+
+    def fill_all(c, send):
+        for k in ORDER:
+            peer = flipped(me, k)
+            fill(c, peer, og.at[c, peer])
+            if send:
+                row_copy(c, k, peer).start()
+        fill(c, me, inc.at[c, me])
+
+    tile = 240
+    depth = 1024
+
+    def prepare(c):
+        lane = lax.broadcasted_iota(jnp.int32, (pairs, lanes), 1)
+        for v in range(owners):
+            for d in range(sources):
+                b = v * sources + d
+                straight = inc[c, v, d].astype(F32)
+                crossed = pltpu.roll(straight, 64, 1)
+                for h in range(2):
+                    column = asked_columns[:, h * owners * sources + b : h * owners * sources + b + 1]
+                    value = jnp.where(lane < 64, crossed if h else straight, straight if h else crossed)
+                    keep = (lane < 64) == (column < tall)
+                    rhs[h, pl.ds(b * pairs, pairs), :] = jnp.where(keep, value, 0.0).astype(BF)
+
+    def gather_rows(c, first, count):
+        def one(t, carry):
+            at = pl.multiple_of(t * tile, tile)
+            total = jnp.zeros((tile, lanes), F32)
+            for h in range(2):
+                for b in range(owners * sources * pairs // depth):
+                    ids = asked[h, :, b * depth : (b + 1) * depth]
+                    ids = jnp.where(ids >= tall, ids - tall, ids) - at
+                    hit = lax.broadcasted_iota(jnp.int32, (tile, depth), 0) == ids
+                    total = total + dot_nn(
+                        jnp.where(hit, 1.0, 0.0).astype(BF), rhs[h, pl.ds(b * depth, depth), :]
+                    )
+            dense[c, pl.ds(at, tile), :] = total.astype(BF)
+            return carry
+
+        lax.fori_loop(first, first + count, one, 0)
+
+    part = tall // 2
+
+    def lines_of(p):
+        return pl.ds(p * part, part)
+
+    def keep_copy(c, p):
+        return pltpu.make_async_copy(
+            dense.at[c, lines_of(p)], word.at[c, spot, lines_of(p)], own_sem.at[3 + 2 * c + p]
         )
 
-    def slots_of(peer):
-        wanted = lax.broadcasted_iota(jnp.int32, (cap, tokens), 0) + peer * cap
-        hot = jnp.where(wanted == slot[...], 1.0, 0.0).astype(BF)
-        return jnp.dot(hot, demb[...], preferred_element_type=F32).astype(BF)
-
-    for k in ORDER:
-        peer = flipped(me, k)
-        rows = slots_of(peer)
-        for c in range(chunks):
-            og[c, peer] = rows[:, c * cols : (c + 1) * cols]
-        row_copy(0, k).start()
-    rows = slots_of(me)
-    for c in range(chunks):
-        inc[c, me] = rows[:, c * cols : (c + 1) * cols]
-
-    width = demb.shape[1]
+    def near_copies(c, p):
+        return [
+            remote(
+                dense.at[c, lines_of(p)], word.at[c, spot, lines_of(p)], d_send.at[c, 2 * p], d_recv.at[c, 2 * p], across_x
+            ),
+            remote(
+                dense.at[c, lines_of(p)],
+                word.at[c, spot, lines_of(p)],
+                d_send.at[c, 2 * p + 1],
+                d_recv.at[c, 2 * p + 1],
+                across_y,
+            ),
+        ]
+
+    def far_copy(c, p):
+        source = flipped(spot, 1) if p == 0 else flipped(spot, 2)
+        view = word.at[c, source, lines_of(p)]
+        return remote(view, view, d_send.at[c, 4 + p], d_recv.at[c, 4 + p], across_y if p == 0 else across_x)
+
     per = width // owners
     block = 256
+    quarter = wown.shape[0]
 
     def turn(which):
-        for i in range(tokens // block):
+        def one(i, carry):
+            at = pl.ds(pl.multiple_of(i * block, block), block)
             for j in range(width // block):
-                turned[pl.ds(j * block, block), pl.ds(i * block, block)] = ops[
-                    which, pl.ds(i * block, block), pl.ds(j * block, block)
-                ].T
+                there = pl.ds(j * block, block)
+                turned[there, at] = ops[which, at, there].T
+            return carry
+
+        lax.fori_loop(0, tokens // block, one, 0)
 
     def weight(which, at):
         def one(n, carry):
-            there = pl.multiple_of(n * block, block)
-            out = jnp.dot(turned[...], ops[which, :, pl.ds(there, block)], preferred_element_type=F32).astype(BF)
-            there = pl.multiple_of(at * width + n * block, block)
+            there = pl.ds(pl.multiple_of(n * block, block), block)
+            out = dot_nn(turned[...], ops[which, :, there]).astype(BF)
             for v in range(owners):
-                wbuf[v // 2, v % 2, pl.ds(0, per), pl.ds(there, block)] = out[v * per : (v + 1) * per]
+                wbuf[v // 2, v % 2, pl.ds(at * per, per), there] = out[v * per : (v + 1) * per]
             return carry
 
         lax.fori_loop(0, width // block, one, 0)
 
+    core_copy = remote(wbuf.at[:, 1 - core], wcore, w_send.at[0], w_recv.at[0], {"vocab": flipped(me, 1)})
+
+    def wide(b):
+        return pl.ds(pl.multiple_of(b * 2 * quarter, quarter), 2 * quarter)
+
+    def narrow(b, c):
+        return pl.ds(pl.multiple_of((2 * b + c) * quarter, quarter), quarter)
+
+    def add(view, value):
+        view[...] = (view[...].astype(F32) + value.astype(F32)).astype(BF)
+
+    def core_step():
+        core_copy.wait_recv()
+
+        def one(i, carry):
+            z = lax.div(i, 4)
+            at = pl.ds(pl.multiple_of(lax.rem(i, 4) * quarter, quarter), quarter)
+            add(wbuf.at[z, core, at, :], wcore[z, at, :])
+            return carry
+
+        lax.fori_loop(0, 16, one, 0)
+
+    def first_weights():
+        return [
+            remote(wbuf.at[pl.ds(0, 2), core, wide(1 - xb), :], w1a, w_send.at[1], w_recv.at[1], across_x),
+            remote(wbuf.at[pl.ds(2, 2), core, wide(1 - yb), :], w1b, w_send.at[2], w_recv.at[2], across_y),
+        ]
+
+    def second_weights():
+        return [
+            remote(wbuf.at[pl.ds(0, 2), core, narrow(xb, 1 - yb), :], w2a, w_send.at[3], w_recv.at[3], across_y),
+            remote(wbuf.at[pl.ds(2, 2), core, narrow(yb, 1 - xb), :], w2b, w_send.at[4], w_recv.at[4], across_x),
+        ]
+
+    def first_step():
+        arrived(first_weights())
+        for z in range(2):
+            add(wbuf.at[z, core, wide(xb), :], w1a[z])
+            add(wbuf.at[2 + z, core, wide(yb), :], w1b[z])
+
+    def second_step():
+        arrived(second_weights())
+        for z in range(2):
+            add(wbuf.at[z, core, narrow(xb, yb), :], w2a[z])
+            add(wbuf.at[2 + z, core, narrow(yb, xb), :], w2b[z])
+
+    def owned(z):
+        at = 2 * xb + yb + lax.div(z, 2) * (yb - xb)
+        return wbuf.at[z, core, pl.ds(pl.multiple_of(at * quarter, quarter), quarter), :]
+
+    def third_weights():
+        copies = []
+        for k in (3, 2, 1):
+            to = flipped(place, k)
+            copies.append(
+                remote(owned(to), wz.at[k - 1], w_send.at[4 + k], w_recv.at[4 + k], {"vocab": 2 * to + core})
+            )
+        return copies
+
+    def third_step():
+        arrived(third_weights())
+        total = owned(place)[...].astype(F32)
+        for k in range(3):
+            total = total + wz[k].astype(F32)
+        wown[...] = total.astype(BF)
+
+    def spread(own, target, at):
+        wide_half = width // 2
+        left, right = pl.ds(0, wide_half), pl.ds(wide_half, wide_half)
+        kept = pltpu.make_async_copy(own, target.at[xb, yb], own_sem.at[9 + at])
+        sems = [(w_send.at[8 + 4 * at + i], w_recv.at[8 + 4 * at + i]) for i in range(4)]
+        near = [
+            remote(own, target.at[xb, yb], *sems[0], across_x),
+            remote(own, target.at[xb, yb], *sems[1], across_y),
+        ]
+        from_x, from_y = target.at[1 - xb, yb, :, left], target.at[xb, 1 - yb, :, right]
+        far = [remote(from_x, from_x, *sems[2], across_y), remote(from_y, from_y, *sems[3], across_x)]
+        return kept, near, far
+
+    feed_kept, feed_near, feed_far = spread(feed_own, feed_out, 0)
+    kept, fourth_weights, fifth_weights = spread(wown, packed, 1)
+
+    def small_copies():
+        copies = []
+        for k in ORDER:
+            peer = flipped(me, k)
+            copies.append(remote(small_by.at[peer], small_in.at[k], s_send.at[k], s_recv.at[k], {"vocab": peer}))
+        return copies
+
+    def small_last():
+        return [
+            remote(small_in.at[0], small_dp.at[k - 1], s_send.at[7 + k], s_recv.at[7 + k], {"dp": flipped(spot, k)})
+            for k in (1, 2, 3)
+        ]
+
+    start(small_copies())
     loads[0].wait()
     turn(0)
-    for i in range(3):
+    loads[1].wait()
+    weight(1, 0)
+    token_own(0).wait()
+    arrived(token_copies(0))
+    fill_all(0, True)
+    for i in (1, 2):
         loads[1 + i].wait()
         weight(1 + i, i)
     loads[4].wait()
     turn(4)
     loads[5].wait()
     weight(5, 3)
-    half = tokens // 2
-    lines = half // owners // 4
+    share = half // owners
     for v in range(owners):
-        for j in range(4):
-            at = v * (half // owners) + j * lines
-            total = demb[pl.ds(at, lines), :].astype(F32) + demb[pl.ds(half + at, lines), :].astype(F32)
-            wbuf[v // 2, v % 2, pl.ds(per, lines), pl.ds(j * width, width)] = total.astype(BF)
-        wbuf[v // 2, v % 2, pl.ds(per + lines, 16), :] = jnp.zeros((16, 4 * width), BF)
-        wbuf[v // 2, v % 2, pl.ds(per + lines, 16), pl.ds(0, 128)] = jnp.pad(
-            small[:, v * per : (v + 1) * per], ((0, 0), (0, 128 - per))
-        ).astype(BF)
-    partner = {"vocab": flipped(me, 1)}
-    core_copy = remote(wbuf.at[:, 1 - core], wcore, w_send.at[0], w_recv.at[0], partner)
+        wbuf[v // 2, v % 2, pl.ds(4 * per, share), :] = pos[pl.ds(v * share, share), :]
     core_copy.start()
-
-    tile = 240
-    rows_local = 8 * part
-
-    def match(t, carry):
-        at = pl.multiple_of(t * tile, tile)
-        row = lax.broadcasted_iota(jnp.int32, (tile, owners * cap), 0) + at
-        hits[pl.ds(at, tile), :] = jnp.where(row == asked[...], 1.0, 0.0).astype(BF)
-        return carry
-
-    lax.fori_loop(0, rows_local // tile, match, 0)
-
-    quarter = wown.shape[0]
-    def w_view(z, x, y):
-        return wbuf.at[z, core, pl.ds(pl.multiple_of((2 * x + y) * quarter, quarter), quarter), :]
-
-    def w_half(z, x):
-        return wbuf.at[z, core, pl.ds(pl.multiple_of(2 * x * quarter, quarter), 2 * quarter), :]
-
-    def core_sum(i, carry):
-        z = lax.div(i, 4)
-        at = pl.multiple_of(lax.rem(i, 4) * quarter, quarter)
-        mine = wbuf[z, core, pl.ds(at, quarter), :].astype(F32)
-        wbuf[z, core, pl.ds(at, quarter), :] = (mine + wcore[z, pl.ds(at, quarter), :].astype(F32)).astype(BF)
-        return carry
-
-    def first_weights():
-        copies = []
-        for z in range(2):
-            copies.append(remote(w_half(z, 1 - xb), w1a.at[z], w_send.at[1 + z], w_recv.at[1 + z], across_x))
-            for x in range(2):
-                at = 2 * z + x
-                copies.append(
-                    remote(w_view(2 + z, x, 1 - yb), w1b.at[z, x], w_send.at[3 + at], w_recv.at[3 + at], across_y)
-                )
-        return copies
-
-    def add_to(z, x, y, value):
-        view = w_view(z, x, y)
-        view[...] = (view[...].astype(F32) + value.astype(F32)).astype(BF)
-
-    def second_weights():
-        copies = []
-        for z in range(2):
-            copies.append(remote(w_view(z, xb, 1 - yb), w2a.at[z], w_send.at[7 + z], w_recv.at[7 + z], across_y))
-            copies.append(remote(w_view(2 + z, 1 - xb, yb), w2b.at[z], w_send.at[9 + z], w_recv.at[9 + z], across_x))
-        return copies
-
-    def place_copy(k):
-        to = flipped(place, k)
-        return remote(
-            w_view(to, xb, yb), wz.at[k - 1], w_send.at[10 + k], w_recv.at[10 + k], {"vocab": 2 * to + core}
-        )
-
-    def third_weights():
-        return [place_copy(k) for k in (3, 2, 1)]
-
-    def own_weights():
-        return pltpu.make_async_copy(wown, packed.at[xb, yb], own_sem.at[0])
-
-    def fourth_weights():
-        return [
-            remote(wown, packed.at[xb, yb], w_send.at[14], w_recv.at[14], across_x),
-            remote(wown, packed.at[xb, yb], w_send.at[15], w_recv.at[15], across_y),
-        ]
-
-    wide = 2 * width
-
-    def fifth_weights():
-        left, right = pl.ds(0, wide), pl.ds(wide, wide)
-        return [
-            remote(
-                packed.at[1 - xb, yb, :, left], packed.at[1 - xb, yb, :, left], w_send.at[16], w_recv.at[16], across_y
-            ),
-            remote(
-                packed.at[xb, 1 - yb, :, right], packed.at[xb, 1 - yb, :, right], w_send.at[17], w_recv.at[17], across_x
-            ),
-        ]
-
-    def first_rows(c):
-        return [
-            remote(dense.at[c, 0, 1 - xb], r1a.at[c], d_send.at[c, 0], d_recv.at[c, 0], across_x),
-            remote(dense.at[c, 1, :, 1 - yb], r1b.at[c], d_send.at[c, 1], d_recv.at[c, 1], across_y),
-        ]
-
-    def second_rows(c):
-        return [
-            remote(dense.at[c, 0, xb, 1 - yb], r2a.at[c], d_send.at[c, 2], d_recv.at[c, 2], across_y),
-            remote(dense.at[c, 1, 1 - xb, yb], r2b.at[c], d_send.at[c, 3], d_recv.at[c, 3], across_x),
-        ]
-
-    def spread(c):
-        return pl.ds(c * cols, cols)
-
-    def own_rows(c):
-        return [
-            pltpu.make_async_copy(dense.at[c, h, xb, yb], word.at[h, xb, yb, :, spread(c)], own_sem.at[1 + 2 * c + h])
-            for h in range(2)
-        ]
-
-    def third_rows(c):
-        return [
-            remote(dense.at[c, 0, xb, yb], word.at[0, xb, yb, :, spread(c)], d_send.at[c, 4], d_recv.at[c, 4], across_x),
-            remote(dense.at[c, 1, xb, yb], word.at[1, xb, yb, :, spread(c)], d_send.at[c, 5], d_recv.at[c, 5], across_y),
-        ]
-
-    def fourth_rows(c):
-        return [
-            remote(
-                word.at[0, :, yb, :, spread(c)], word.at[0, :, yb, :, spread(c)], d_send.at[c, 6], d_recv.at[c, 6], across_y
-            ),
-            remote(
-                word.at[1, xb, :, :, spread(c)], word.at[1, xb, :, :, spread(c)], d_send.at[c, 7], d_recv.at[c, 7], across_x
-            ),
-        ]
-
-    def start(copies):
-        for copy in copies:
-            copy.start()
-
-    def arrived(copies):
-        for copy in copies:
-            copy.wait_recv()
-
-    def gone(copies):
-        for copy in copies:
-            copy.wait_send()
-
-    def arrive_slots(c):
-        for k in ORDER:
-            row_copy(c, k).wait_recv()
-
-    def sum_slots(c):
-        def one(t, carry):
-            h, x, y = lax.div(t, 4), lax.rem(lax.div(t, 2), 2), lax.rem(t, 2)
-            at = pl.multiple_of(t * part, part)
-            total = jnp.zeros((part, cols), F32)
-            for p in range(owners):
-                total = total + jnp.dot(
-                    hits[pl.ds(at, part), pl.ds(p * cap, cap)], inc[c, p], preferred_element_type=F32
-                )
-            dense[c, h, x, y] = total.astype(BF)
-            return carry
-
-        lax.fori_loop(0, 8, one, 0)
-
-    def add_rows(c, h, x, y, value):
-        dense[c, h, x, y] = (dense[c, h, x, y].astype(F32) + value.astype(F32)).astype(BF)
-
-    def add_first(c):
-        arrived(first_rows(c))
-        for i in range(2):
-            add_rows(c, 0, xb, i, r1a[c, i])
-            add_rows(c, 1, i, yb, r1b[c, i])
-        start(second_rows(c))
-
-    def add_second(c):
-        arrived(second_rows(c))
-        add_rows(c, 0, xb, yb, r2a[c])
-        add_rows(c, 1, xb, yb, r2b[c])
-        start(third_rows(c))
-        start(own_rows(c))
+    token_own(1).wait()
+    arrived(token_copies(1))
+    fill_all(1, False)
+    core_step()
+    start(first_weights())
+    arrived(small_copies())
+    total = small_by[me]
+    for k in ORDER:
+        total = total + small_in[k]
+    small_in[0] = total
+    start(small_last())
+    token_own(2).wait()
+    arrived(token_copies(2))
+    fill_all(2, False)
+
+    def close_chunk(c, between):
+        arrived(row_copies(c))
+        if c + 1 < chunks:
+            start(row_copies(c + 1))
+        else:
+            start(third_weights())
+        prepare(c)
+        gather_rows(c, 0, 4)
+        start(near_copies(c, 0))
+        keep_copy(c, 0).start()
+        between()
+        gather_rows(c, 4, 4)
+        start(near_copies(c, 1))
+        keep_copy(c, 1).start()
 
     def pass_on(c):
-        for copy in own_rows(c):
-            copy.wait()
-        arrived(third_rows(c))
-        start(fourth_rows(c))
-
-    core_copy.wait_recv()
+        arrived(near_copies(c, 0))
+        far_copy(c, 0).start()
+        arrived(near_copies(c, 1))
+        far_copy(c, 1).start()
+
+    def nothing():
+        return None
+
+    first_step()
+    start(second_weights())
+    close_chunk(0, nothing)
+    second_step()
+    start(feed_near)
+    feed_kept.start()
+    pass_on(0)
+    feed_kept.wait()
+    arrived(feed_near)
+    start(feed_far)
+    close_chunk(1, nothing)
+    arrived(small_last())
+    total = small_in[0]
+    for k in range(3):
+        total = total + small_dp[k]
+    small_out[...] = total
+    pass_on(1)
+    close_chunk(2, nothing)
+    third_step()
+    start(fourth_weights)
+    kept.start()
+    pass_on(2)
+    kept.wait()
+    arrived(fourth_weights)
+    start(fifth_weights)
+
+    for c in range(chunks):
+        for p in range(2):
+            keep_copy(c, p).wait()
+            far_copy(c, p).wait_recv()
+    arrived(feed_far)
+    arrived(fifth_weights)
     core_copy.wait_send()
-    lax.fori_loop(0, 16, core_sum, 0)
-    start(first_weights())
-
-    arrive_slots(0)
-    for k in ORDER:
-        row_copy(1, k).start()
-    sum_slots(0)
-    start(first_rows(0))
-
-    arrived(first_weights())
-    for z in range(2):
-        for i in range(2):
-            add_to(z, xb, i, w1a[z, pl.ds(i * quarter, quarter), :])
-            add_to(2 + z, i, yb, w1b[z, i])
-    start(second_weights())
-
-    add_first(0)
-    arrive_slots(1)
-    for k in ORDER:
-        row_copy(2, k).start()
-    sum_slots(1)
-    start(first_rows(1))
-    add_second(0)
-
-    arrived(second_weights())
-    for z in range(2):
-        add_to(z, xb, yb, w2a[z])
-        add_to(2 + z, xb, yb, w2b[z])
-    start(third_weights())
-
-    pass_on(0)
-    add_first(1)
-    arrive_slots(2)
-    sum_slots(2)
-    start(first_rows(2))
-    add_second(1)
-
-    arrived(third_weights())
-    mine = w_view(place, xb, yb)[...].astype(F32)
-    for k in range(3):
-        mine = mine + wz[k].astype(F32)
-    wown[...] = mine.astype(BF)
-    start(fourth_weights())
-    own_weights().start()
-
-    add_first(2)
-    pass_on(1)
-    own_weights().wait()
-    arrived(fourth_weights())
-    start(fifth_weights())
-    add_second(2)
-    pass_on(2)
-
+    gone(small_copies())
+    gone(small_last())
     for c in range(chunks):
-        arrived(fourth_rows(c))
-    arrived(fifth_weights())
-    for c in range(chunks):
-        for k in ORDER:
-            row_copy(c, k).wait_send()
-        for step in (first_rows, second_rows, third_rows, fourth_rows):
-            gone(step(c))
-    for step in (first_weights, second_weights, third_weights, fourth_weights, fifth_weights):
-        gone(step())
-
-
-def tail(demb, slot, asked, small, normed, mixed, gfirst, dq, dk, dv, rows_local, owners):
-    tokens, width = demb.shape
-    cap = asked.size // owners
-    chunks = 3
-    cols = width // chunks
-    part = rows_local // 8
-    lines = 128
-    wide = 4 * width
+        gone(token_copies(c))
+        gone(row_copies(c))
+        for p in range(2):
+            gone(near_copies(c, p))
+            far_copy(c, p).wait_send()
+    for copies in (first_weights(), second_weights(), third_weights(), fourth_weights, fifth_weights, feed_near, feed_far):
+        gone(copies)
+
+
+def tail(slots, asked, pos, small, raw, normed, mixed, gfirst, dq, dk, dv, feed_own, rows_local):
+    half, width = pos.shape
+    sources, owners, cap = asked.shape
+    chunks = raw.shape[0]
+    pairs = cap // 2
+    tall = rows_local // 2
+    lines = 4 * (width // owners) + half // owners
     vmem = pl.BlockSpec(memory_space=pltpu.VMEM)
     hbm = pl.BlockSpec(memory_space=pl.ANY)
-    word, packed = pl.pallas_call(
+    by_half = asked.reshape(sources, owners, 2, pairs).transpose(2, 1, 0, 3)
+    columns = by_half.reshape(2 * owners * sources, pairs).T
+    return pl.pallas_call(
         tail_kernel,
         out_shape=(
-            jax.ShapeDtypeStruct((2, 2, 2, part, width), BF),
-            jax.ShapeDtypeStruct((2, 2, lines // 4, wide), BF),
+            jax.ShapeDtypeStruct((chunks, sources, tall, 128), BF),
+            jax.ShapeDtypeStruct((2, 2, lines // 4, width), BF),
+            jax.ShapeDtypeStruct((2, 2) + feed_own.shape, BF),
+            jax.ShapeDtypeStruct((16, 128), F32),
         ),
-        in_specs=[vmem] * 4 + [hbm] * 6,
-        out_specs=(hbm, hbm),
+        in_specs=[vmem] * 5 + [hbm] * 8,
+        out_specs=(hbm, hbm, hbm, vmem),
         scratch_shapes=[
-            pltpu.VMEM((chunks, owners, cap, cols), BF),
-            pltpu.VMEM((chunks, owners, cap, cols), BF),
-            pltpu.VMEM((rows_local, owners * cap), BF),
-            pltpu.VMEM((chunks, 2, 2, 2, part, cols), BF),
-            pltpu.VMEM((chunks, 2, part, cols), BF),
-            pltpu.VMEM((chunks, 2, part, cols), BF),
-            pltpu.VMEM((chunks, part, cols), BF),
-            pltpu.VMEM((chunks, part, cols), BF),
-            pltpu.VMEM((6, tokens, width), BF),
-            pltpu.VMEM((width, tokens), BF),
-            pltpu.VMEM((4, 2, lines, wide), BF),
-            pltpu.VMEM((4, lines, wide), BF),
-            pltpu.VMEM((2, lines // 2, wide), BF),
-            pltpu.VMEM((2, 2, lines // 4, wide), BF),
-            pltpu.VMEM((2, lines // 4, wide), BF),
-            pltpu.VMEM((2, lines // 4, wide), BF),
-            pltpu.VMEM((3, lines // 4, wide), BF),
-            pltpu.VMEM((lines // 4, wide), BF),
+            pltpu.VMEM((chunks, sources, half, 128), BF),
+            pltpu.VMEM((chunks, owners, sources, pairs, 128), BF),
+            pltpu.VMEM((chunks, owners, sources, pairs, 128), BF),
+            pltpu.VMEM((2, owners * sources * pairs, 128), BF),
+            pltpu.VMEM((chunks, tall, 128), BF),
+            pltpu.VMEM((6, 2 * half, width), BF),
+            pltpu.VMEM((width, 2 * half), BF),
+            pltpu.VMEM((4, 2, lines, width), BF),
+            pltpu.VMEM((4, lines, width), BF),
+            pltpu.VMEM((2, lines // 2, width), BF),
+            pltpu.VMEM((2, lines // 2, width), BF),
+            pltpu.VMEM((2, lines // 4, width), BF),
+            pltpu.VMEM((2, lines // 4, width), BF),
+            pltpu.VMEM((3, lines // 4, width), BF),
+            pltpu.VMEM((lines // 4, width), BF),
+            pltpu.VMEM((owners, 16, 128), F32),
+            pltpu.VMEM((owners, 16, 128), F32),
+            pltpu.VMEM((3, 16, 128), F32),
             pltpu.SemaphoreType.DMA((6,)),
+            pltpu.SemaphoreType.DMA((chunks, 4)),
+            pltpu.SemaphoreType.DMA((chunks, 4)),
             pltpu.SemaphoreType.DMA((chunks, owners)),
             pltpu.SemaphoreType.DMA((chunks, owners)),
-            pltpu.SemaphoreType.DMA((chunks, 8)),
-            pltpu.SemaphoreType.DMA((chunks, 8)),
-            pltpu.SemaphoreType.DMA((18,)),
-            pltpu.SemaphoreType.DMA((18,)),
-            pltpu.SemaphoreType.DMA((7,)),
+            pltpu.SemaphoreType.DMA((chunks, 6)),
+            pltpu.SemaphoreType.DMA((chunks, 6)),
+            pltpu.SemaphoreType.DMA((16,)),
+            pltpu.SemaphoreType.DMA((16,)),
+            pltpu.SemaphoreType.DMA((11,)),
+            pltpu.SemaphoreType.DMA((11,)),
+            pltpu.SemaphoreType.DMA((11,)),
         ],
-        compiler_params=pltpu.CompilerParams(
-            collective_id=1, has_side_effects=True, vmem_limit_bytes=62 * 1024 * 1024
+        compiler_params=pltpu.CompilerParams(collective_id=1, has_side_effects=True, vmem_limit_bytes=60 * MIB),
+        name="tail",
+    )(
+        slots.reshape(sources, 1, 2 * half), by_half.reshape(2, 1, -1), columns, pos, small,
+        raw, normed, mixed, gfirst, dq, dk, dv, feed_own,
+    )
+
+
+def finish_kernel(near, word_in, packed, feeds, word, query, keys, values, out, pos, up, down):
+    lane = lax.broadcasted_iota(jnp.int32, word_in.shape[2:], 1)
+    chunks, sources = word_in.shape[:2]
+    for c in range(chunks):
+        for q in range(0, sources, 2):
+            one, two = word_in[c, q].astype(F32), word_in[c, q + 1].astype(F32)
+            at = pl.ds((c * sources + q) * 64, 128)
+            word[0, :, at] = jnp.where(lane < 64, one, pltpu.roll(two, 64, 1))
+            word[1, :, at] = jnp.where(lane < 64, pltpu.roll(one, 64, 1), two)
+
+    @pl.when(pl.program_id(0) == 0)
+    def _():
+        n = near[0]
+        order = ((0, 0), (1 - n, n), (n, 1 - n), (1, 1))
+        per, width = query.shape
+        rows = jnp.concatenate([packed[a, b] for a, b in order], 0).astype(F32)
+        for i, target in enumerate((query, keys, values, out)):
+            target[...] = rows[i * per : (i + 1) * per]
+        pos[...] = rows[4 * per :]
+        lines = []
+        for i, (a, b) in enumerate(order):
+            up[:, pl.ds(i * width, width)] = feeds[a, b, per:, :].astype(F32)
+            for j in range(2):
+                lines.append(feeds[a, b, :per, j * 4 * per : (j + 1) * 4 * per])
+        down[...] = jnp.concatenate(lines, 0).astype(F32).T
+
+
+def finish(near, word, packed, feeds, rows_local, owners):
+    chunks, sources, tall, _ = word.shape
+    width = packed.shape[3]
+    per = width // owners
+    steps = 8
+    part = tall // steps
+    held = jax.ShapeDtypeStruct((per, width), F32)
+    share = packed.shape[2] * 4 - 4 * per
+    shapes = [held] * 4 + [
+        jax.ShapeDtypeStruct((share, width), F32),
+        jax.ShapeDtypeStruct((per, 4 * width), F32),
+        jax.ShapeDtypeStruct((4 * per, width), F32),
+    ]
+    results = pl.pallas_call(
+        finish_kernel,
+        grid_spec=pltpu.PrefetchScalarGridSpec(
+            num_scalar_prefetch=1,
+            grid=(steps,),
+            in_specs=[
+                pl.BlockSpec((chunks, sources, part, 128), lambda i, *_: (0, 0, i, 0)),
+                fixed(packed.shape),
+                fixed(feeds.shape),
+            ],
+            out_specs=[pl.BlockSpec((2, part, width), lambda i, *_: (0, i, 0))] + [fixed(s.shape) for s in shapes],
         ),
-        name="tail",
-    )(demb, slot.reshape(1, tokens), asked.reshape(1, owners * cap), small, normed, mixed, gfirst, dq, dk, dv)
-    return word.reshape(rows_local, width), packed.reshape(lines, wide)
+        out_shape=[jax.ShapeDtypeStruct((2, tall, width), F32)] + shapes,
+        compiler_params=pltpu.CompilerParams(vmem_limit_bytes=48 * MIB),
+        name="finish",
+    )(near.astype(jnp.int32).reshape(1), word, packed, feeds)
+    return [results[0].reshape(rows_local, width)] + list(results[1:])
 
 
 def local(
@@ -935,29 +1417,57 @@
         sums[i] for i in range(6)
     ]
     grad_up_bias = grad_up_bias[0]
-    grad_down = matmul_tn(active_low, grad_second_low)
-    grad_up = matmul_tn(hidden_low, grad_upper_low)
-    grad_first_low, grad_query_low, grad_keys_low, grad_values_low, embedding_output_gradient, sums = attend_back(
-        grad_first,
-        embedded,
-        type_ids,
-        query,
-        keys,
-        values,
-        probs,
-        query_weight,
-        key_weight,
-        value_weight,
-        out_weight,
-        emb_gain,
-    )
+    fast = owners == 8 and lax.axis_size("dp") == 4
+    if fast:
+        (
+            grad_first_low,
+            grad_query_low,
+            grad_keys_low,
+            grad_values_low,
+            raw,
+            grad_pos,
+            feed_own,
+            sums,
+        ) = mid(
+            active_low,
+            grad_upper_low,
+            grad_second_low,
+            hidden_low,
+            grad_first,
+            embedded,
+            query,
+            keys,
+            values,
+            probs,
+            query_weight,
+            key_weight,
+            value_weight,
+            out_weight,
+            type_ids,
+            emb_gain,
+        )
+    else:
+        grad_down = matmul_tn(active_low, grad_second_low)
+        grad_up = matmul_tn(hidden_low, grad_upper_low)
+        grad_first_low, grad_query_low, grad_keys_low, grad_values_low, embedding_output_gradient, sums = attend_back(
+            grad_first,
+            embedded,
+            type_ids,
+            query,
+            keys,
+            values,
+            probs,
+            query_weight,
+            key_weight,
+            value_weight,
+            out_weight,
+            emb_gain,
+        )
+        grad_pos = jnp.sum(embedding_output_gradient.astype(jnp.float32).reshape(seq_count, seq_len, width), 0)
     grad_query_bias, grad_value_bias, grad_emb_gain, grad_emb_bias = [sums[i] for i in range(4)]
     token_type_gradient = sums[4:6]
-    grad_pos = jnp.sum(embedding_output_gradient.astype(jnp.float32).reshape(seq_count, seq_len, width), 0)
     bf = jnp.bfloat16
     per = width // owners
-    grad_down_all = sum_over_all(grad_down.astype(bf))
-    grad_up_all = sum_over_all(grad_up.astype(bf))
     small = jnp.stack(
         [
             grad_query_bias,
@@ -974,33 +1484,39 @@
             token_type_gradient[1],
         ]
     )
-    if owners == 8 and lax.axis_size("dp") == 4:
+    if fast:
         ups = grad_up_bias.reshape(owners, 4, per).transpose(1, 0, 2).reshape(4, width)
-        word_low, packed = tail(
-            embedding_output_gradient.reshape(tokens, width).astype(bf),
-            slot,
-            asked,
+        lists = lax.all_gather(jnp.concatenate([slot, asked.reshape(-1)]), "dp")
+        word_pairs, packed, feeds, small = tail(
+            lists[:, :tokens],
+            lists[:, tokens:].reshape(-1, owners, capacity),
+            grad_pos,
             jnp.concatenate([small, ups], 0),
+            raw,
             normed_low,
             mixed_low,
             grad_first_low,
             grad_query_low,
             grad_keys_low,
             grad_values_low,
+            feed_own,
             rows_local,
-            owners,
         )
-        grad_word = word_low.astype(jnp.float32)
-        packed = packed.astype(jnp.float32)
-        grad_query_weight, grad_key_weight, grad_value_weight, grad_out_weight = [
-            packed[:per, i * width : (i + 1) * width] for i in range(4)
-        ]
-        lines = seq_len // owners // 4
-        grad_pos = (
-            packed[per : per + lines].reshape(lines, 4, width).transpose(1, 0, 2).reshape(4 * lines, width)
-        )
-        small = packed[per + lines :, :per]
+        near = lax.axis_index("vocab") < owners // 2
+        (
+            grad_word,
+            grad_query_weight,
+            grad_key_weight,
+            grad_value_weight,
+            grad_out_weight,
+            grad_pos,
+            grad_up,
+            grad_down,
+        ) = finish(near, word_pairs, packed, feeds, rows_local, owners)
+        small = small[:, :per]
     else:
+        grad_down = sum_over_all(grad_down.astype(bf))
+        grad_up = sum_over_all(grad_up.astype(bf))
         places = slot[None, :] == jnp.arange(owners * capacity)[:, None]
         outgoing = matmul(
             places.astype(bf), embedding_output_gradient.reshape(tokens, width).astype(bf)
@@ -1062,7 +1578,6 @@
     ) = [small[i] for i in range(10)]
     token_type_gradient = small[10:12]
     grad_up_bias = small[12:].reshape(-1)
-    grad_up, grad_down = grad_up_all, grad_down_all
     return (
         encoded.reshape(seq_count, seq_len, width),
         grad_word,

time: 511 us -> 445 us (0.87)
  waiting for transfers between devices: 100 us -> 53 us
  Pallas kernels: 271 us -> 303 us
  starting transfers between devices: 28.5 us -> 3.79 us
  other arithmetic: 32.8 us -> 13.1 us
  matrix products: 16.5 us -> 2.71 us
  blocking collectives: 11.7 us -> 20 us
    ppermute x24 -> x0, waiting for transfers between devices: 38.3 us -> none  [the longest x18 25.6 us: swap(): return lax.ppermute(value, axis_name, [(i, i ^ bit) for i in range(size)])]
    pallas_call x2 -> x3, Pallas kernels: 197 us -> 229 us  [the longest x1 136 us: tail(): pl.pallas_call(tail_kernel, out_shape=(jax.ShapeDtypeStruct((chunks, sour...]
    ppermute x24 -> x0, starting transfers between devices: 24.9 us -> none  [the longest x18 17.6 us: swap(): return lax.ppermute(value, axis_name, [(i, i ^ bit) for i in range(size)])]
    convert_element_type x16 -> x0, other arithmetic: 18.5 us -> none  [the longest x1 8.77 us: local(): grad_word = word_low.astype(jnp.float32)]
    dot_general x2 -> x0, matrix products: 13.7 us -> none  [matmul_tn(): lax.dot_general(left, right, (((0,), (0,)), ((), ())), preferred_element_...]
    all_to_all x1, waiting for transfers between devices: 61.9 us -> 53 us  [local(): lax.all_to_all(found, 'vocab', split_axis=0, concat_axis=0, tiled=True)]
    all_gather x0 -> x1, blocking collectives: none -> 8.25 us  [local(): lists = lax.all_gather(jnp.concatenate([slot, asked.reshape(-1)]), 'dp')]
  transfers between devices with their start and end apart: 25 -> 1, of which waited for: 10 -> 1; matrix products, arithmetic and copies ran while one was open for 8% -> 2% of each run, Pallas kernels for 39% -> 0%
where the time goes in v4:
time: 445 us; the launch traced here: 438 us
  Pallas kernels  303 us (68%)
  waiting for transfers between devices  53 us (12%)
  local copies, waits for them, and re-layouts  40.6 us (9%)
  blocking collectives  20 us (4%)
  other arithmetic  13.1 us (3%)
    pallas_call x1, Pallas kernels, tail(): pl.pallas_call(tail_kernel, out_shape=(jax.ShapeDtypeStruct((chunks, sour...  136 us
    pallas_call x1, Pallas kernels, mid(): pl.pallas_call(mid_kernel, out_shape=[low] * 4 + [jax.ShapeDtypeStruct((3...  82 us
    all_to_all x1, waiting for transfers between devices, local(): lax.all_to_all(found, 'vocab', split_axis=0, concat_axis=0, tiled=True)  53 us
    pallas_call x1, Pallas kernels, feed(): pl.pallas_call(feed_kernel, grid=(tokens // tile,), in_specs=[part, part,...  42.3 us
    pallas_call x1, Pallas kernels, attend(): pl.pallas_call(attend_kernel, grid_spec=pltpu.PrefetchScalarGridSpec(num_...  32 us
    gather x1, local copies, waits for them, and re-layouts, local(): found = word_table[jnp.maximum(asked, 0)]  11.9 us
    all_to_all x1, blocking collectives, local(): lax.all_to_all(requests, 'vocab', split_axis=0, concat_axis=0, tiled=True)  11.7 us
    pallas_call x1, Pallas kernels, finish(): pl.pallas_call(finish_kernel, grid_spec=pltpu.PrefetchScalarGridSpec(num_...  10.8 us
  transfers between devices with their start and end apart: 1, of which 1 were waited for; matrix products, arithmetic and copies ran while one was open for 2% of the time, Pallas kernels for 0%

profile of v4, /device:TPU:0, one launch (start us, length us, event | category | flops | bytes accessed | tf_op | source)
XLA Modules:
  0.0 437.8 jit_solution(91523649181229052)
XLA Ops:
  0.7 0.7 broadcast_divide_fusion
  1.4 0.7 compare_and_fusion
  2.1 0.7 fusion.19
  2.8 0.7 fusion.20
  3.5 2.3 reduce-window.6
  6.3 0.7 copy.64
  7.1 4.3 scatter_custom_fusion
  11.5 11.7 %all_to_all.14 = s32[8,1,256]{2,1,0:T(1,128)S(1)} all-to-all(s32[8,1,256]{2,1,0:T(1,128)S(1)} %bitcast.110), channel_id=1, replica_groups=mesh['dp'=4,'vocab'=8] {'vocab'}, dimensions={0} | all-to-all | bytes 16384 | tf_op jit(solution)/shard_map/all_to_all | solution.py:1380
  23.2 11.9 %gather_fusion = bf16[2048,768]{1,0:T(8,128)(2,1)S(1)} fusion(bf16[3840,768]{1,0:T(8,128)(2,1)} %param.27, s32[2048]{0:T(1024)S(1)} %broadcast_clamp_fusion), kind=kCustom, calls=%fused_computation | custom fusion | bytes 6299648 | tf_op jit(solution)/shard_map/gather | solution.py:1382
  35.1 1.9 broadcast_select_fusion
  37.1 3.8 all-to-all-start.1
  40.9 2.4 convert_element_type.23
  48.0 1.0 copy.70
  49.7 8.3 %all-gather = s32[12288]{0:T(1024)S(1)} all-gather(s32[3072]{0:T(1024)S(1)} %pad_add_fusion), channel_id=2, replica_groups=mesh['dp'=4,'vocab'=8] {'dp'}, dimensions={0}, use_global_device_ids=true | all-gather | bytes 61440 | tf_op jit(solution)/shard_map/all_gather | solution.py:1489
  58.0 0.7 copy.59
  59.4 53.0 %all-to-all-done.1 = bf16[8,256,768]{2,1,0:T(8,128)(2,1)S(1)} async-done(((bf16[8,256,768]{2,1,0:T(8,128)(2,1)}), bf16[8,256,768]{2,1,0:T(8,128)(2,1)S(1)}, u32[]{:S(2)}, u32[]{:S(2)}) %all-to-all-start.1) | async-done | bytes 3145760 | tf_op jit(solution)/shard_map/all_to_all | solution.py:1384
  112.4 5.2 %gather_fusion.1 = bf16[1024,768]{1,0:T(8,128)(2,1)} fusion(bf16[2048,768]{1,0:T(8,128)(2,1)S(1)} %bitcast.96, s32[1024]{0:T(1024)S(1)} %broadcast_clamp_fusion.1), kind=kCustom, calls=%fused_computation.1 | custom fusion | bytes 3149824 | tf_op jit(solution)/shard_map/gather | solution.py:1385
  117.6 2.7 fusion.18
  121.0 2.2 multiply_add_fusion.normed
  123.2 32.0 %attend.1 = (bf16[1024,768]{1,0:T(8,128)(2,1)}, bf16[1024,768]{1,0:T(8,128)(2,1)}, bf16[1024,768]{1,0:T(8,128)(2,1)}, bf16[1024,768]{1,0:T(8,128)(2,1)}, bf16[10...) custom-call(s32[2]{0:T(128)} %lengths.1, f32[1024,768]{1,0:T(8,128)} %multiply_add_fusion.normed, ...), custom_call_target="tpu_custom_call" | custom-call | flops 20000000000 | bytes 30000000 | tf_op jit(solution)/shard_map/attend/pallas_call | solution.py:254
  155.2 42.3 %feed.1 = (f32[1024,768]{1,0:T(8,128)}, bf16[1024,3072]{1,0:T(8,128)(2,1)}, bf16[1024,768]{1,0:T(8,128)(2,1)}, bf16[1024,768]{1,0:T(8,128)(2,1)}, bf16[1024,3072...) custom-call(f32[1024,768]{1,0:T(8,128)} %get-tuple-element.56.first, ...), custom_call_target="tpu_custom_call" | custom-call | flops 40000000000 | bytes 40000000 | tf_op jit(solution)/shard_map/feed/pallas_call | solution.py:324
  197.5 0.8 fusion.17
  198.4 82.0 %mid.1 = (bf16[1024,768]{1,0:T(8,128)(2,1)}, bf16[1024,768]{1,0:T(8,128)(2,1)}, bf16[1024,768]{1,0:T(8,128)(2,1)}, bf16[1024,768]{1,0:T(8,128)(2,1)}, bf16[3,4,5...) custom-call(bf16[1024,3072]{1,0:T(8,128)(2,1)} %get-tuple-element.58.active, ...), custom_call_target="tpu_custom_call" | custom-call | tf_op jit(solution)/shard_map/mid/pallas_call | solution.py:775
  280.4 0.9 fusion.15
  282.6 1.3 concatenate.7.small
  283.9 136.1 %tail.1 = (bf16[3,4,1920,128]{3,2,1,0:T(8,128)(2,1)}, bf16[2,2,112,768]{3,2,1,0:T(8,128)(2,1)}, bf16[2,2,192,768]{3,2,1,0:T(8,128)(2,1)}, f32[16,128]{1,0:T(8,128)}) custom-call(s32[4,1,1024]{2,1,0:T(1,128)} %reshape.303.slots, s32[2,1,4096]{2,1,0:T(1,128)} %bitcast.102, s32[128,64]{1,0:T(8,128)} %bitcast.103, bf16[512,768]{1,0:T(8,128)(2,1)} %get-tuple-element.67.pos, ...), custom_call_target="tpu_custom_call" | custom-call | tf_op jit(solution)/shard_map/tail/pallas_call | solution.py:1229
  420.0 1.5 slice_bitcast_fusion
  421.5 0.7 slice.114
  422.2 1.2 slice.106
  424.1 1.3 copy-done.2
  425.4 1.1 copy-done.3
  426.5 10.8 %finish.1 = (f32[2,1920,768]{2,1,0:T(8,128)}, f32[96,768]{1,0:T(8,128)}, f32[96,768]{1,0:T(8,128)}, f32[96,768]{1,0:T(8,128)}, f32[96,768]{1,0:T(8,128)}, /*inde...) custom-call(s32[1]{0:T(128)} %bitcast.13.near, bf16[3,4,1920,128]{3,2,1,0:T(8,128)(2,1)} %get-tuple-element.79.word_in, ...), custom_call_target="tpu_custom_call" | custom-call | tf_op jit(solution)/shard_map/finish/pallas_call | solution.py:1319
  (82 shorter events, 9.5 us)
Async XLA Ops:
  0.7 116.9 %copy-start = (bf16[2,768]{1,0:T(2,128)(2,1)S(1)}, bf16[2,768]{1,0:T(2,128)(2,1)}, u32[]{:S(2)}) copy-start(bf16[2,768]{1,0:T(2,128)(2,1)} %param.29) | copy-start | bytes 9220
  37.0 6.3 %copy-start.11 = (f32[768]{0:T(1024)S(1)}, f32[768]{0:T(1024)}, u32[]{:S(2)}) copy-start(f32[768]{0:T(1024)} %param.33) | copy-start | bytes 9220
  37.0 6.9 %copy-start.12 = (f32[768]{0:T(1024)S(1)}, f32[768]{0:T(1024)}, u32[]{:S(2)}) copy-start(f32[768]{0:T(1024)} %param.36) | copy-start | bytes 9220
  37.0 7.4 %copy-start.13 = (f32[768]{0:T(1024)S(1)}, f32[768]{0:T(1024)}, u32[]{:S(2)}) copy-start(f32[768]{0:T(1024)} %param.38) | copy-start | bytes 9220
  37.0 8.0 %copy-start.14 = (f32[768]{0:T(1024)S(1)}, f32[768]{0:T(1024)}, u32[]{:S(2)}) copy-start(f32[768]{0:T(1024)} %param.44) | copy-start | bytes 9220
  37.0 8.6 %copy-start.15 = (f32[768]{0:T(1024)S(1)}, f32[768]{0:T(1024)}, u32[]{:S(2)}) copy-start(f32[768]{0:T(1024)} %param.39) | copy-start | bytes 9220
  37.0 9.2 %copy-start.16 = (f32[768]{0:T(1024)S(1)}, f32[768]{0:T(1024)}, u32[]{:S(2)}) copy-start(f32[768]{0:T(1024)} %param.40) | copy-start | bytes 9220
  37.1 9.8 %copy-start.17 = (f32[768]{0:T(1024)S(1)}, f32[768]{0:T(1024)}, u32[]{:S(2)}) copy-start(f32[768]{0:T(1024)} %param.45) | copy-start | bytes 9220
  37.1 10.4 %copy-start.18 = (f32[768]{0:T(1024)S(1)}, f32[768]{0:T(1024)}, u32[]{:S(2)}) copy-start(f32[768]{0:T(1024)} %param.46) | copy-start | bytes 9220
  37.1 10.9 %copy-start.7 = (s32[2,512]{1,0:T(2,128)S(1)}, s32[2,512]{1,0:T(2,128)}, u32[]{:S(2)}) copy-start(s32[2,512]{1,0:T(2,128)} %param.25) | copy-start | bytes 12292
  37.1 12.0 %copy-start.6 = (f32[768]{0:T(1024)S(1)}, f32[768]{0:T(1024)}, u32[]{:S(2)}) copy-start(f32[768]{0:T(1024)} %param.30) | copy-start | bytes 9220
  37.1 75.3 %all-to-all-start.1 = ((bf16[8,256,768]{2,1,0:T(8,128)(2,1)}), bf16[8,256,768]{2,1,0:T(8,128)(2,1)S(1)}, u32[]{:S(2)}, u32[]{:S(2)}) async-start(bf16[8,256,768]{2,1,0:T(8,128)(2,1)} %broadcast_select_fusion), calls=%async_computation.1 | async-start | bytes 6291456 | tf_op jit(solution)/shard_map/all_to_all | solution.py:1384
  58.0 59.5 %copy-start.5 = (s32[4,8,2,128]{3,0,1,2:T(4,128)}, s32[4,8,2,128]{3,0,1,2:T(4,128)S(1)}, u32[]{:S(2)}) copy-start(s32[4,8,2,128]{3,0,1,2:T(4,128)S(1)} %copy.58) | copy-start | bytes 98308
  120.3 2.9 copy-start.4
  120.3 0.7 copy-start.10
  198.3 82.0 %copy-start.8 = (f32[8,768]{1,0:T(8,128)S(1)}, f32[8,768]{1,0:T(8,128)}, u32[]{:S(2)}) copy-start(f32[8,768]{1,0:T(8,128)} %get-tuple-element.69) | copy-start | bytes 73732
  198.3 83.4 %copy-start.9 = (f32[1,3072]{1,0:T(1,128)S(1)}, f32[1,3072]{1,0:T(1,128)}, u32[]{:S(2)}) copy-start(f32[1,3072]{1,0:T(1,128)} %get-tuple-element.70) | copy-start | bytes 36868
  424.1 13.2 %copy-start.1 = (bf16[2,768]{1,0:T(2,128)(2,1)S(1)}, bf16[2,768]{1,0:T(2,128)(2,1)}, u32[]{:S(2)}) copy-start(bf16[2,768]{1,0:T(2,128)(2,1)} %param.29) | copy-start | bytes 9220
  424.1 1.3 copy-start.2
  425.4 1.1 copy-start.3
